TPU v7x, 32 devices: a whole 2x2x4 slice. The times are simulated.
32 devices in a mesh: shard: 2 (over core), ctx: 4 (over y, x), tp: 4 (over z).
Axes of the slice: x: 2, y: 2, z: 4, core: 2. Of those that a mesh axis runs over, the one named last changes fastest.
Arguments:
- inputs: bfloat16 [4, 2048, 1536], P('shard', 'ctx'), may hold values from -6 to 6
- starts: int32 [4, 2], P('shard'), may hold values from 0 to 1792, as said below
- first_gain: bfloat16 [1536], P(('shard', 'ctx')), may hold values from 0.099609375 to 1.8984375
- query_weight: bfloat16 [1536, 1536], P(('shard', 'ctx'), 'tp'), may hold values from -0.15625 to 0.15625
- key_matrix: bfloat16 [1536, 768], P(('shard', 'ctx'), 'tp'), may hold values from -0.15625 to 0.15625
- value_matrix: bfloat16 [1536, 768], P(('shard', 'ctx'), 'tp'), may hold values from -0.15625 to 0.15625
- out_weight: bfloat16 [1536, 1536], P('tp', ('shard', 'ctx')), may hold values from -2.5 to 2.5
- second_gain: bfloat16 [1536], P(('shard', 'ctx')), may hold values from 0.099609375 to 1.8984375
- gate_weight: bfloat16 [1536, 4096], P(('shard', 'ctx'), 'tp'), may hold values from -0.15625 to 0.15625
- up_weight: bfloat16 [1536, 4096], P(('shard', 'ctx'), 'tp'), may hold values from -0.15625 to 0.15625
- down_weight: bfloat16 [4096, 1536], P('tp', ('shard', 'ctx')), may hold values from -0.375 to 0.375
- grad_out: bfloat16 [4, 2048, 1536], P('shard', 'ctx'), may hold values from -6 to 6
Outputs:
- outputs: bfloat16 [4, 2048, 1536], P('shard', 'ctx')
- grad_inputs: bfloat16 [4, 2048, 1536], P('shard', 'ctx')
- grad_first_gain: float32 [1536], P(('shard', 'ctx'))
- grad_query_weight: float32 [1536, 1536], P(('shard', 'ctx'), 'tp')
- grad_key_weight: float32 [1536, 768], P(('shard', 'ctx'), 'tp')
- grad_value_weight: float32 [1536, 768], P(('shard', 'ctx'), 'tp')
- grad_out_weight: float32 [1536, 1536], P('tp', ('shard', 'ctx'))
- grad_second_gain: float32 [1536], P(('shard', 'ctx'))
- grad_gate_weight: float32 [1536, 4096], P(('shard', 'ctx'), 'tp')
- grad_up_weight: float32 [1536, 4096], P(('shard', 'ctx'), 'tp')
- grad_down_weight: float32 [4096, 1536], P('tp', ('shard', 'ctx'))
Inputs may be any that keep to these rules, and one draw needn't show every extreme that they name: `starts`: each sequence's 2 image pieces of 256 tokens start in increasing order, do not intersect and lie inside the sequence.
All inputs are finite; a program needn't handle non-finite values.
Results may differ from a plain program's by a relative error of at most 0.025.
Values may be sent and summed in bfloat16 or wider, within the bound.
No kernel may reach another device: no remote copies, remote signals or barrier semaphores. Data moves between devices by JAX's collectives and lax.ppermute only.
A program may use at most 192 MiB of HBM per device.

v0:
```python
import math

import jax
import jax.numpy as jnp
from jax import lax
from jax.sharding import PartitionSpec as P

HEAD_SIZE = 96
PIECE = 256


EPSILON = 1e-05
ROPE_BASE = 100000.0
NEGATIVE = -1e30


def rotation_tables(positions, head_dim):
    half_width = head_dim // 2
    inverse = jnp.exp(
        jnp.arange(half_width, dtype=jnp.float32) * (-2.0 * math.log(ROPE_BASE) / head_dim)
    )
    angles = positions.astype(jnp.float32)[:, None] * inverse[None, :]
    return (jnp.cos(angles)[:, None, :], jnp.sin(angles)[:, None, :])


def apply_rotary_heads(tensor, cosine_lookup, sine_lookup):
    half_width = tensor.shape[-1] // 2
    front_half = tensor[..., :half_width]
    back_half = tensor[..., half_width:]
    return jnp.concatenate(
        [
            front_half * cosine_lookup - back_half * sine_lookup,
            back_half * cosine_lookup + front_half * sine_lookup,
        ],
        axis=-1,
    )


def rotate_back(tensor, cosine_lookup, sine_lookup):
    half_width = tensor.shape[-1] // 2
    front_half = tensor[..., :half_width]
    back_half = tensor[..., half_width:]
    return jnp.concatenate(
        [
            front_half * cosine_lookup + back_half * sine_lookup,
            back_half * cosine_lookup - front_half * sine_lookup,
        ],
        axis=-1,
    )


def piece_number(positions, start_row):
    inside = (positions[:, None] >= start_row[None, :]) & (
        positions[:, None] < start_row[None, :] + PIECE
    )
    labels = jnp.arange(1, start_row.shape[0] + 1, dtype=jnp.int32)
    return jnp.sum(jnp.where(inside, labels[None, :], 0), axis=1)


def allowed_mask(query_pos, key_pos, start_row):
    query_piece = piece_number(query_pos, start_row)
    key_piece = piece_number(key_pos, start_row)
    causal = key_pos[None, :] <= query_pos[:, None]
    same_piece = (query_piece[:, None] == key_piece[None, :]) & (query_piece[:, None] > 0)
    return causal | same_piece


def norm_back(grad_normed, hat_values, inverse_rms, gain_values):
    scaled = grad_normed * gain_values
    return inverse_rms * (
        scaled - hat_values * jnp.mean(scaled * hat_values, axis=-1, keepdims=True)
    )


def local(
    inputs,
    starts,
    first_gain,
    query_weight,
    key_matrix,
    value_matrix,
    out_weight,
    second_gain,
    gate_weight,
    up_weight,
    down_weight,
    grad_out,
):
    seq_count, tok_count, model_width = inputs.shape
    local_heads = query_weight.shape[1] // HEAD_SIZE
    group_heads = key_matrix.shape[1] // HEAD_SIZE
    repeat = local_heads // group_heads
    score_scale = HEAD_SIZE ** (-0.5)
    count_of_rows = seq_count * tok_count
    seq_length = tok_count * lax.axis_size("ctx")
    query_pos = lax.axis_index("ctx") * tok_count + jnp.arange(tok_count, dtype=jnp.int32)
    key_pos = jnp.arange(seq_length, dtype=jnp.int32)
    cosine_lookup, sine_lookup = rotation_tables(query_pos, HEAD_SIZE)
    attn_set = (
        lax.all_gather(first_gain, ("shard", "ctx"), axis=0, tiled=True),
        lax.all_gather(query_weight, ("shard", "ctx"), axis=0, tiled=True),
        lax.all_gather(key_matrix, ("shard", "ctx"), axis=0, tiled=True),
        lax.all_gather(value_matrix, ("shard", "ctx"), axis=0, tiled=True),
        lax.all_gather(out_weight, ("shard", "ctx"), axis=1, tiled=True),
    )
    gain_one, query_full, key_full, value_full, out_full = attn_set
    stream = inputs.reshape(count_of_rows, model_width).astype(jnp.float32)
    inverse_one = lax.rsqrt(jnp.mean(stream * stream, axis=-1, keepdims=True) + EPSILON)
    hat_one = stream * inverse_one
    normed_one = (hat_one * gain_one.astype(jnp.float32)).astype(jnp.bfloat16)
    query_pre = jnp.dot(normed_one, query_full, preferred_element_type=jnp.float32)
    key_unrotated = jnp.dot(normed_one, key_full, preferred_element_type=jnp.float32)
    value_low = (
        jnp.dot(normed_one, value_full, preferred_element_type=jnp.float32)
        .astype(jnp.bfloat16)
        .reshape(seq_count, tok_count, group_heads * HEAD_SIZE)
    )
    query_low = apply_rotary_heads(
        query_pre.reshape(seq_count, tok_count, local_heads, HEAD_SIZE), cosine_lookup, sine_lookup
    ).astype(jnp.bfloat16)
    key_low = (
        apply_rotary_heads(
            key_unrotated.reshape(seq_count, tok_count, group_heads, HEAD_SIZE),
            cosine_lookup,
            sine_lookup,
        )
        .astype(jnp.bfloat16)
        .reshape(seq_count, tok_count, group_heads * HEAD_SIZE)
    )
    key_all, value_all = (
        lax.all_gather(key_low, "ctx", axis=1, tiled=True),
        lax.all_gather(value_low, "ctx", axis=1, tiled=True),
    )

    def scores_of(query_one, key_one, start_row):
        allowed = allowed_mask(query_pos, key_pos, start_row)
        query_grouped = query_one.reshape(tok_count, group_heads, repeat, HEAD_SIZE)
        key_heads = key_one.reshape(seq_length, group_heads, HEAD_SIZE)
        raw_scores = (
            jnp.einsum(
                "qgrd,kgd->grqk", query_grouped, key_heads, preferred_element_type=jnp.float32
            )
            * score_scale
        )
        return (query_grouped, key_heads, jnp.where(allowed, raw_scores, NEGATIVE))

    def attend(operands):
        query_one, key_one, value_one, start_row = operands
        query_grouped, key_heads, masked = scores_of(query_one, key_one, start_row)
        top_score = jnp.max(masked, axis=-1, keepdims=True)
        exp_scores = jnp.exp(masked - top_score)
        total_score = jnp.sum(exp_scores, axis=-1, keepdims=True)
        soft_low = (exp_scores / total_score).astype(jnp.bfloat16)
        value_per_head = value_one.reshape(seq_length, group_heads, HEAD_SIZE)
        mixed_heads = jnp.einsum(
            "grqk,kgd->qgrd", soft_low, value_per_head, preferred_element_type=jnp.float32
        )
        return (mixed_heads.reshape(tok_count, local_heads * HEAD_SIZE), top_score, total_score)

    mixed_heads, top_scores, total_scores = lax.map(attend, (query_low, key_all, value_all, starts))
    mixed_low = mixed_heads.reshape(count_of_rows, local_heads * HEAD_SIZE).astype(jnp.bfloat16)
    attn_sum = lax.psum(
        jnp.dot(mixed_low, out_full, preferred_element_type=jnp.float32).astype(jnp.bfloat16), "tp"
    ).astype(jnp.float32)
    middle = stream + attn_sum
    inverse_two = lax.rsqrt(jnp.mean(middle * middle, axis=-1, keepdims=True) + EPSILON)
    hat_two = middle * inverse_two
    ffn_set = (
        lax.all_gather(second_gain, ("shard", "ctx"), axis=0, tiled=True),
        lax.all_gather(gate_weight, ("shard", "ctx"), axis=0, tiled=True),
        lax.all_gather(up_weight, ("shard", "ctx"), axis=0, tiled=True),
        lax.all_gather(down_weight, ("shard", "ctx"), axis=1, tiled=True),
    )
    gain_two, gate_full, up_full, down_full = ffn_set
    gain_two_wide = gain_two.astype(jnp.float32)
    gain_one_wide = gain_one.astype(jnp.float32)
    normed_two = (hat_two * gain_two_wide).astype(jnp.bfloat16)
    gate_pre = jnp.dot(normed_two, gate_full, preferred_element_type=jnp.float32)
    up_pre = jnp.dot(normed_two, up_full, preferred_element_type=jnp.float32)
    hidden_low = (jax.nn.silu(gate_pre) * up_pre).astype(jnp.bfloat16)
    ffn_sum = lax.psum(
        jnp.dot(hidden_low, down_full, preferred_element_type=jnp.float32).astype(jnp.bfloat16),
        "tp",
    ).astype(jnp.float32)
    result = (middle + ffn_sum).astype(jnp.bfloat16).reshape(seq_count, tok_count, model_width)
    grad_rows = grad_out.reshape(count_of_rows, model_width)
    grad_hidden = jnp.dot(grad_rows, down_full.T, preferred_element_type=jnp.float32)
    grad_down = jnp.dot(hidden_low.T, grad_rows, preferred_element_type=jnp.float32)
    sigmoid_gate = jax.nn.sigmoid(gate_pre)
    grad_gate = (
        grad_hidden * up_pre * sigmoid_gate * (1.0 + gate_pre * (1.0 - sigmoid_gate))
    ).astype(jnp.bfloat16)
    grad_up = (grad_hidden * gate_pre * sigmoid_gate).astype(jnp.bfloat16)
    grad_two_part = jnp.dot(grad_gate, gate_full.T, preferred_element_type=jnp.float32) + jnp.dot(
        grad_up, up_full.T, preferred_element_type=jnp.float32
    )
    grad_gate_weight = jnp.dot(normed_two.T, grad_gate, preferred_element_type=jnp.float32)
    grad_up_weight = jnp.dot(normed_two.T, grad_up, preferred_element_type=jnp.float32)
    grad_normed_two = lax.psum(grad_two_part.astype(jnp.bfloat16), "tp").astype(jnp.float32)
    grad_gain_two = jnp.sum(grad_normed_two * hat_two, axis=0)
    grad_middle = grad_rows.astype(jnp.float32) + norm_back(
        grad_normed_two, hat_two, inverse_two, gain_two_wide
    )
    grad_attn = grad_middle.astype(jnp.bfloat16)
    ffn_grads = (
        lax.psum_scatter(
            grad_gain_two.astype(jnp.bfloat16), ("shard", "ctx"), scatter_dimension=0, tiled=True
        ).astype(jnp.float32),
        lax.psum_scatter(
            grad_gate_weight.astype(jnp.bfloat16), ("shard", "ctx"), scatter_dimension=0, tiled=True
        ).astype(jnp.float32),
        lax.psum_scatter(
            grad_up_weight.astype(jnp.bfloat16), ("shard", "ctx"), scatter_dimension=0, tiled=True
        ).astype(jnp.float32),
        lax.psum_scatter(
            grad_down.astype(jnp.bfloat16), ("shard", "ctx"), scatter_dimension=1, tiled=True
        ).astype(jnp.float32),
    )
    grad_out_weight = jnp.dot(mixed_low.T, grad_attn, preferred_element_type=jnp.float32)
    grad_mixed = (
        jnp.dot(grad_attn, out_full.T, preferred_element_type=jnp.float32)
        .astype(jnp.bfloat16)
        .reshape(seq_count, tok_count, local_heads * HEAD_SIZE)
    )

    def attend_back(operands):
        query_one, key_one, value_one, grad_one, top_one, total_one, start_row = operands
        query_grouped, key_heads, masked = scores_of(query_one, key_one, start_row)
        soft_values = jnp.exp(masked - top_one) / total_one
        soft_low = soft_values.astype(jnp.bfloat16)
        value_per_head = value_one.reshape(seq_length, group_heads, HEAD_SIZE)
        grad_group = grad_one.reshape(tok_count, group_heads, repeat, HEAD_SIZE)
        grad_soft = jnp.einsum(
            "qgrd,kgd->grqk", grad_group, value_per_head, preferred_element_type=jnp.float32
        )
        grad_scores = (
            soft_values * (grad_soft - jnp.sum(soft_values * grad_soft, axis=-1, keepdims=True))
        ).astype(jnp.bfloat16)
        grad_query_one = (
            jnp.einsum("grqk,kgd->qgrd", grad_scores, key_heads, preferred_element_type=jnp.float32)
            * score_scale
        )
        grad_key_one = (
            jnp.einsum(
                "grqk,qgrd->kgd", grad_scores, query_grouped, preferred_element_type=jnp.float32
            )
            * score_scale
        )
        grad_value_one = jnp.einsum(
            "grqk,qgrd->kgd", soft_low, grad_group, preferred_element_type=jnp.float32
        )
        return (
            grad_query_one.reshape(tok_count, local_heads, HEAD_SIZE),
            grad_key_one.reshape(seq_length, group_heads * HEAD_SIZE),
            grad_value_one.reshape(seq_length, group_heads * HEAD_SIZE),
        )

    grad_query_heads, grad_key_all, grad_value_all = lax.map(
        attend_back, (query_low, key_all, value_all, grad_mixed, top_scores, total_scores, starts)
    )
    grad_key_part, grad_value_part = (
        lax.psum_scatter(
            grad_key_all.astype(jnp.bfloat16), "ctx", scatter_dimension=1, tiled=True
        ).astype(jnp.float32),
        lax.psum_scatter(
            grad_value_all.astype(jnp.bfloat16), "ctx", scatter_dimension=1, tiled=True
        ).astype(jnp.float32),
    )
    grad_query = (
        rotate_back(grad_query_heads, cosine_lookup, sine_lookup)
        .astype(jnp.bfloat16)
        .reshape(count_of_rows, local_heads * HEAD_SIZE)
    )
    grad_key = (
        rotate_back(
            grad_key_part.reshape(seq_count, tok_count, group_heads, HEAD_SIZE),
            cosine_lookup,
            sine_lookup,
        )
        .astype(jnp.bfloat16)
        .reshape(count_of_rows, group_heads * HEAD_SIZE)
    )
    grad_value = grad_value_part.astype(jnp.bfloat16).reshape(
        count_of_rows, group_heads * HEAD_SIZE
    )
    grad_one_part = (
        jnp.dot(grad_query, query_full.T, preferred_element_type=jnp.float32)
        + jnp.dot(grad_key, key_full.T, preferred_element_type=jnp.float32)
        + jnp.dot(grad_value, value_full.T, preferred_element_type=jnp.float32)
    )
    grad_query_weight = jnp.dot(normed_one.T, grad_query, preferred_element_type=jnp.float32)
    grad_key_weight = jnp.dot(normed_one.T, grad_key, preferred_element_type=jnp.float32)
    grad_value_weight = jnp.dot(normed_one.T, grad_value, preferred_element_type=jnp.float32)
    grad_normed_one = lax.psum(grad_one_part.astype(jnp.bfloat16), "tp").astype(jnp.float32)
    grad_gain_one = jnp.sum(grad_normed_one * hat_one, axis=0)
    grad_stream = grad_middle + norm_back(grad_normed_one, hat_one, inverse_one, gain_one_wide)
    grad_flat = grad_stream.astype(jnp.bfloat16)
    attn_grads = (
        lax.psum_scatter(
            grad_gain_one.astype(jnp.bfloat16), ("shard", "ctx"), scatter_dimension=0, tiled=True
        ).astype(jnp.float32),
        lax.psum_scatter(
            grad_query_weight.astype(jnp.bfloat16),
            ("shard", "ctx"),
            scatter_dimension=0,
            tiled=True,
        ).astype(jnp.float32),
        lax.psum_scatter(
            grad_key_weight.astype(jnp.bfloat16), ("shard", "ctx"), scatter_dimension=0, tiled=True
        ).astype(jnp.float32),
        lax.psum_scatter(
            grad_value_weight.astype(jnp.bfloat16),
            ("shard", "ctx"),
            scatter_dimension=0,
            tiled=True,
        ).astype(jnp.float32),
        lax.psum_scatter(
            grad_out_weight.astype(jnp.bfloat16), ("shard", "ctx"), scatter_dimension=1, tiled=True
        ).astype(jnp.float32),
    )
    grad_inputs = grad_flat.reshape(seq_count, tok_count, model_width)
    return (
        result,
        grad_inputs,
        attn_grads[0],
        attn_grads[1],
        attn_grads[2],
        attn_grads[3],
        attn_grads[4],
        ffn_grads[0],
        ffn_grads[1],
        ffn_grads[2],
        ffn_grads[3],
    )


def solution(mesh):
    return jax.shard_map(
        local,
        mesh=mesh,
        in_specs=(
            P("shard", "ctx", None),
            P("shard", None),
            P(("shard", "ctx")),
            P(("shard", "ctx"), "tp"),
            P(("shard", "ctx"), "tp"),
            P(("shard", "ctx"), "tp"),
            P("tp", ("shard", "ctx")),
            P(("shard", "ctx")),
            P(("shard", "ctx"), "tp"),
            P(("shard", "ctx"), "tp"),
            P("tp", ("shard", "ctx")),
            P("shard", "ctx", None),
        ),
        out_specs=(
            P("shard", "ctx", None),
            P("shard", "ctx", None),
            P(("shard", "ctx")),
            P(("shard", "ctx"), "tp"),
            P(("shard", "ctx"), "tp"),
            P(("shard", "ctx"), "tp"),
            P("tp", ("shard", "ctx")),
            P(("shard", "ctx")),
            P(("shard", "ctx"), "tp"),
            P(("shard", "ctx"), "tp"),
            P("tp", ("shard", "ctx")),
        ),
        check_vma=False,
    )
```

profile of v0, /device:TPU:12, one launch (start us, length us, event | category | flops | bytes accessed | tf_op | source)
XLA Modules:
  0.0 1276.8 jit_solution(10196900254032959735)
XLA Ops:
  11.7 16.1 %all-reduce.5 = (bf16[1536]{0:T(1024)(128)(2,1)S(1)}, bf16[1536]{0:T(1024)(128)(2,1)}) all-reduce(bf16[1536]{0:T(1024)(128)(2,1)S(1)} %dynamic-update-slice, bf16[1536]{0:T(1024)(128)(2,1)S(1)} %dynamic-update-slice.1), channel_id=1, replica_groups=mesh['shard'=2,'ctx'=4,'tp'=4] {'shard','ctx'}, use_global_device_ids=true, to_apply=%add | all-reduce | flops 3072 | bytes 12288
  27.9 29.8 %all_gather.36 = bf16[1536,192]{1,0:T(8,128)(2,1)} all-gather(bf16[192,192]{1,0:T(8,128)(2,1)} %param.20), channel_id=1, replica_groups=mesh['shard'=2,'ctx'=4,'tp'=4] {'shard','ctx'}, dimensions={0}, use_global_device_ids=true | all-gather | bytes 663552 | tf_op jit(solution)/shard_map/all_gather | solution.py:102
  57.7 2.2 copy.63
  59.9 2.6 fusion.46
  66.3 28.3 %all_gather.34 = bf16[1536,192]{1,0:T(8,128)(2,1)S(1)} all-gather(bf16[192,192]{1,0:T(8,128)(2,1)S(1)} %copy-done.41), channel_id=1, replica_groups=mesh['shard'=2,'ctx'=4,'tp'=4] {'shard','ctx'}, dimensions={0}, use_global_device_ids=true | all-gather | bytes 663552 | tf_op jit(solution)/shard_map/all_gather | solution.py:103
  98.4 2.4 copy.64
  100.8 2.7 fusion.50
  103.9 31.7 %all-gather.8.cloned.1.call-done = bf16[2,2048,192]{1,2,0:T(8,128)(2,1)} async-done(((bf16[2,512,192]{1,2,0:T(8,128)(2,1)}), bf16[2,2048,192]{1,2,0:T(8,128)(2,1)}) %all-gather.8.cloned.1.call-update) | async-done | bytes 1572880 | tf_op jit(solution)/shard_map/all_gather | solution.py:132
  135.6 32.0 %while.32 = (s32[]{:T(128)}, bf16[2,512,384]{2,1,0:T(8,128)(2,1)S(1)}, f32[2,2,2,512,1]{3,2,1,4,0:T(2,128)S(1)}, f32[2,2,2,512,1]{3,2,1,4,0:T(2,128)S(1)}, bf16[...) while((s32[]{:T(128)}, ...), condition=%wide.region_6.7_spmd.clone.clone, body=%wide.region_1.6_spmd.clone.clone.sunk | while | flops 1665158656 | bytes 62493912 | solution.py:160
  139.6 3.3 fusion.155
  142.9 3.7 fusion.156
  146.6 4.7 fusion.157
  155.6 3.3 fusion.155
  158.9 3.7 fusion.156
  162.6 4.7 fusion.157
  168.7 4.8 convolution_convert_fusion
  176.1 116.8 %all-reduce.11.cloned.1.call-done = bf16[1024,1536]{1,0:T(8,128)(2,1)} async-done(((bf16[1024,1536]{1,0:T(8,128)(2,1)}), bf16[1024,1536]{1,0:T(8,128)(2,1)}) %all-reduce.11.cloned.1.call-update) | async-done | bytes 3145744 | tf_op jit(solution)/shard_map/psum | solution.py:162
  292.9 3.1 multiply_reduce_fusion
  296.0 2.8 multiply_convert_fusion
  298.8 28.9 %all-gather.18.cloned.1.call-done = bf16[1536,1024]{1,0:T(8,128)(2,1)} async-done(((bf16[192,1024]{1,0:T(8,128)(2,1)}), bf16[1536,1024]{1,0:T(8,128)(2,1)}) %all-gather.18.cloned.1.call-update) | async-done | bytes 3145744 | tf_op jit(solution)/shard_map/all_gather | solution.py:171
  327.8 8.3 fusion.65
  336.0 26.0 %all-gather.16.cloned.1.call-done = bf16[1536,1024]{1,0:T(8,128)(2,1)} async-done(((bf16[192,1024]{1,0:T(8,128)(2,1)}), bf16[1536,1024]{1,0:T(8,128)(2,1)}) %all-gather.16.cloned.1.call-update) | async-done | bytes 3145744 | tf_op jit(solution)/shard_map/all_gather | solution.py:170
  362.0 8.2 fusion.64
  370.2 26.0 %all-gather.20.cloned.1.call-done = bf16[1024,1536]{0,1:T(8,128)(2,1)} async-done(((bf16[1024,192]{0,1:T(8,128)(2,1)}), bf16[1024,1536]{0,1:T(8,128)(2,1)}) %all-gather.20.cloned.1.call-update) | async-done | bytes 3145744 | tf_op jit(solution)/shard_map/all_gather | solution.py:172
  396.2 11.6 multiply_convert_fusion.1
  407.9 3.7 fusion.66
  411.6 5.0 add_convert_fusion.1
  416.6 119.3 %all-reduce.13.cloned.1.call-done = bf16[1024,1536]{1,0:T(8,128)(2,1)} async-done(((bf16[1024,1536]{1,0:T(8,128)(2,1)}), bf16[1024,1536]{1,0:T(8,128)(2,1)}) %all-reduce.13.cloned.1.call-update) | async-done | bytes 3145744 | tf_op jit(solution)/shard_map/psum | solution.py:199
  536.0 5.9 fusion.41
  541.9 3.0 fusion.40
  547.5 97.9 %while.33 = (s32[]{:T(128)}, f32[2,512,4,96]{1,3,2,0:T(8,128)}, bf16[2,2048,192]{1,2,0:T(8,128)(2,1)}, bf16[2,2048,192]{1,2,0:T(8,128)(2,1)}, bf16[2,2048,192]{1...) while((s32[]{:T(128)}, f32[2,512,4,96]{1,3,2,0:T(8,128)}, ...), condition=%wide.region_16.17_spmd.clone.clone, body=%wide.region_12.16_spmd.clone.clone.sunk | while | flops 4073674240 | bytes 258831888 | solution.py:258
  551.1 2.4 constant_dynamic-slice_fusion.18
  553.5 2.4 fusion.168
  555.9 11.9 fusion.173
  567.8 11.5 fusion.174
  579.3 8.6 fusion.176
  589.4 2.7 fusion.175
  600.0 2.4 constant_dynamic-slice_fusion.18
  602.4 2.4 fusion.168
  604.8 11.9 fusion.173
  616.7 11.5 fusion.174
  628.2 8.6 fusion.176
  638.3 2.7 fusion.175
  647.3 7.0 convolution_convert_fusion.1
  656.2 6.5 convolution_convert_fusion.2
  662.8 6.5 convolution_convert_fusion.3
  670.5 5.6 convolution_convert_fusion.5
  678.2 2.9 convolution_convert_fusion.6
  685.3 8.0 convolution_convert_fusion.4
  693.3 4.5 fusion.67
  697.9 13.5 %reduce-scatter.12.cloned.1.call-done = bf16[2,512,192]{1,2,0:T(8,128)(2,1)} async-done(((bf16[2,2048,192]{1,2,0:T(8,128)(2,1)}), bf16[2,512,192]{1,2,0:T(8,128)(2,1)}) %reduce-scatter.12.cloned.1.call-update) | async-done | bytes 393232 | tf_op jit(solution)/shard_map/reduce_scatter | solution.py:265
  711.3 3.8 fusion.54
  716.5 5.7 add_convert_fusion
  723.0 37.8 %reduce-scatter.26.cloned.1.call-done = bf16[1024,192]{0,1:T(8,128)(2,1)} async-done(((bf16[1024,1536]{0,1:T(8,128)(2,1)}), bf16[1024,192]{0,1:T(8,128)(2,1)}) %reduce-scatter.26.cloned.1.call-update) | async-done | bytes 393232 | tf_op jit(solution)/shard_map/reduce_scatter | solution.py:215
  762.8 48.0 %reduce-scatter.24.cloned.1.call-done = bf16[192,1024]{1,0:T(8,128)(2,1)} async-done(((bf16[1536,1024]{1,0:T(8,128)(2,1)}), bf16[192,1024]{1,0:T(8,128)(2,1)}) %reduce-scatter.24.cloned.1.call-update) | async-done | bytes 393232 | tf_op jit(solution)/shard_map/reduce_scatter | solution.py:212
  812.8 47.6 %reduce-scatter.22.cloned.1.call-done = bf16[192,1024]{1,0:T(8,128)(2,1)} async-done(((bf16[1536,1024]{1,0:T(8,128)(2,1)}), bf16[192,1024]{1,0:T(8,128)(2,1)}) %reduce-scatter.22.cloned.1.call-update) | async-done | bytes 393232 | tf_op jit(solution)/shard_map/reduce_scatter | solution.py:209
  862.3 38.2 %reduce-scatter.20.cloned.1.call-done = bf16[384,192]{0,1:T(8,128)(2,1)} async-done(((bf16[384,1536]{0,1:T(8,128)(2,1)}), bf16[384,192]{0,1:T(8,128)(2,1)}) %reduce-scatter.20.cloned.1.call-update) | async-done | bytes 147472 | tf_op jit(solution)/shard_map/reduce_scatter | solution.py:317
  902.2 38.2 %reduce-scatter.14.cloned.1.call-done = bf16[192,384]{1,0:T(8,128)(2,1)} async-done(((bf16[1536,384]{1,0:T(8,128)(2,1)}), bf16[192,384]{1,0:T(8,128)(2,1)}) %reduce-scatter.14.cloned.1.call-update) | async-done | bytes 147472 | tf_op jit(solution)/shard_map/reduce_scatter | solution.py:302
  942.1 36.7 %reduce-scatter.16.cloned.1.call-done = bf16[192,192]{1,0:T(8,128)(2,1)} async-done(((bf16[1536,192]{1,0:T(8,128)(2,1)}), bf16[192,192]{1,0:T(8,128)(2,1)}) %reduce-scatter.16.cloned.1.call-update) | async-done | bytes 73744 | tf_op jit(solution)/shard_map/reduce_scatter | solution.py:308
  980.4 36.8 %reduce-scatter.18.cloned.1.call-done = bf16[192,192]{1,0:T(8,128)(2,1)} async-done(((bf16[1536,192]{1,0:T(8,128)(2,1)}), bf16[192,192]{1,0:T(8,128)(2,1)}) %reduce-scatter.18.cloned.1.call-update) | async-done | bytes 73744 | tf_op jit(solution)/shard_map/reduce_scatter | solution.py:311
  1018.7 222.8 %all-reduce.15.cloned.1.call-done = (bf16[1024,1536]{1,0:T(8,128)(2,1)}, bf16[1024,1536]{1,0:T(8,128)(2,1)}) async-done(((bf16[1024,1536]{1,0:T(8,128)(2,1)}, bf16[1024,1536]{1,0:T(8,128)(2,1)}), (bf16[1024,1536]{1,0:T(8,128)(2,1)}, bf16[1024,1536]{1,0:T(8,128)(2,1)})) %all-reduce.15.cloned.1.call-update) | async-done | bytes 6291472 | tf_op jit(solution)/shard_map/psum | solution.py:181
  1241.5 3.8 fusion.42
  1245.4 15.4 %all-reduce.4 = (bf16[1536]{0:T(1024)(128)(2,1)S(1)}, bf16[1536]{0:T(1024)(128)(2,1)S(1)}) all-reduce(bf16[1536]{0:T(1024)(128)(2,1)S(1)} %get-tuple-element.308, bf16[1536]{0:T(1024)(128)(2,1)S(1)} %copy-done.45), channel_id=4, replica_groups=mesh['shard'=2,'ctx'=4,'tp'=4] {'shard','ctx'}, use_global_device_ids=true, to_apply=%region_22.23.clone | all-reduce | flops 3072 | bytes 12288
  1261.5 8.6 fusion.37
  (273 shorter events, 70.3 us)
Async XLA Ops:
  7.2 55.8 %copy-start.1 = (bf16[2,512,1536]{2,1,0:T(8,128)(2,1)S(1)}, bf16[2,512,1536]{2,1,0:T(8,128)(2,1)}, u32[]{:S(2)}) copy-start(bf16[2,512,1536]{2,1,0:T(8,128)(2,1)} %param.16) | copy-start | bytes 9437188
  7.2 91.2 %all-gather.12.cloned.1.call-start = ((), (), s32[]{:S(2)}) async-start(), calls=%async_computation.11 | async-start | bytes 1327104 | tf_op jit(solution)/shard_map/all_gather | solution.py:101
  7.9 95.9 %all-gather.10.cloned.1.call-start = ((), (), s32[]{:S(2)}) async-start(), calls=%async_computation.10 | async-start | bytes 1966080 | tf_op jit(solution)/shard_map/all_gather | solution.py:131
  27.9 66.8 %copy-start.39 = (f32[1536]{0:T(1024)}, f32[1536]{0:T(1024)S(1)}, u32[]{:S(2)}) copy-start(f32[1536]{0:T(1024)S(1)} %convert_element_type.209) | copy-start | bytes 18436
  62.9 40.5 %copy-start.23 = (f32[512,48]{0,1:T(8,128)}, f32[512,48]{0,1:T(8,128)S(1)}, u32[]{:S(2)}) copy-start(f32[512,48]{0,1:T(8,128)S(1)} %get-tuple-element.387) | copy-start | bytes 294916
  62.9 40.5 %copy-start.25 = (f32[512,48]{0,1:T(8,128)}, f32[512,48]{0,1:T(8,128)S(1)}, u32[]{:S(2)}) copy-start(f32[512,48]{0,1:T(8,128)S(1)} %get-tuple-element.388) | copy-start | bytes 294916
  64.1 2.2 copy-start.41
  66.2 69.4 %all-gather.8.cloned.1.call-start = ((), (), s32[]{:S(2)}) async-start(), calls=%async_computation.9 | async-start | bytes 1966080 | tf_op jit(solution)/shard_map/all_gather | solution.py:132
  66.3 29.1 %copy-start.42 = (f32[1,4,2,128]{3,1,2,0:T(4,128)}, f32[1,4,2,128]{3,1,2,0:T(4,128)S(1)}, u32[]{:S(2)}) copy-start(f32[1,4,2,128]{3,1,2,0:T(4,128)S(1)} %copy.94) | copy-start | bytes 12292
  95.5 5.2 copy-start.18
  97.5 70.1 %all-gather.14.cloned.1.call-start = ((), (), s32[]{:S(2)}) async-start(), calls=%async_computation.12 | async-start | bytes 1327104 | tf_op jit(solution)/shard_map/all_gather | solution.py:104
  98.1 194.8 %all-reduce.11.cloned.1.call-start = ((), (), s32[]{:S(2)}) async-start(), calls=%async_computation.13 | async-start | bytes 6291456 | tf_op jit(solution)/shard_map/psum | solution.py:162
  103.5 32.1 %copy-start.34 = (bf16[2,512,384]{2,1,0:T(8,128)(2,1)S(1)}, bf16[2,512,384]{2,1,0:T(8,128)(2,1)}, u32[]{:S(2)}) copy-start(bf16[2,512,384]{2,1,0:T(8,128)(2,1)} %custom-call) | copy-start | bytes 2359300
  103.5 32.1 %copy-start.44 = (s32[2,2]{1,0:T(2,128)S(1)}, s32[2,2]{1,0:T(2,128)}, u32[]{:S(2)}) copy-start(s32[2,2]{1,0:T(2,128)} %param.17) | copy-start | bytes 52
  173.5 2.6 copy-start.46
  173.5 119.4 %copy-start.2 = (bf16[2,512,1536]{2,1,0:T(8,128)(2,1)S(1)}, bf16[2,512,1536]{2,1,0:T(8,128)(2,1)}, u32[]{:S(2)}) copy-start(bf16[2,512,1536]{2,1,0:T(8,128)(2,1)} %param.16) | copy-start | bytes 9437188
  173.5 154.2 %all-gather.18.cloned.1.call-start = ((), (), s32[]{:S(2)}) async-start(), calls=%async_computation.15 | async-start | bytes 3538944 | tf_op jit(solution)/shard_map/all_gather | solution.py:171
  174.1 187.9 %all-gather.16.cloned.1.call-start = ((), (), s32[]{:S(2)}) async-start(), calls=%async_computation.14 | async-start | bytes 3538944 | tf_op jit(solution)/shard_map/all_gather | solution.py:170
  174.9 221.4 %all-gather.20.cloned.1.call-start = ((), (), s32[]{:S(2)}) async-start(), calls=%async_computation.16 | async-start | bytes 3538944 | tf_op jit(solution)/shard_map/all_gather | solution.py:172
  175.6 360.4 %all-reduce.13.cloned.1.call-start = ((), (), s32[]{:S(2)}) async-start(), calls=%async_computation.17 | async-start | bytes 6291456 | tf_op jit(solution)/shard_map/psum | solution.py:199
  292.9 3.1 copy-start.5
  396.2 11.6 copy-start.48
  407.9 3.7 copy-start.50
  407.9 3.7 copy-start.51
  407.9 3.7 copy-start.47
  416.6 264.6 %reduce-scatter.10.cloned.1.call-start = ((), (), s32[]{:S(2)}) async-start(), calls=%async_computation.18 | async-start | bytes 1966080 | tf_op jit(solution)/shard_map/reduce_scatter | solution.py:262
  536.0 5.9 copy-start.6
  536.0 5.9 copy-start.9
  536.0 5.9 copy-start.21
  541.9 3.0 copy-start.49
  544.9 2.6 copy-start.7
  547.5 6.0 copy-start.13
  555.9 11.9 copy-start
  579.3 8.6 copy-start.4
  589.4 2.7 copy-start.31
  589.4 2.8 copy-start.29
  592.1 2.0 copy-start.27
  592.1 4.4 copy-start.14
  596.5 6.0 copy-start.13
  604.8 11.9 copy-start
  628.2 8.6 copy-start.4
  638.3 2.7 copy-start.31
  638.3 2.8 copy-start.29
  641.0 2.0 copy-start.27
  641.0 4.4 copy-start.14
  645.4 65.9 %reduce-scatter.12.cloned.1.call-start = ((), (), s32[]{:S(2)}) async-start(), calls=%async_computation.19 | async-start | bytes 1966080 | tf_op jit(solution)/shard_map/reduce_scatter | solution.py:265
  646.2 114.7 %reduce-scatter.26.cloned.1.call-start = ((), (), s32[]{:S(2)}) async-start(), calls=%async_computation.26 | async-start | bytes 3538944 | tf_op jit(solution)/shard_map/reduce_scatter | solution.py:215
  654.3 156.5 %reduce-scatter.24.cloned.1.call-start = ((), (), s32[]{:S(2)}) async-start(), calls=%async_computation.25 | async-start | bytes 3538944 | tf_op jit(solution)/shard_map/reduce_scatter | solution.py:212
  662.8 197.6 %reduce-scatter.22.cloned.1.call-start = ((), (), s32[]{:S(2)}) async-start(), calls=%async_computation.24 | async-start | bytes 3538944 | tf_op jit(solution)/shard_map/reduce_scatter | solution.py:209
  669.3 6.9 copy-start.24
  669.4 6.9 copy-start.26
  669.4 6.9 copy-start.33
  669.4 231.2 %reduce-scatter.20.cloned.1.call-start = ((), (), s32[]{:S(2)}) async-start(), calls=%async_computation.23 | async-start | bytes 1327104 | tf_op jit(solution)/shard_map/reduce_scatter | solution.py:317
  676.1 264.3 %reduce-scatter.14.cloned.1.call-start = ((), (), s32[]{:S(2)}) async-start(), calls=%async_computation.20 | async-start | bytes 1327104 | tf_op jit(solution)/shard_map/reduce_scatter | solution.py:302
  681.1 297.8 %reduce-scatter.16.cloned.1.call-start = ((), (), s32[]{:S(2)}) async-start(), calls=%async_computation.21 | async-start | bytes 884736 | tf_op jit(solution)/shard_map/reduce_scatter | solution.py:308
  681.1 2.0 copy-start.20
  685.1 8.2 copy-start.15
  685.1 332.1 %reduce-scatter.18.cloned.1.call-start = ((), (), s32[]{:S(2)}) async-start(), calls=%async_computation.22 | async-start | bytes 884736 | tf_op jit(solution)/shard_map/reduce_scatter | solution.py:311
  697.9 17.4 %copy-start.12 = (bf16[1536,192]{1,0:T(8,128)(2,1)S(1)}, bf16[1536,192]{1,0:T(8,128)(2,1)}, u32[]{:S(2)}) copy-start(bf16[1536,192]{1,0:T(8,128)(2,1)} %all_gather.36) | copy-start | bytes 1769476
  715.2 526.3 %all-reduce.15.cloned.1.call-start = ((), (), s32[]{:S(2)}) async-start(), calls=%async_computation.27 | async-start | bytes 12582912 | tf_op jit(solution)/shard_map/psum | solution.py:181
  722.2 519.3 %copy-start.3 = (bf16[2,512,1536]{2,1,0:T(8,128)(2,1)S(1)}, bf16[2,512,1536]{2,1,0:T(8,128)(2,1)}, u32[]{:S(2)}) copy-start(bf16[2,512,1536]{2,1,0:T(8,128)(2,1)} %param.16) | copy-start | bytes 9437188
  722.2 519.3 %copy-start.40 = (f32[1536]{0:T(1024)S(1)}, f32[1536]{0:T(1024)}, u32[]{:S(2)}) copy-start(f32[1536]{0:T(1024)} %copy-done.39) | copy-start | bytes 18436
  722.2 519.3 %copy-start.43 = (f32[1,4,2,128]{3,1,2,0:T(4,128)S(1)}, f32[1,4,2,128]{3,1,2,0:T(4,128)}, u32[]{:S(2)}) copy-start(f32[1,4,2,128]{3,1,2,0:T(4,128)} %copy-done.42) | copy-start | bytes 12292
  1241.5 3.8 copy-start.45
  (17 other events, 23.7 us)
Sparse Core Ops, SparseCore 0:
  9.9 27.7 all-gather.11
  66.4 35.6 all-gather.9
  104.5 31.0 all-gather.7
  137.3 24.0 all-gather.13
  173.7 119.1 all-reduce.10
  294.6 33.1 all-gather.17
  329.7 32.3 all-gather.15
  363.9 32.3 all-gather.19
  416.7 119.2 all-reduce.12
  645.6 31.7 reduce-scatter.9
  680.4 30.8 reduce-scatter.11
  714.6 46.2 reduce-scatter.25
  764.6 46.2 reduce-scatter.23
  814.1 46.2 reduce-scatter.21
  863.8 36.7 reduce-scatter.19
  903.7 36.7 reduce-scatter.13
  943.8 34.9 reduce-scatter.15
  982.1 34.9 reduce-scatter.17
  1020.3 221.1 all-reduce.14
where the time goes:
time: 1290 us; the launch traced here: 1280 us
  waiting for transfers between devices  872 us (68%)
  matrix products  172 us (13%)
  blocking collectives  89.7 us (7%)
  other arithmetic  85.5 us (7%)
  local copies, waits for them, and re-layouts  38.7 us (3%)
  between operations  16.4 us (1%)
    psum x1, waiting for transfers between devices, local(): lax.psum(jnp.dot(hidden_low, down_full, preferred_element_type=jnp.float3...  223 us
    psum x1, waiting for transfers between devices, local(): lax.psum(grad_two_part.astype(jnp.bfloat16), 'tp').astype(jnp.float32)  119 us
    psum x1, waiting for transfers between devices, local(): lax.psum(jnp.dot(mixed_low, out_full, preferred_element_type=jnp.float32)...  117 us
    reduce_scatter x1, waiting for transfers between devices, local(): lax.psum_scatter(grad_up_weight.astype(jnp.bfloat16), ('shard', 'ctx'), s...  48 us
    reduce_scatter x1, waiting for transfers between devices, local(): lax.psum_scatter(grad_gate_weight.astype(jnp.bfloat16), ('shard', 'ctx'),...  47.6 us
    reduce_scatter x1, waiting for transfers between devices, local(): lax.psum_scatter(grad_query_weight.astype(jnp.bfloat16), ('shard', 'ctx')...  38.2 us
    reduce_scatter x1, waiting for transfers between devices, local(): lax.psum_scatter(grad_out_weight.astype(jnp.bfloat16), ('shard', 'ctx'),...  38.2 us
    reduce_scatter x1, waiting for transfers between devices, local(): lax.psum_scatter(grad_down.astype(jnp.bfloat16), ('shard', 'ctx'), scatte...  37.8 us
  transfers between devices with their start and end apart: 19, of which 15 were waited for; matrix products, arithmetic and copies ran while one was open for 11% of the time, Pallas kernels for 0%

commit v1 on v0

v1 whole, which is shorter than its diff:
```python
import functools
import math

import jax
import jax.numpy as jnp
from jax import lax
from jax.experimental import pallas as pl
from jax.experimental.pallas import tpu as pltpu
from jax.sharding import PartitionSpec as P

HEAD_SIZE = 96
PIECE = 256

EPSILON = 1e-05
ROPE_BASE = 100000.0
NEGATIVE = -1e30
F32 = jnp.float32
BF16 = jnp.bfloat16
LANES = 128
VMEM_LIMIT=56<<20

def nt(left, right):
    return lax.dot_general(left, right, (((1,), (1,)), ((), ())), preferred_element_type=F32)
def nn(left, right):
    return jnp.dot(left, right, preferred_element_type=F32)

def head_pair(block, group, repeat):
    first = group * repeat
    return jnp.concatenate(
        [block[:, (first + r) * HEAD_SIZE : (first + r + 1) * HEAD_SIZE] for r in range(repeat)], axis=0)

def side_by_side(groups, repeat, tile):
    return jnp.concatenate([g[r * tile : (r + 1) * tile] for g in groups for r in range(repeat)], axis=1)

def attend_kernel(n_groups, repeat, n_blocks, block, bases_ref, q_ref, kv_ref, limit_ref, mixed_ref, lse_ref, k_s, vt_s):
    tile = q_ref.shape[1]
    cols = repeat * tile
    kv_width = n_groups * HEAD_SIZE
    factor = HEAD_SIZE ** (-0.5) * math.log2(math.e)

    @pl.when(pl.program_id(1) == 0)
    def _():
        for g in range(n_groups):
            k_s[g] = kv_ref[0, :, g * HEAD_SIZE : (g + 1) * HEAD_SIZE]
            vt_s[g] = kv_ref[0, :, kv_width + g * HEAD_SIZE : kv_width + (g + 1) * HEAD_SIZE].T

    limit = jnp.concatenate([limit_ref[0, 0]] * repeat, axis=1)
    offset = lax.broadcasted_iota(jnp.int32, (block, cols), 0)
    results = []
    for g in range(n_groups):
        q = head_pair(q_ref[0], g, repeat)
        blocks = []
        for j in range(n_blocks):
            scores = nt(k_s[g, j * block : (j + 1) * block, :], q) * factor
            blocks.append(jnp.where(offset <= limit - bases_ref[j], scores, NEGATIVE))
        top = functools.reduce(jnp.maximum, [jnp.max(x, axis=0, keepdims=True) for x in blocks])
        total = jnp.zeros((1, cols), F32)
        acc = jnp.zeros((HEAD_SIZE, cols), F32)
        for j in range(n_blocks):
            probs = jnp.exp2(blocks[j] - top)
            total = total + jnp.sum(probs, axis=0, keepdims=True)
            acc = acc + nn(vt_s[g, :, j * block : (j + 1) * block], probs.astype(BF16))
        lse_ref[0, 0, g : g + 1, :] = top + jnp.log2(total)
        results.append((acc / total).T)
    mixed_ref[0] = side_by_side(results, repeat, tile).astype(BF16)

def attend(query, kv_all, limits, bases, tile=128):
    seqs, toks, q_width = query.shape
    length = kv_all.shape[1]
    n_groups = kv_all.shape[2] // (2 * HEAD_SIZE)
    repeat = q_width // HEAD_SIZE // n_groups
    n_blocks = bases.shape[0]
    block = length // n_blocks
    n_tiles = toks // tile
    return pl.pallas_call(
        functools.partial(attend_kernel, n_groups, repeat, n_blocks, block),
        grid_spec=pltpu.PrefetchScalarGridSpec(
            num_scalar_prefetch=1,
            grid=(seqs, n_tiles),
            in_specs=[
                pl.BlockSpec((1, tile, q_width), lambda b, t, _: (b, t, 0)),
                pl.BlockSpec((1, length, kv_all.shape[2]), lambda b, t, _: (b, 0, 0)),
                pl.BlockSpec((1, 1, 1, tile), lambda b, t, _: (b, t, 0, 0)),
            ],
            out_specs=[
                pl.BlockSpec((1, tile, q_width), lambda b, t, _: (b, t, 0)),
                pl.BlockSpec((1, 1, n_groups, repeat * tile), lambda b, t, _: (b, t, 0, 0)),
            ],
            scratch_shapes=[
                pltpu.VMEM((n_groups, length, HEAD_SIZE), BF16),
                pltpu.VMEM((n_groups, HEAD_SIZE, length), BF16),
            ],
        ),
        out_shape=[
            jax.ShapeDtypeStruct((seqs, toks, q_width), BF16),
            jax.ShapeDtypeStruct((seqs, n_tiles, n_groups, repeat * tile), F32),
        ],
        compiler_params=pltpu.CompilerParams(vmem_limit_bytes=VMEM_LIMIT),
        cost_estimate=pl.CostEstimate(
            flops=4 * seqs * toks * length * 256 * n_groups * repeat,
            bytes_accessed=4 * seqs * toks * q_width + 4 * seqs * length * q_width,
            transcendentals=seqs * toks * length * n_groups * repeat),
        name="attend",
    )(bases, query, kv_all, limits)

def turn(value, cosine, sine):
    half = HEAD_SIZE // 2
    width = value.shape[-1]
    lane = lax.broadcasted_iota(jnp.int32, value.shape, 1) % HEAD_SIZE
    other = jnp.where(lane < half, pltpu.roll(value, width - half, 1), pltpu.roll(value, half, 1))
    return value * cosine + other * sine

def attend_back_kernel(n_groups, repeat, n_blocks, block, bases_ref, q_ref, kv_ref, limit_ref, lse_ref, mixed_ref,
                       grad_ref, cos_ref, sin_ref, dq_ref, dkv_ref, k_s, v_s, kt_s, dk_s, dv_s):
    tile = q_ref.shape[1]
    cols = repeat * tile
    kv_width = n_groups * HEAD_SIZE
    scale = HEAD_SIZE ** (-0.5)
    factor = scale * math.log2(math.e)

    @pl.when(pl.program_id(1) == 0)
    def _():
        for g in range(n_groups):
            k = kv_ref[0, :, g * HEAD_SIZE : (g + 1) * HEAD_SIZE]
            k_s[g] = k
            kt_s[g] = k.T
            v_s[g] = kv_ref[0, :, kv_width + g * HEAD_SIZE : kv_width + (g + 1) * HEAD_SIZE]
        dk_s[...] = jnp.zeros_like(dk_s)
        dv_s[...] = jnp.zeros_like(dv_s)

    limit = jnp.concatenate([limit_ref[0, 0]] * repeat, axis=1)
    offset = lax.broadcasted_iota(jnp.int32, (block, cols), 0)
    ones = jnp.ones((8, HEAD_SIZE), BF16)
    results = []
    for g in range(n_groups):
        q = head_pair(q_ref[0], g, repeat)
        grad = head_pair(grad_ref[0], g, repeat)
        mixed = head_pair(mixed_ref[0], g, repeat)
        product = grad.astype(F32) * mixed.astype(F32)
        high = product.astype(BF16)
        low = (product - high.astype(F32)).astype(BF16)
        delta = (nt(ones, high) + nt(ones, low))[0:1]
        lse = lse_ref[0, 0, g : g + 1, :]
        dqt = jnp.zeros((HEAD_SIZE, cols), F32)
        for j in range(n_blocks):
            keys = slice(j * block, (j + 1) * block)
            scores = nt(k_s[g, keys, :], q) * factor - lse
            probs = jnp.where(offset <= limit - bases_ref[j], jnp.exp2(scores), 0.0)
            grad_soft = nt(v_s[g, keys, :], grad)
            grad_scores = (probs * (grad_soft - delta)).astype(BF16)
            dv_s[g, keys, :] += nn(probs.astype(BF16), grad)
            dk_s[g, keys, :] += nn(grad_scores, q)
            dqt = dqt + nn(kt_s[g, :, keys], grad_scores)
        results.append(dqt.T * scale)
    dq_ref[0] = turn(side_by_side(results, repeat, tile), cos_ref[...], sin_ref[...]).astype(BF16)

    @pl.when(pl.program_id(1) == pl.num_programs(1) - 1)
    def _():
        dkv_ref[0] = jnp.concatenate(
            [(dk_s[g] * scale).astype(BF16) for g in range(n_groups)]
            + [dv_s[g].astype(BF16) for g in range(n_groups)], axis=1)

def attend_back(query, kv_all, limits, lse, mixed, grad, cosine, sine, bases, tile=128):
    seqs, toks, q_width = query.shape
    length = kv_all.shape[1]
    n_groups = kv_all.shape[2] // (2 * HEAD_SIZE)
    repeat = q_width // HEAD_SIZE // n_groups
    n_blocks = bases.shape[0]
    block = length // n_blocks
    n_tiles = toks // tile
    rows = pl.BlockSpec((1, tile, q_width), lambda b, t, _: (b, t, 0))
    whole = pl.BlockSpec((1, length, kv_all.shape[2]), lambda b, t, _: (b, 0, 0))
    table = pl.BlockSpec((tile, q_width), lambda b, t, _: (t, 0))
    return pl.pallas_call(
        functools.partial(attend_back_kernel, n_groups, repeat, n_blocks, block),
        grid_spec=pltpu.PrefetchScalarGridSpec(
            num_scalar_prefetch=1,
            grid=(seqs, n_tiles),
            in_specs=[
                rows,
                whole,
                pl.BlockSpec((1, 1, 1, tile), lambda b, t, _: (b, t, 0, 0)),
                pl.BlockSpec((1, 1, n_groups, repeat * tile), lambda b, t, _: (b, t, 0, 0)),
                rows,
                rows,
                table,
                table,
            ],
            out_specs=[rows, whole],
            scratch_shapes=[
                pltpu.VMEM((n_groups, length, HEAD_SIZE), BF16),
                pltpu.VMEM((n_groups, length, HEAD_SIZE), BF16),
                pltpu.VMEM((n_groups, HEAD_SIZE, length), BF16),
                pltpu.VMEM((n_groups, length, HEAD_SIZE), F32),
                pltpu.VMEM((n_groups, length, HEAD_SIZE), F32),
            ],
        ),
        out_shape=[
            jax.ShapeDtypeStruct((seqs, toks, q_width), BF16),
            jax.ShapeDtypeStruct((seqs, length, kv_all.shape[2]), BF16),
        ],
        compiler_params=pltpu.CompilerParams(vmem_limit_bytes=VMEM_LIMIT),
        cost_estimate=pl.CostEstimate(
            flops=10 * seqs * toks * length * 256 * n_groups * repeat,
            bytes_accessed=8 * seqs * toks * q_width + 8 * seqs * length * q_width,
            transcendentals=seqs * toks * length * n_groups * repeat),
        name="attend_back",
    )(bases, query, kv_all, limits, lse, mixed, grad, cosine, sine)

def ffn_kernel(keep, steps, normed_ref, grad_ref, gate_ref, up_ref, down_ref, out_ref, back_ref, *rest):
    if steps > 1:
        out_acc, back_acc = rest[-2:]
    step = pl.program_id(1)
    normed = normed_ref[...]
    grad = grad_ref[...]
    gate_w, up_w, down_w = gate_ref[...], up_ref[...], down_ref[...]
    gate = nn(normed, gate_w)
    up = nn(normed, up_w)
    grad_hidden = nn(grad, down_w)
    sig = jax.nn.sigmoid(gate)
    silu = gate * sig
    hidden = (silu * up).astype(BF16)
    grad_gate = (grad_hidden * up * (sig + silu * (1.0 - sig))).astype(BF16)
    grad_up = (grad_hidden * silu).astype(BF16)
    if keep:
        for ref, value in zip(rest[:3], (hidden, grad_gate, grad_up)):
            ref[...] = value
    out_part = nt(hidden, down_w)
    back_part = nt(grad_gate, gate_w) + nt(grad_up, up_w)

    if steps == 1:
        out_ref[...] = out_part.astype(BF16)
        back_ref[...] = back_part.astype(BF16)
        return

    @pl.when(step == 0)
    def _():
        out_acc[...] = out_part
        back_acc[...] = back_part

    @pl.when(step > 0)
    def _():
        out_acc[...] += out_part
        back_acc[...] += back_part

    @pl.when(step == steps - 1)
    def _():
        out_ref[...] = out_acc[...].astype(BF16)
        back_ref[...] = back_acc[...].astype(BF16)

def ffn_slice(normed, grad, weights, keep, row_tile=256, tile=None):
    rows, width = normed.shape
    hidden = weights.shape[1] // 3
    tile = tile or hidden
    steps = hidden // tile
    row_spec = pl.BlockSpec((row_tile, width), lambda r, f: (r, 0))
    hid_spec = pl.BlockSpec((row_tile, tile), lambda r, f: (r, f))
    wide = jax.ShapeDtypeStruct((rows, width), BF16)
    hid = jax.ShapeDtypeStruct((rows, hidden), BF16)
    return pl.pallas_call(
        functools.partial(ffn_kernel, keep, steps),
        grid=(rows // row_tile, steps),
        in_specs=[
            row_spec,
            row_spec,
            pl.BlockSpec((width, tile), lambda r, f: (0, f)),
            pl.BlockSpec((width, tile), lambda r, f: (0, steps + f)),
            pl.BlockSpec((width, tile), lambda r, f: (0, 2 * steps + f)),
        ],
        out_specs=[row_spec, row_spec] + [hid_spec] * (3 if keep else 0),
        out_shape=[wide, wide] + [hid] * (3 if keep else 0),
        scratch_shapes=[pltpu.VMEM((row_tile, width), F32)] * (2 if steps > 1 else 0),
        compiler_params=pltpu.CompilerParams(vmem_limit_bytes=VMEM_LIMIT),
        cost_estimate=pl.CostEstimate(
            flops=12 * rows * width * hidden, bytes_accessed=8 * rows * width + 12 * width * hidden,
            transcendentals=rows * hidden),
        name="ffn_slice",
    )(normed, grad, weights, weights, weights)

def project_kernel(q_width, rows_ref, gain_ref, weight_ref, cos_ref, sin_ref, normed_ref, q_ref, kv_ref):
    rows = rows_ref[...].astype(F32)
    inverse = lax.rsqrt(jnp.mean(rows * rows, axis=-1, keepdims=True) + EPSILON)
    normed = (rows * inverse * gain_ref[...]).astype(BF16)
    normed_ref[...] = normed
    turned = turn(nn(normed, weight_ref[...]), cos_ref[...], sin_ref[...]).astype(BF16)
    q_ref[...] = turned[:, :q_width]
    kv_ref[...] = turned[:, q_width:]


def project(inputs, gain, weights, cosine, sine, q_width, row_tile=256):
    rows, width = inputs.shape
    out_width = cosine.shape[1]
    per_seq = cosine.shape[0] // row_tile
    table = pl.BlockSpec((row_tile, out_width), lambda r: (r % per_seq, 0))
    return pl.pallas_call(
        functools.partial(project_kernel, q_width),
        grid=(rows // row_tile,),
        in_specs=[
            pl.BlockSpec((row_tile, width), lambda r: (r, 0)),
            pl.BlockSpec((1, width), lambda r: (0, 0)),
            pl.BlockSpec((width, out_width), lambda r: (0, 0)),
            table,
            table,
        ],
        out_specs=[
            pl.BlockSpec((row_tile, width), lambda r: (r, 0)),
            pl.BlockSpec((row_tile, q_width), lambda r: (r, 0)),
            pl.BlockSpec((row_tile, out_width - q_width), lambda r: (r, 0)),
        ],
        out_shape=[
            jax.ShapeDtypeStruct((rows, width), BF16),
            jax.ShapeDtypeStruct((rows, q_width), BF16),
            jax.ShapeDtypeStruct((rows, out_width - q_width), BF16),
        ],
        compiler_params=pltpu.CompilerParams(vmem_limit_bytes=VMEM_LIMIT),
        cost_estimate=pl.CostEstimate(
            flops=2 * rows * width * out_width,
            bytes_accessed=4 * rows * width + 2 * width * out_width,
            transcendentals=rows,
        ),
        name="project",
    )(inputs, gain, weights, cosine, sine)


def sum_turn_kernel(count, cos_ref, sin_ref, *refs):
    total = refs[0][0].astype(F32)
    for ref in refs[1:count]:
        total = total + ref[0].astype(F32)
    refs[count][0] = turn(total, cos_ref[...], sin_ref[...]).astype(BF16)


def sum_turn(pieces, cosine, sine):
    toks, width = cosine.shape
    seqs = pieces[0].shape[0]
    block = pl.BlockSpec((1, toks, width), lambda b: (b, 0, 0))
    table = pl.BlockSpec((toks, width), lambda b: (0, 0))
    return pl.pallas_call(
        functools.partial(sum_turn_kernel, len(pieces)),
        grid=(seqs,),
        in_specs=[table, table] + [block] * len(pieces),
        out_specs=block,
        out_shape=jax.ShapeDtypeStruct((seqs, toks, width), BF16),
        compiler_params=pltpu.CompilerParams(vmem_limit_bytes=VMEM_LIMIT),
        name="sum_turn",
    )(cosine, sine, *pieces)


TILE = 128


def rotation_tables(positions, heads, plain):
    half_width = HEAD_SIZE // 2
    inverse = jnp.exp(
        jnp.arange(half_width, dtype=F32) * (-2.0 * math.log(ROPE_BASE) / HEAD_SIZE)
    )
    angles = positions.astype(F32)[:, None] * inverse[None, :]
    cosine, sine = jnp.cos(angles), jnp.sin(angles)
    still = jnp.ones((positions.shape[0], plain * HEAD_SIZE), F32)
    return (
        jnp.concatenate([cosine] * (2 * heads) + [still], axis=1),
        jnp.concatenate([-sine, sine] * heads + [0.0 * still], axis=1),
    )


def last_allowed(positions, start_row):
    begin = start_row[:, None, :]
    inside = (positions[None, :, None] >= begin) & (positions[None, :, None] < begin + PIECE)
    ends = jnp.where(inside, begin + PIECE - 1, -1)
    return jnp.maximum(positions[None, :], jnp.max(ends, axis=-1)).astype(jnp.int32)


def norm_back(grad_normed, hat_values, inverse_rms, gain_values):
    scaled = grad_normed * gain_values
    return inverse_rms * (
        scaled - hat_values * jnp.mean(scaled * hat_values, axis=-1, keepdims=True)
    )


def swap(value, axis, step):
    count = lax.axis_size(axis)
    return lax.ppermute(value, axis, [(i, i ^ step) for i in range(count)])


def partners(value, axis):
    return [value] + [swap(value, axis, j) for j in range(1, lax.axis_size(axis))]


def place(pieces, axis, dim):
    me = lax.axis_index(axis)
    width = pieces[0].shape[dim]
    shape = list(pieces[0].shape)
    shape[dim] = width * len(pieces)
    whole = jnp.zeros(shape, pieces[0].dtype)
    for j, piece in enumerate(pieces):
        whole = lax.dynamic_update_slice_in_dim(whole, piece, (me ^ j) * width, dim)
    return whole


def tn(left, right):
    return lax.dot_general(left, right, (((0,), (0,)), ((), ())), preferred_element_type=F32)


def local(
    inputs,
    starts,
    first_gain,
    query_weight,
    key_matrix,
    value_matrix,
    out_weight,
    second_gain,
    gate_weight,
    up_weight,
    down_weight,
    grad_out,
):
    seq_count, tok_count, model_width = inputs.shape
    q_width = query_weight.shape[1]
    kv_width = key_matrix.shape[1]
    local_heads = q_width // HEAD_SIZE
    group_heads = kv_width // HEAD_SIZE
    rows = seq_count * tok_count
    n_ctx = lax.axis_size("ctx")
    n_tp = lax.axis_size("tp")
    ctx = lax.axis_index("ctx")
    tp = lax.axis_index("tp")
    both = ("shard", "ctx")
    qkv_width = q_width + 2 * kv_width
    hidden = gate_weight.shape[1]

    own_rows = query_weight.shape[0]
    qkv_own = jnp.concatenate([query_weight, key_matrix, value_matrix], axis=1)
    gains_own = jnp.concatenate(
        [
            first_gain[:, None],
            second_gain[:, None],
            jnp.zeros((own_rows, LANES - 2), BF16),
        ],
        axis=1,
    )
    attn_own = jnp.concatenate([qkv_own, gains_own], axis=1)
    attn_full = place(partners(attn_own, "ctx"), "ctx", 0)
    attn_full = place(partners(attn_full, "shard"), "shard", 0)
    gain_one = attn_full[:, qkv_width].astype(F32)[None, :]
    gain_two = attn_full[:, qkv_width + 1].astype(F32)[None, :]

    ffn_own = jnp.concatenate([gate_weight, up_weight, down_weight.T], axis=1)
    ffn_slices = [
        lax.all_gather(piece, both, axis=0, tiled=True) for piece in partners(ffn_own, "tp")
    ]
    out_rows = place(partners(out_weight.T, "tp"), "tp", 1)
    out_full = lax.all_gather(out_rows, both, axis=0, tiled=True)
    qkv_rows = place(partners(qkv_own, "tp"), "tp", 1)
    qkv_full = lax.all_gather(qkv_rows, both, axis=0, tiled=True)

    query_pos = ctx * tok_count + jnp.arange(tok_count, dtype=jnp.int32)
    bases = jnp.stack([(ctx ^ j) * tok_count for j in range(n_ctx)]).astype(jnp.int32)
    limits = last_allowed(query_pos, starts).reshape(seq_count, tok_count // TILE, 1, TILE)
    cosine, sine = rotation_tables(query_pos, local_heads + group_heads, group_heads)
    rows_in = inputs.reshape(rows, model_width)
    normed_one, query_low, kv_own = project(
        rows_in, gain_one, attn_full, cosine, sine, q_width
    )
    query_low = query_low.reshape(seq_count, tok_count, q_width)
    kv_own = kv_own.reshape(seq_count, tok_count, 2 * kv_width)
    kv_all = jnp.concatenate(partners(kv_own, "ctx"), axis=1)
    mixed_seqs, lse = attend(query_low, kv_all, limits, bases, TILE)
    mixed_low = mixed_seqs.reshape(rows, q_width)
    mixed_all = place(partners(mixed_low, "tp"), "tp", 1)

    stream = rows_in.astype(F32)
    middle = stream + nt(mixed_all, out_full)
    inverse_two = lax.rsqrt(jnp.mean(middle * middle, axis=-1, keepdims=True) + EPSILON)
    hat_two = middle * inverse_two
    normed_two = (hat_two * gain_two).astype(BF16)
    grad_rows = grad_out.reshape(rows, model_width)

    total_out = middle
    grad_normed_two = jnp.zeros((rows, model_width), F32)
    for j in range(n_tp):
        out_term, back_term, *kept = ffn_slice(normed_two, grad_rows, ffn_slices[j], j == 0)
        total_out = total_out + out_term.astype(F32)
        grad_normed_two = grad_normed_two + back_term.astype(F32)
        if j == 0:
            hidden_low, grad_gate, grad_up = kept
            ffn_grads = jnp.concatenate(
                [
                    tn(normed_two, grad_gate).astype(BF16),
                    tn(normed_two, grad_up).astype(BF16),
                    tn(grad_rows, hidden_low).astype(BF16),
                ],
                axis=1,
            )
    ffn_grads = lax.psum_scatter(ffn_grads, both, scatter_dimension=0, tiled=True).astype(F32)
    result = total_out.astype(BF16).reshape(seq_count, tok_count, model_width)

    grad_gain_two = jnp.sum(grad_normed_two * hat_two, axis=0)
    grad_middle = grad_rows.astype(F32) + norm_back(grad_normed_two, hat_two, inverse_two, gain_two)
    grad_attn = grad_middle.astype(BF16)
    out_own = lax.dynamic_slice_in_dim(out_full, tp * q_width, q_width, 1)
    grad_out_rows = tn(grad_attn, mixed_low)
    grad_mixed = nn(grad_attn, out_own).astype(BF16).reshape(seq_count, tok_count, q_width)

    grad_query, grad_kv_all = attend_back(
        query_low,
        kv_all,
        limits,
        lse,
        mixed_seqs,
        grad_mixed,
        cosine[:, :q_width],
        -sine[:, :q_width],
        bases,
        TILE,
    )
    grad_query = grad_query.reshape(rows, q_width)
    pieces = [grad_kv_all] + [
        swap(grad_kv_all[:, j * tok_count : (j + 1) * tok_count], "ctx", j) for j in range(1, n_ctx)
    ]
    grad_kv = sum_turn(pieces, cosine[:, q_width:], -sine[:, q_width:]).reshape(rows, 2 * kv_width)
    grad_q_pieces = partners(grad_query, "tp")
    grad_kv_pieces = partners(grad_kv, "tp")
    grad_qkv_all = place(
        [jnp.concatenate(pair, axis=1) for pair in zip(grad_q_pieces, grad_kv_pieces)], "tp", 1
    )
    grad_normed_one = nt(grad_qkv_all, qkv_full)
    attn_grads = jnp.concatenate(
        [
            tn(normed_one, grad_query).astype(BF16),
            tn(normed_one, grad_kv).astype(BF16),
            grad_out_rows.astype(BF16),
            jnp.broadcast_to(grad_gain_two.astype(BF16)[:, None], (model_width, LANES)),
        ],
        axis=1,
    )
    attn_grads = lax.psum_scatter(attn_grads, both, scatter_dimension=0, tiled=True).astype(F32)

    inverse_one = lax.rsqrt(jnp.mean(stream * stream, axis=-1, keepdims=True) + EPSILON)
    hat_one = stream * inverse_one
    grad_gain_one = jnp.sum(grad_normed_one * hat_one, axis=0)
    for axis in both:
        pieces = partners(grad_gain_one, axis)
        grad_gain_one = sum(pieces[1:], pieces[0])
    part = lax.axis_index("shard") * n_ctx + ctx
    grad_gain_one = lax.dynamic_slice_in_dim(grad_gain_one, part * own_rows, own_rows, 0)
    grad_stream = grad_middle + norm_back(grad_normed_one, hat_one, inverse_one, gain_one)
    grad_inputs = grad_stream.astype(BF16).reshape(seq_count, tok_count, model_width)
    return (
        result,
        grad_inputs,
        grad_gain_one,
        attn_grads[:, :q_width],
        attn_grads[:, q_width : q_width + kv_width],
        attn_grads[:, q_width + kv_width : qkv_width],
        attn_grads[:, qkv_width : qkv_width + q_width].T,
        attn_grads[:, qkv_width + q_width],
        ffn_grads[:, :hidden],
        ffn_grads[:, hidden : 2 * hidden],
        ffn_grads[:, 2 * hidden :].T,
    )


def solution(mesh):
    both = ("shard", "ctx")
    rows = P("shard", "ctx", None)
    return jax.shard_map(
        local,
        mesh=mesh,
        in_specs=(
            rows,
            P("shard", None),
            P(both),
            P(both, "tp"),
            P(both, "tp"),
            P(both, "tp"),
            P("tp", both),
            P(both),
            P(both, "tp"),
            P(both, "tp"),
            P("tp", both),
            rows,
        ),
        out_specs=(
            rows,
            rows,
            P(both),
            P(both, "tp"),
            P(both, "tp"),
            P(both, "tp"),
            P("tp", both),
            P(both),
            P(both, "tp"),
            P(both, "tp"),
            P("tp", both),
        ),
        check_vma=False,
    )
```

time: 1290 us -> 863 us (0.67)
  waiting for transfers between devices: 872 us -> 435 us
  Pallas kernels: 0 us -> 180 us
  matrix products: 172 us -> 48.6 us
  blocking collectives: 89.7 us -> 0 us
  local copies, waits for them, and re-layouts: 38.7 us -> 83.9 us
  starting transfers between devices: 1.52 us -> 33.7 us
  other arithmetic: 85.5 us -> 56.8 us
    psum x3 -> x0, waiting for transfers between devices: 459 us -> none  [the longest x1 223 us: local(): lax.psum(jnp.dot(hidden_low, down_full, preferred_element_type=jnp.float3...]
    ppermute x0 -> x32, waiting for transfers between devices: none -> 435 us  [swap(): return lax.ppermute(value, axis, [(i, i ^ step) for i in range(count)])]
    reduce_scatter x9 -> x0, waiting for transfers between devices: 297 us -> none  [the longest x1 48 us: local(): lax.psum_scatter(grad_up_weight.astype(jnp.bfloat16), ('shard', 'ctx'), s...]
    pallas_call x0 -> x8, Pallas kernels: none -> 180 us  [the longest x4 108 us: ffn_slice(): pl.pallas_call(functools.partial(ffn_kernel, keep, steps), grid=(rows //...]
    dot_general x35 -> x9, matrix products: 172 us -> 48.6 us  [the longest x2 23.9 us: nt(): lax.dot_general(left, right, (((1,), (1,)), ((), ())), preferred_element_...]
    all_gather x7 -> x6, waiting for transfers between devices: 113 us -> 0.04 us  [the longest x4 0.03 us: local(): lax.all_gather(piece, both, axis=0, tiled=True)]
    all_gather x2 -> x0, blocking collectives: 58.2 us -> none  [the longest x1 29.8 us: local(): lax.all_gather(key_matrix, ('shard', 'ctx'), axis=0, tiled=True)]
    convert_element_type x19 -> x5, other arithmetic: 49.1 us -> 6.34 us  [the longest x1 3.33 us: local(): grad_stream.astype(BF16).reshape(seq_count, tok_count, model_width)]
  transfers between devices with their start and end apart: 19 -> 40, of which waited for: 15 -> 22; matrix products, arithmetic and copies ran while one was open for 11% -> 20% of each run, Pallas kernels for 0% -> 21%
where the time goes in v1:
time: 863 us; the launch traced here: 853 us
  waiting for transfers between devices  435 us (50%)
  Pallas kernels  180 us (21%)
  local copies, waits for them, and re-layouts  83.9 us (10%)
  other arithmetic  56.8 us (7%)
  matrix products  48.6 us (6%)
  starting transfers between devices  33.7 us (4%)
  between operations  15.3 us (2%)
    ppermute x32, waiting for transfers between devices, swap(): return lax.ppermute(value, axis, [(i, i ^ step) for i in range(count)])  435 us
    pallas_call x4, Pallas kernels, ffn_slice(): pl.pallas_call(functools.partial(ffn_kernel, keep, steps), grid=(rows //...  108 us
    unnamed x96, local copies, waits for them, and re-layouts  40.8 us
    pallas_call x1, Pallas kernels, attend_back(): pl.pallas_call(functools.partial(attend_back_kernel, n_groups, repeat, n_...  33.9 us
    ppermute x32, starting transfers between devices, swap(): return lax.ppermute(value, axis, [(i, i ^ step) for i in range(count)])  33.2 us
    pallas_call x1, Pallas kernels, attend(): pl.pallas_call(functools.partial(attend_kernel, n_groups, repeat, n_block...  24.7 us
    dot_general x2, matrix products, nt(): lax.dot_general(left, right, (((1,), (1,)), ((), ())), preferred_element_...  23.9 us
    dot_general x6, matrix products, tn(): lax.dot_general(left, right, (((0,), (0,)), ((), ())), preferred_element_...  19.9 us
  transfers between devices with their start and end apart: 40, of which 22 were waited for; matrix products, arithmetic and copies ran while one was open for 20% of the time, Pallas kernels for 21%

profile of v1, /device:TPU:12, one launch (start us, length us, event | category | flops | bytes accessed | tf_op | source)
XLA Modules:
  0.0 853.1 jit_solution(18306174592708960512)
XLA Ops:
  7.7 2.6 collective-permute-start.11
  11.8 2.1 collective-permute-done.10
  13.9 7.1 collective-permute-done.11
  21.1 2.7 collective-permute-done.12
  24.8 2.4 pad_maximum_fusion.3
  27.4 26.8 %collective-permute-done.13 = bf16[192,3072]{1,0:T(8,128)(2,1)S(1)} collective-permute-done((bf16[192,3072]{1,0:T(8,128)(2,1)}, bf16[192,3072]{1,0:T(8,128)(2,1)S(1)}, u32[]{:S(2)}, u32[]{:S(2)}) %collective-permute-start.13) | collective-permute-done | bytes 1179680 | tf_op jit(solution)/shard_map/ppermute | solution.py:381
  56.8 49.3 %collective-permute-done.14 = bf16[192,3072]{1,0:T(8,128)(2,1)S(1)} collective-permute-done((bf16[192,3072]{1,0:T(8,128)(2,1)}, bf16[192,3072]{1,0:T(8,128)(2,1)S(1)}, u32[]{:S(2)}, u32[]{:S(2)}) %collective-permute-start.14) | collective-permute-done | bytes 1179680 | tf_op jit(solution)/shard_map/ppermute | solution.py:381
  107.5 51.9 %collective-permute-done.15 = bf16[192,3072]{1,0:T(8,128)(2,1)S(1)} collective-permute-done((bf16[192,3072]{1,0:T(8,128)(2,1)S(1)}, bf16[192,3072]{1,0:T(8,128)(2,1)S(1)}, u32[]{:S(2)}, u32[]{:S(2)}) %collective-permute-start.15) | collective-permute-done | bytes 1179680 | tf_op jit(solution)/shard_map/ppermute | solution.py:381
  164.8 7.3 collective-permute-done
  172.2 7.0 collective-permute-done.1
  179.3 4.0 collective-permute-done.2
  186.2 5.0 concatenate.50.cos_ref
  192.1 5.1 concatenate.51.sin_ref
  200.7 9.2 %project.1 = (bf16[1024,1536]{1,0:T(8,128)(2,1)}, bf16[1024,384]{1,0:T(8,128)(2,1)}, bf16[1024,384]{1,0:T(8,128)(2,1)}) custom-call(bf16[1024,1536]{1,0:T(8,128)(2,1)} %bitcast.50, f32[1,1536]{1,0:T(1,128)} %reshape.161.gain_ref, bf16[1536,896]{1,0:T(8,128)(2,1)} %copy-done.4, f32[512,768]{1,0:T(8,128)} %concatenate.50.cos_ref, f32[512,768]{1,0:T(8,128)} %concatenate.51.sin_ref), custom_call_target="tpu_custom_call" | custom-call | flops 2415919104 | bytes 8650752 | tf_op jit(solution)/shard_map/project/pallas_call | solution.py:295
  209.9 2.6 collective-permute-start.4
  215.5 28.3 %collective-permute-done.4 = bf16[2,512,384]{2,1,0:T(8,128)(2,1)S(1)} collective-permute-done((bf16[2,512,384]{2,1,0:T(8,128)(2,1)}, bf16[2,512,384]{2,1,0:T(8,128)(2,1)S(1)}, u32[]{:S(2)}, u32[]{:S(2)}) %collective-permute-start.4) | collective-permute-done | bytes 786464 | tf_op jit(solution)/shard_map/ppermute | solution.py:381
  243.8 9.1 %collective-permute-done.5 = bf16[2,512,384]{2,1,0:T(8,128)(2,1)} collective-permute-done((bf16[2,512,384]{2,1,0:T(8,128)(2,1)}, bf16[2,512,384]{2,1,0:T(8,128)(2,1)}, u32[]{:S(2)}, u32[]{:S(2)}) %collective-permute-start.5) | collective-permute-done | bytes 786464 | tf_op jit(solution)/shard_map/ppermute | solution.py:381
  252.9 20.7 %collective-permute-done.6 = bf16[2,512,384]{2,1,0:T(8,128)(2,1)} collective-permute-done((bf16[2,512,384]{2,1,0:T(8,128)(2,1)}, bf16[2,512,384]{2,1,0:T(8,128)(2,1)}, u32[]{:S(2)}, u32[]{:S(2)}) %collective-permute-start.6) | collective-permute-done | bytes 786464 | tf_op jit(solution)/shard_map/ppermute | solution.py:381
  273.6 3.1 pad_maximum_fusion.2.kv_ref
  276.7 24.7 %attend.1 = (bf16[2,512,384]{2,1,0:T(8,128)(2,1)}, f32[2,4,2,256]{3,2,1,0:T(2,128)}) custom-call(s32[4]{0:T(128)} %pad_add_fusion.bases_ref, bf16[2,512,384]{2,1,0:T(8,128)(2,1)} %bitcast.85, bf16[2,2048,384]{2,1,0:T(8,128)(2,1)} %pad_maximum_fusion.2.kv_ref, s32[2,4,1,128]{3,2,1,0:T(1,128)} %broadcast_maximum_fusion.limit_ref), custom_call_target="tpu_custom_call" | custom-call | flops 8589934592 | bytes 7864320 | tf_op jit(solution)/shard_map/attend/pallas_call | solution.py:75
  303.4 2.9 collective-permute-start.8
  314.2 2.1 neg.10.sin_ref
  318.3 7.6 collective-permute-done.26
  326.9 55.8 %collective-permute-done.27 = bf16[192,768]{1,0:T(8,128)(2,1)} collective-permute-done((bf16[192,768]{1,0:T(8,128)(2,1)}, bf16[192,768]{1,0:T(8,128)(2,1)}, u32[]{:S(2)}, u32[]{:S(2)}) %collective-permute-start.27) | collective-permute-done | bytes 294944 | tf_op jit(solution)/shard_map/ppermute | solution.py:381
  386.9 2.2 constant_dynamic-update-slice_fusion.11
  389.1 2.1 constant_dynamic-update-slice_fusion.10
  391.2 2.2 constant_dynamic-update-slice_fusion.9
  393.4 4.9 collective-permute-done.9
  398.4 2.1 constant_dynamic-update-slice_fusion.8
  400.5 8.4 multiply_reduce_fusion.3
  408.9 2.7 copy-done.1
  411.6 2.3 multiply_convert_fusion.normed_ref
  413.9 27.9 %ffn_slice.4 = (bf16[1024,1536]{1,0:T(8,128)(2,1)}, bf16[1024,1536]{1,0:T(8,128)(2,1)}, bf16[1024,1024]{1,0:T(8,128)(2,1)}, bf16[1024,1024]{1,0:T(8,128)(2,1)}, bf16[1024,1024]{1,0:T(8,128)(2,1)}) custom-call(bf16[1024,1536]{1,0:T(8,128)(2,1)} %multiply_convert_fusion.normed_ref, bf16[1024,1536]{1,0:T(8,128)(2,1)} %bitcast.52, ...), custom_call_target="tpu_custom_call" | custom-call | flops 19327352832 | bytes 31457280 | tf_op jit(solution)/shard_map/ffn_slice/pallas_call | solution.py:260
  441.8 26.5 %ffn_slice.5 = (bf16[1024,1536]{1,0:T(8,128)(2,1)}, bf16[1024,1536]{1,0:T(8,128)(2,1)}) custom-call(bf16[1024,1536]{1,0:T(8,128)(2,1)} %multiply_convert_fusion.normed_ref, bf16[1024,1536]{1,0:T(8,128)(2,1)} %bitcast.53, bf16[1536,3072]{1,0:T(8,128)(2,1)} %all-gather.11.cloned.1.call-done.gate_ref.up_ref.down_ref, ...), custom_call_target="tpu_custom_call" | custom-call | flops 19327352832 | bytes 31457280 | tf_op jit(solution)/shard_map/ffn_slice/pallas_call | solution.py:260
  468.3 26.9 %ffn_slice.6 = (bf16[1024,1536]{1,0:T(8,128)(2,1)}, bf16[1024,1536]{1,0:T(8,128)(2,1)}) custom-call(bf16[1024,1536]{1,0:T(8,128)(2,1)} %multiply_convert_fusion.normed_ref, bf16[1024,1536]{1,0:T(8,128)(2,1)} %bitcast.54, bf16[1536,3072]{1,0:T(8,128)(2,1)} %all-gather.13.cloned.1.call-done.gate_ref.up_ref.down_ref, ...), custom_call_target="tpu_custom_call" | custom-call | flops 19327352832 | bytes 31457280 | tf_op jit(solution)/shard_map/ffn_slice/pallas_call | solution.py:260
  495.2 26.6 %ffn_slice.7 = (bf16[1024,1536]{1,0:T(8,128)(2,1)}, bf16[1024,1536]{1,0:T(8,128)(2,1)}) custom-call(bf16[1024,1536]{1,0:T(8,128)(2,1)} %multiply_convert_fusion.normed_ref, bf16[1024,1536]{1,0:T(8,128)(2,1)} %bitcast.55, bf16[1536,3072]{1,0:T(8,128)(2,1)} %all-gather.15.cloned.1.call-done.gate_ref.up_ref.down_ref, ...), custom_call_target="tpu_custom_call" | custom-call | flops 19327352832 | bytes 31457280 | tf_op jit(solution)/shard_map/ffn_slice/pallas_call | solution.py:260
  521.8 6.4 multiply_reduce_fusion
  528.1 14.7 %multiply_add_fusion = (f32[1024,1536]{1,0:T(8,128)S(1)}, bf16[1024,1536]{1,0:T(8,128)(2,1)}) fusion(f32[1024,1536]{1,0:T(8,128)} %copy-done.1, f32[1024]{0:T(1024)S(1)} %broadcast_multiply_fusion.1, f32[1536]{0:T(1024)S(1)} %get-tuple-element.95, f32[1024]{0:T(1024)S(1)} %add_rsqrt_fusion, bf16[2,512,1536]{2,1,0:T(8,128)(2,1)} %param.23, ...), kind=kLoop, calls=%fused_computation.14 | loop fusion | flops 36175872 | bytes 44054528 | tf_op jit(solution)/shard_map/add | solution.py:498
  542.8 4.9 fusion.13
  547.7 33.9 %attend_back.1 = (bf16[2,512,384]{2,1,0:T(8,128)(2,1)}, bf16[2,2048,384]{2,1,0:T(8,128)(2,1)}) custom-call(s32[4]{0:T(128)} %pad_add_fusion.bases_ref, bf16[2,512,384]{2,1,0:T(8,128)(2,1)} %bitcast.86, bf16[2,2048,384]{2,1,0:T(8,128)(2,1)} %pad_maximum_fusion.2.kv_ref, s32[2,4,1,128]{3,2,1,0:T(1,128)} %broadcast_maximum_fusion.limit_ref, ...), custom_call_target="tpu_custom_call" | custom-call | flops 21474836480 | bytes 15728640 | tf_op jit(solution)/shard_map/attend_back/pallas_call | solution.py:174
  587.1 2.4 convolution_convert_fusion.5
  591.0 13.1 %collective-permute-done.16.refs_1_ = bf16[2,512,384]{2,1,0:T(8,128)(2,1)S(1)} collective-permute-done((bf16[2,512,384]{2,1,0:T(8,128)(2,1)S(1)}, bf16[2,512,384]{2,1,0:T(8,128)(2,1)S(1)}, u32[]{:S(2)}, u32[]{:S(2)}) %collective-permute-start.16) | collective-permute-done | bytes 786464 | tf_op jit(solution)/shard_map/ppermute | solution.py:381
  604.1 16.0 %collective-permute-done.17.refs_2_ = bf16[2,512,384]{2,1,0:T(8,128)(2,1)S(1)} collective-permute-done((bf16[2,512,384]{2,1,0:T(8,128)(2,1)S(1)}, bf16[2,512,384]{2,1,0:T(8,128)(2,1)S(1)}, u32[]{:S(2)}, u32[]{:S(2)}) %collective-permute-start.17) | collective-permute-done | bytes 786464 | tf_op jit(solution)/shard_map/ppermute | solution.py:381
  621.0 4.0 sum_turn.1
  625.1 2.6 convolution_convert_fusion.4
  627.8 2.1 pad_maximum_fusion.1
  629.9 6.3 copy.57
  638.1 5.7 convolution_convert_fusion.1
  643.9 3.8 convolution_convert_fusion.2
  647.7 3.8 fusion.9
  651.5 4.4 pad_maximum_fusion
  655.9 12.7 %copy.59 = bf16[1536,3072]{1,0:T(8,128)(2,1)} copy(bf16[1536,3072]{0,1:T(8,128)(2,1)} %pad_maximum_fusion) | data formatting | bytes 18874368
  674.0 29.6 %collective-permute-done.19 = bf16[1024,384]{1,0:T(8,128)(2,1)} collective-permute-done((bf16[1024,384]{1,0:T(8,128)(2,1)}, bf16[1024,384]{1,0:T(8,128)(2,1)}, u32[]{:S(2)}, u32[]{:S(2)}) %collective-permute-start.19) | collective-permute-done | bytes 786464 | tf_op jit(solution)/shard_map/ppermute | solution.py:381
  704.7 3.5 broadcast_in_dim.70
  709.7 21.5 %collective-permute-done.20 = bf16[1024,384]{1,0:T(8,128)(2,1)} collective-permute-done((bf16[1024,384]{1,0:T(8,128)(2,1)}, bf16[1024,384]{1,0:T(8,128)(2,1)}, u32[]{:S(2)}, u32[]{:S(2)}) %collective-permute-start.20) | collective-permute-done | bytes 786464 | tf_op jit(solution)/shard_map/ppermute | solution.py:381
  731.1 2.8 maximum_dynamic-update-slice_fusion.1
  733.9 56.2 %collective-permute-done.22 = bf16[1024,384]{1,0:T(8,128)(2,1)} collective-permute-done((bf16[1024,384]{1,0:T(8,128)(2,1)}, bf16[1024,384]{1,0:T(8,128)(2,1)}, u32[]{:S(2)}, u32[]{:S(2)}) %collective-permute-start.22) | collective-permute-done | bytes 786464 | tf_op jit(solution)/shard_map/ppermute | solution.py:381
  790.1 2.9 maximum_dynamic-update-slice_fusion.2
  793.0 12.6 %collective-permute-done.24 = bf16[1024,384]{1,0:T(8,128)(2,1)} collective-permute-done((bf16[1024,384]{1,0:T(8,128)(2,1)}, bf16[1024,384]{1,0:T(8,128)(2,1)}, u32[]{:S(2)}, u32[]{:S(2)}) %collective-permute-start.24) | collective-permute-done | bytes 786464 | tf_op jit(solution)/shard_map/ppermute | solution.py:381
  805.6 2.7 maximum_dynamic-update-slice_fusion.3
  808.4 15.5 %fusion.8 = (f32[1536]{0:T(1024)S(1)}, f32[1024]{0:T(1024)S(1)}, f32[1024,1536]{1,0:T(8,128)S(1)}) fusion(f32[1024]{0:T(1024)S(1)} %bitcast.82, bf16[2,512,1536]{2,1,0:T(8,128)(2,1)S(1)} %copy-done.3, f32[1536]{0:T(1024)S(1)} %copy-done.32, bf16[1024,3072]{1,0:T(8,128)(2,1)} %maximum_dynamic-update-slice_fusion.3, ...), kind=kOutput, calls=%fused_computation.11 | convolution fusion | flops 9674683392 | bytes 25186304 | tf_op jit(solution)/shard_map/dot_general | solution.py:23
  825.9 2.7 collective-permute-start.31
  828.6 3.3 fusion.7
  842.2 2.4 copy.54
  (216 shorter events, 71.0 us)
Async XLA Ops:
  7.2 393.3 %all-gather.7.cloned.1.call-start = ((), (), s32[]{:S(2)}) async-start(), calls=%async_computation.2 | async-start | bytes 5308416 | tf_op jit(solution)/shard_map/all_gather | solution.py:452
  7.2 6.7 collective-permute-start.10
  7.7 13.3 %collective-permute-start.11 = (bf16[192,384]{1,0:T(8,128)(2,1)}, bf16[192,384]{1,0:T(8,128)(2,1)S(1)}, u32[]{:S(2)}, u32[]{:S(2)}) collective-permute-start(bf16[192,384]{1,0:T(8,128)(2,1)} %bitcast.80), channel_id=1, source_target_pairs={{0,2},{1,3},{2,0},{3,1},{4,6},{5,7},{6,4},{7,5},{8,10},{9,11},{10,... | collective-permute-start | bytes 442376 | tf_op jit(solution)/shard_map/ppermute | solution.py:381
  10.3 13.5 %collective-permute-start.12 = (bf16[192,384]{1,0:T(8,128)(2,1)}, bf16[192,384]{1,0:T(8,128)(2,1)S(1)}, u32[]{:S(2)}, u32[]{:S(2)}) collective-permute-start(bf16[192,384]{1,0:T(8,128)(2,1)} %bitcast.81), channel_id=1, source_target_pairs={{0,3},{1,2},{2,1},{3,0},{4,7},{5,6},{6,5},{7,4},{8,11},{9,10},{10,... | collective-permute-start | bytes 442376 | tf_op jit(solution)/shard_map/ppermute | solution.py:381
  24.7 389.2 %all-gather.9.cloned.1.call-start = ((), (), s32[]{:S(2)}) async-start(), calls=%async_computation.3 | async-start | bytes 10616832 | tf_op jit(solution)/shard_map/all_gather | solution.py:449
  24.7 135.9 %copy-start.34 = (bf16[192]{0:T(256)(128)(2,1)S(1)}, bf16[192]{0:T(256)(128)(2,1)}, u32[]{:S(2)}) copy-start(bf16[192]{0:T(256)(128)(2,1)} %param.14) | copy-start | bytes 1156
  24.8 136.0 %copy-start.35 = (bf16[192]{0:T(256)(128)(2,1)S(1)}, bf16[192]{0:T(256)(128)(2,1)}, u32[]{:S(2)}) copy-start(bf16[192]{0:T(256)(128)(2,1)} %param.19) | copy-start | bytes 1156
  24.8 136.1 %copy-start.26 = (bf16[192,384]{1,0:T(8,128)(2,1)S(1)}, bf16[192,384]{1,0:T(8,128)(2,1)}, u32[]{:S(2)}) copy-start(bf16[192,384]{1,0:T(8,128)(2,1)} %param.15) | copy-start | bytes 442372
  24.8 136.1 %copy-start.27 = (bf16[192,192]{1,0:T(8,128)(2,1)S(1)}, bf16[192,192]{1,0:T(8,128)(2,1)}, u32[]{:S(2)}) copy-start(bf16[192,192]{1,0:T(8,128)(2,1)} %param.16) | copy-start | bytes 221188
  24.8 136.1 %copy-start.29 = (bf16[192,192]{1,0:T(8,128)(2,1)S(1)}, bf16[192,192]{1,0:T(8,128)(2,1)}, u32[]{:S(2)}) copy-start(bf16[192,192]{1,0:T(8,128)(2,1)} %param.17) | copy-start | bytes 221188
  27.2 80.0 %copy-start.8 = (bf16[192,3072]{1,0:T(8,128)(2,1)S(1)}, bf16[192,3072]{1,0:T(8,128)(2,1)}, u32[]{:S(2)}) copy-start(bf16[192,3072]{1,0:T(8,128)(2,1)} %pad_maximum_fusion.3) | copy-start | bytes 3538948
  27.2 414.5 %all-gather.11.cloned.1.call-start = ((), (), s32[]{:S(2)}) async-start(), calls=%async_computation.4 | async-start | bytes 10616832 | tf_op jit(solution)/shard_map/all_gather | solution.py:449
  27.3 26.9 %collective-permute-start.13 = (bf16[192,3072]{1,0:T(8,128)(2,1)}, bf16[192,3072]{1,0:T(8,128)(2,1)S(1)}, u32[]{:S(2)}, u32[]{:S(2)}) collective-permute-start(bf16[192,3072]{1,0:T(8,128)(2,1)} %pad_maximum_fusion.3), channel_id=1, source_target_pairs={{0,1},{1,0},{2,3},{3,2},{4,5},{5,4},{6,7},{7,6},{8,9},{9,8},{10,11... | collective-permute-start | bytes 3538952 | tf_op jit(solution)/shard_map/ppermute | solution.py:381
  55.2 413.1 %all-gather.13.cloned.1.call-start = ((), (), s32[]{:S(2)}) async-start(), calls=%async_computation.5 | async-start | bytes 10616832 | tf_op jit(solution)/shard_map/all_gather | solution.py:449
  55.2 50.9 %collective-permute-start.14 = (bf16[192,3072]{1,0:T(8,128)(2,1)}, bf16[192,3072]{1,0:T(8,128)(2,1)S(1)}, u32[]{:S(2)}, u32[]{:S(2)}) collective-permute-start(bf16[192,3072]{1,0:T(8,128)(2,1)} %pad_maximum_fusion.3), channel_id=1, source_target_pairs={{0,2},{1,3},{2,0},{3,1},{4,6},{5,7},{6,4},{7,5},{8,10},{9,11},{10,... | collective-permute-start | bytes 3538952 | tf_op jit(solution)/shard_map/ppermute | solution.py:381
  107.1 388.0 %all-gather.15.cloned.1.call-start = ((), (), s32[]{:S(2)}) async-start(), calls=%async_computation.6 | async-start | bytes 10616832 | tf_op jit(solution)/shard_map/all_gather | solution.py:449
  107.2 52.3 %collective-permute-start.15 = (bf16[192,3072]{1,0:T(8,128)(2,1)S(1)}, bf16[192,3072]{1,0:T(8,128)(2,1)S(1)}, u32[]{:S(2)}, u32[]{:S(2)}) collective-permute-start(bf16[192,3072]{1,0:T(8,128)(2,1)S(1)} %copy-done.8), channel_id=1, source_target_pairs={{0,3},{1,2},{2,1},{3,0},{4,7},{5,6},{6,5},{7,4},{8,11},{9,10},{10,... | collective-permute-start | bytes 3538952 | tf_op jit(solution)/shard_map/ppermute | solution.py:381
  160.6 647.8 %all-gather.17.cloned.1.call-start = ((), (), s32[]{:S(2)}) async-start(), calls=%async_computation.7 | async-start | bytes 10616832 | tf_op jit(solution)/shard_map/all_gather | solution.py:454
  160.8 22.7 %copy-start.28 = (bf16[192,192]{1,0:T(8,128)(2,1)S(1)}, bf16[192,192]{1,0:T(8,128)(2,1)}, u32[]{:S(2)}) copy-start(bf16[192,192]{1,0:T(8,128)(2,1)} %param.16) | copy-start | bytes 221188
  160.8 22.7 %copy-start.30 = (bf16[192,192]{1,0:T(8,128)(2,1)S(1)}, bf16[192,192]{1,0:T(8,128)(2,1)}, u32[]{:S(2)}) copy-start(bf16[192,192]{1,0:T(8,128)(2,1)} %param.17) | copy-start | bytes 221188
  161.1 11.1 %collective-permute-start = (bf16[192,896]{1,0:T(8,128)(2,1)S(1)}, bf16[192,896]{1,0:T(8,128)(2,1)S(1)}, u32[]{:S(2)}, u32[]{:S(2)}) collective-permute-start(bf16[192,896]{1,0:T(8,128)(2,1)S(1)} %concatenate.49), channel_id=1, source_target_pairs={{0,4},{4,0},{8,12},{12,8},{1,5},{5,1},{9,13},{13,9},{2,6},{6,2},{1... | collective-permute-start | bytes 1032200 | tf_op jit(solution)/shard_map/ppermute | solution.py:381
  162.7 16.6 %collective-permute-start.1 = (bf16[192,896]{1,0:T(8,128)(2,1)S(1)}, bf16[192,896]{1,0:T(8,128)(2,1)S(1)}, u32[]{:S(2)}, u32[]{:S(2)}) collective-permute-start(bf16[192,896]{1,0:T(8,128)(2,1)S(1)} %concatenate.49), channel_id=1, source_target_pairs={{0,8},{4,12},{8,0},{12,4},{1,9},{5,13},{9,1},{13,5},{2,10},{6,14},... | collective-permute-start | bytes 1032200 | tf_op jit(solution)/shard_map/ppermute | solution.py:381
  163.2 20.1 %collective-permute-start.2 = (bf16[192,896]{1,0:T(8,128)(2,1)S(1)}, bf16[192,896]{1,0:T(8,128)(2,1)S(1)}, u32[]{:S(2)}, u32[]{:S(2)}) collective-permute-start(bf16[192,896]{1,0:T(8,128)(2,1)S(1)} %concatenate.49), channel_id=1, source_target_pairs={{0,12},{4,8},{8,4},{12,0},{1,13},{5,9},{9,5},{13,1},{2,14},{6,10},... | collective-permute-start | bytes 1032200 | tf_op jit(solution)/shard_map/ppermute | solution.py:381
  183.3 14.3 %collective-permute-start.3 = (bf16[768,896]{1,0:T(8,128)(2,1)S(1)}, bf16[768,896]{1,0:T(8,128)(2,1)}, u32[]{:S(2)}, u32[]{:S(2)}) collective-permute-start(bf16[768,896]{1,0:T(8,128)(2,1)S(1)} %constant_dynamic-update-slice_fusion.14), channel_id=1, source_target_pairs={{0,16},{16,0},{1,17},{17,1},{2,18},{18,2},{3,19},{19,3},{4,20},{20... | collective-permute-start | bytes 4128776 | tf_op jit(solution)/shard_map/ppermute | solution.py:381
  184.4 122.0 %collective-permute-start.25 = (bf16[192,768]{1,0:T(8,128)(2,1)}, bf16[192,768]{1,0:T(8,128)(2,1)}, u32[]{:S(2)}, u32[]{:S(2)}) collective-permute-start(bf16[192,768]{1,0:T(8,128)(2,1)} %get-tuple-element.98), channel_id=1, source_target_pairs={{0,1},{1,0},{2,3},{3,2},{4,5},{5,4},{6,7},{7,6},{8,9},{9,8},{10,11... | collective-permute-start | bytes 884744 | tf_op jit(solution)/shard_map/ppermute | solution.py:381
  199.6 10.3 %copy-start.31 = (f32[1536]{0:T(1024)}, f32[1536]{0:T(1024)S(1)}, u32[]{:S(2)}) copy-start(f32[1536]{0:T(1024)S(1)} %get-tuple-element.96) | copy-start | bytes 18436
  200.7 13.4 %copy-start.33 = (s32[2,2]{1,0:T(2,128)S(1)}, s32[2,2]{1,0:T(2,128)}, u32[]{:S(2)}) copy-start(s32[2,2]{1,0:T(2,128)} %param.13) | copy-start | bytes 52
  209.9 33.9 %collective-permute-start.4 = (bf16[2,512,384]{2,1,0:T(8,128)(2,1)}, bf16[2,512,384]{2,1,0:T(8,128)(2,1)S(1)}, u32[]{:S(2)}, u32[]{:S(2)}) collective-permute-start(bf16[2,512,384]{2,1,0:T(8,128)(2,1)} %bitcast.69), channel_id=1, source_target_pairs={{0,4},{4,0},{8,12},{12,8},{1,5},{5,1},{9,13},{13,9},{2,6},{6,2},{1... | collective-permute-start | bytes 2359304 | tf_op jit(solution)/shard_map/ppermute | solution.py:381
  212.6 40.4 %collective-permute-start.5 = (bf16[2,512,384]{2,1,0:T(8,128)(2,1)}, bf16[2,512,384]{2,1,0:T(8,128)(2,1)}, u32[]{:S(2)}, u32[]{:S(2)}) collective-permute-start(bf16[2,512,384]{2,1,0:T(8,128)(2,1)} %bitcast.70), channel_id=1, source_target_pairs={{0,8},{4,12},{8,0},{12,4},{1,9},{5,13},{9,1},{13,5},{2,10},{6,14},... | collective-permute-start | bytes 2359304 | tf_op jit(solution)/shard_map/ppermute | solution.py:381
  214.1 59.5 %collective-permute-start.6 = (bf16[2,512,384]{2,1,0:T(8,128)(2,1)}, bf16[2,512,384]{2,1,0:T(8,128)(2,1)}, u32[]{:S(2)}, u32[]{:S(2)}) collective-permute-start(bf16[2,512,384]{2,1,0:T(8,128)(2,1)} %bitcast.71), channel_id=1, source_target_pairs={{0,12},{4,8},{8,4},{12,0},{1,13},{5,9},{9,5},{13,1},{2,14},{6,10},... | collective-permute-start | bytes 2359304 | tf_op jit(solution)/shard_map/ppermute | solution.py:381
  301.4 10.1 %copy-start.11 = (f32[512,192]{1,0:T(8,128)S(1)}, f32[512,192]{1,0:T(8,128)}, u32[]{:S(2)}) copy-start(f32[512,192]{1,0:T(8,128)} %mul.196) | copy-start | bytes 1179652
  301.4 87.7 %collective-permute-start.7 = (bf16[1024,384]{1,0:T(8,128)(2,1)}, bf16[1024,384]{1,0:T(8,128)(2,1)}, u32[]{:S(2)}, u32[]{:S(2)}) collective-permute-start(bf16[1024,384]{1,0:T(8,128)(2,1)} %bitcast.58), channel_id=1, source_target_pairs={{0,1},{1,0},{2,3},{3,2},{4,5},{5,4},{6,7},{7,6},{8,9},{9,8},{10,11... | collective-permute-start | bytes 2359304 | tf_op jit(solution)/shard_map/ppermute | solution.py:381
  303.4 22.4 %collective-permute-start.26 = (bf16[192,768]{1,0:T(8,128)(2,1)}, bf16[192,768]{1,0:T(8,128)(2,1)}, u32[]{:S(2)}, u32[]{:S(2)}) collective-permute-start(bf16[192,768]{1,0:T(8,128)(2,1)} %get-tuple-element.98), channel_id=1, source_target_pairs={{0,2},{1,3},{2,0},{3,1},{4,6},{5,7},{6,4},{7,5},{8,10},{9,11},{10,... | collective-permute-start | bytes 884744 | tf_op jit(solution)/shard_map/ppermute | solution.py:381
  303.4 87.8 %collective-permute-start.8 = (bf16[1024,384]{1,0:T(8,128)(2,1)}, bf16[1024,384]{1,0:T(8,128)(2,1)}, u32[]{:S(2)}, u32[]{:S(2)}) collective-permute-start(bf16[1024,384]{1,0:T(8,128)(2,1)} %bitcast.59), channel_id=1, source_target_pairs={{0,2},{1,3},{2,0},{3,1},{4,6},{5,7},{6,4},{7,5},{8,10},{9,11},{10,... | collective-permute-start | bytes 2359304 | tf_op jit(solution)/shard_map/ppermute | solution.py:381
  306.4 76.3 %collective-permute-start.27 = (bf16[192,768]{1,0:T(8,128)(2,1)}, bf16[192,768]{1,0:T(8,128)(2,1)}, u32[]{:S(2)}, u32[]{:S(2)}) collective-permute-start(bf16[192,768]{1,0:T(8,128)(2,1)} %get-tuple-element.98), channel_id=1, source_target_pairs={{0,3},{1,2},{2,1},{3,0},{4,7},{5,6},{6,5},{7,4},{8,11},{9,10},{10,... | collective-permute-start | bytes 884744 | tf_op jit(solution)/shard_map/ppermute | solution.py:381
  306.4 92.0 %collective-permute-start.9 = (bf16[1024,384]{1,0:T(8,128)(2,1)}, bf16[1024,384]{1,0:T(8,128)(2,1)}, u32[]{:S(2)}, u32[]{:S(2)}) collective-permute-start(bf16[1024,384]{1,0:T(8,128)(2,1)} %bitcast.60), channel_id=1, source_target_pairs={{0,3},{1,2},{2,1},{3,0},{4,7},{5,6},{6,5},{7,4},{8,11},{9,10},{10,... | collective-permute-start | bytes 2359304 | tf_op jit(solution)/shard_map/ppermute | solution.py:381
  384.8 447.8 %reduce-scatter.7.cloned.1.call-start = ((), (), s32[]{:S(2)}) async-start(), calls=%async_computation.8 | async-start | bytes 4423680
  386.9 13.6 %copy-start.2 = (bf16[2,512,1536]{2,1,0:T(8,128)(2,1)S(1)}, bf16[2,512,1536]{2,1,0:T(8,128)(2,1)}, u32[]{:S(2)}) copy-start(bf16[2,512,1536]{2,1,0:T(8,128)(2,1)} %param.12) | copy-start | bytes 9437188
  495.1 26.6 %copy-start.5 = (bf16[1024,1536]{1,0:T(8,128)(2,1)S(1)}, bf16[1024,1536]{1,0:T(8,128)(2,1)}, u32[]{:S(2)}) copy-start(bf16[1024,1536]{1,0:T(8,128)(2,1)} %get-tuple-element.36) | copy-start | bytes 9437188
  495.2 26.6 %copy-start.7 = (bf16[1024,1536]{1,0:T(8,128)(2,1)S(1)}, bf16[1024,1536]{1,0:T(8,128)(2,1)}, u32[]{:S(2)}) copy-start(bf16[1024,1536]{1,0:T(8,128)(2,1)} %get-tuple-element.37) | copy-start | bytes 9437188
  521.7 6.4 copy-start.6
  542.8 46.7 %copy-start = (f32[1024,1536]{1,0:T(8,128)}, f32[1024,1536]{1,0:T(8,128)S(1)}, u32[]{:S(2)}) copy-start(f32[1024,1536]{1,0:T(8,128)S(1)} %get-tuple-element.99) | copy-start | bytes 18874372
  581.5 5.6 copy-start.22
  583.5 20.5 %collective-permute-start.16 = (bf16[2,512,384]{2,1,0:T(8,128)(2,1)S(1)}, bf16[2,512,384]{2,1,0:T(8,128)(2,1)S(1)}, u32[]{:S(2)}, u32[]{:S(2)}) collective-permute-start(bf16[2,512,384]{2,1,0:T(8,128)(2,1)S(1)} %get-tuple-element.103), channel_id=1, source_target_pairs={{0,4},{4,0},{8,12},{12,8},{1,5},{5,1},{9,13},{13,9},{2,6},{6,2},{1... | collective-permute-start | bytes 2359304 | tf_op jit(solution)/shard_map/ppermute | solution.py:381
  585.1 35.1 %collective-permute-start.17 = (bf16[2,512,384]{2,1,0:T(8,128)(2,1)S(1)}, bf16[2,512,384]{2,1,0:T(8,128)(2,1)S(1)}, u32[]{:S(2)}, u32[]{:S(2)}) collective-permute-start(bf16[2,512,384]{2,1,0:T(8,128)(2,1)S(1)} %get-tuple-element.102), channel_id=1, source_target_pairs={{0,8},{4,12},{8,0},{12,4},{1,9},{5,13},{9,1},{13,5},{2,10},{6,14},... | collective-permute-start | bytes 2359304 | tf_op jit(solution)/shard_map/ppermute | solution.py:381
  585.7 35.3 %collective-permute-start.18 = (bf16[2,512,384]{2,1,0:T(8,128)(2,1)S(1)}, bf16[2,512,384]{2,1,0:T(8,128)(2,1)}, u32[]{:S(2)}, u32[]{:S(2)}) collective-permute-start(bf16[2,512,384]{2,1,0:T(8,128)(2,1)S(1)} %get-tuple-element.101), channel_id=1, source_target_pairs={{0,12},{4,8},{8,4},{12,0},{1,13},{5,9},{9,5},{13,1},{2,14},{6,10},... | collective-permute-start | bytes 2359304 | tf_op jit(solution)/shard_map/ppermute | solution.py:381
  591.0 34.0 %copy-start.37 = (bf16[1024,1536]{1,0:T(8,128)(2,1)S(1)}, bf16[1024,1536]{1,0:T(8,128)(2,1)}, u32[]{:S(2)}) copy-start(bf16[1024,1536]{1,0:T(8,128)(2,1)} %get-tuple-element.43) | copy-start | bytes 9437188
  604.1 16.9 %copy-start.24 = (bf16[2,512,384]{2,1,0:T(8,128)(2,1)}, bf16[2,512,384]{2,1,0:T(8,128)(2,1)S(1)}, u32[]{:S(2)}) copy-start(bf16[2,512,384]{2,1,0:T(8,128)(2,1)S(1)} %collective-permute-done.16.refs_1_) | copy-start | bytes 2359300
  636.3 201.7 %reduce-scatter.9.cloned.1.call-start = ((), (), s32[]{:S(2)}) async-start(), calls=%async_computation.9 | async-start | bytes 10616832
  638.1 5.7 copy-start.39
  668.6 35.4 %copy-start.3 = (bf16[2,512,1536]{2,1,0:T(8,128)(2,1)S(1)}, bf16[2,512,1536]{2,1,0:T(8,128)(2,1)}, u32[]{:S(2)}) copy-start(bf16[2,512,1536]{2,1,0:T(8,128)(2,1)} %param.12) | copy-start | bytes 9437188
  668.6 35.0 %collective-permute-start.19 = (bf16[1024,384]{1,0:T(8,128)(2,1)}, bf16[1024,384]{1,0:T(8,128)(2,1)}, u32[]{:S(2)}, u32[]{:S(2)}) collective-permute-start(bf16[1024,384]{1,0:T(8,128)(2,1)} %bitcast.73), channel_id=1, source_target_pairs={{0,1},{1,0},{2,3},{3,2},{4,5},{5,4},{6,7},{7,6},{8,9},{9,8},{10,11... | collective-permute-start | bytes 2359304 | tf_op jit(solution)/shard_map/ppermute | solution.py:381
  668.7 62.4 %collective-permute-start.20 = (bf16[1024,384]{1,0:T(8,128)(2,1)}, bf16[1024,384]{1,0:T(8,128)(2,1)}, u32[]{:S(2)}, u32[]{:S(2)}) collective-permute-start(bf16[1024,384]{1,0:T(8,128)(2,1)} %bitcast.65), channel_id=1, source_target_pairs={{0,1},{1,0},{2,3},{3,2},{4,5},{5,4},{6,7},{7,6},{8,9},{9,8},{10,11... | collective-permute-start | bytes 2359304 | tf_op jit(solution)/shard_map/ppermute | solution.py:381
  670.7 63.2 %collective-permute-start.21 = (bf16[1024,384]{1,0:T(8,128)(2,1)}, bf16[1024,384]{1,0:T(8,128)(2,1)}, u32[]{:S(2)}, u32[]{:S(2)}) collective-permute-start(bf16[1024,384]{1,0:T(8,128)(2,1)} %bitcast.74), channel_id=1, source_target_pairs={{0,2},{1,3},{2,0},{3,1},{4,6},{5,7},{6,4},{7,5},{8,10},{9,11},{10,... | collective-permute-start | bytes 2359304 | tf_op jit(solution)/shard_map/ppermute | solution.py:381
  670.7 122.3 %collective-permute-start.23 = (bf16[1024,384]{1,0:T(8,128)(2,1)}, bf16[1024,384]{1,0:T(8,128)(2,1)}, u32[]{:S(2)}, u32[]{:S(2)}) collective-permute-start(bf16[1024,384]{1,0:T(8,128)(2,1)} %bitcast.75), channel_id=1, source_target_pairs={{0,3},{1,2},{2,1},{3,0},{4,7},{5,6},{6,5},{7,4},{8,11},{9,10},{10,... | collective-permute-start | bytes 2359304 | tf_op jit(solution)/shard_map/ppermute | solution.py:381
  672.2 117.9 %collective-permute-start.22 = (bf16[1024,384]{1,0:T(8,128)(2,1)}, bf16[1024,384]{1,0:T(8,128)(2,1)}, u32[]{:S(2)}, u32[]{:S(2)}) collective-permute-start(bf16[1024,384]{1,0:T(8,128)(2,1)} %bitcast.66), channel_id=1, source_target_pairs={{0,2},{1,3},{2,0},{3,1},{4,6},{5,7},{6,4},{7,5},{8,10},{9,11},{10,... | collective-permute-start | bytes 2359304 | tf_op jit(solution)/shard_map/ppermute | solution.py:381
  703.6 102.0 %collective-permute-start.24 = (bf16[1024,384]{1,0:T(8,128)(2,1)}, bf16[1024,384]{1,0:T(8,128)(2,1)}, u32[]{:S(2)}, u32[]{:S(2)}) collective-permute-start(bf16[1024,384]{1,0:T(8,128)(2,1)} %bitcast.67), channel_id=1, source_target_pairs={{0,3},{1,2},{2,1},{3,0},{4,7},{5,6},{6,5},{7,4},{8,11},{9,10},{10,... | collective-permute-start | bytes 2359304 | tf_op jit(solution)/shard_map/ppermute | solution.py:381
  733.9 74.5 %copy-start.32 = (f32[1536]{0:T(1024)S(1)}, f32[1536]{0:T(1024)}, u32[]{:S(2)}) copy-start(f32[1536]{0:T(1024)} %copy-done.31) | copy-start | bytes 18436
  808.4 20.2 %slice-start = ((s8[6291456]{0:T(1024)(128)(4,1)}), s8[4194304]{0:T(1024)(128)(4,1)S(1)}, s32[]{:S(2)}) async-start(s8[6291456]{0:T(1024)(128)(4,1)} %bitcast.48), calls=%async_computation.10 | async-start | bytes 8388608
  808.4 20.2 %slice-start.1 = ((s8[6291456]{0:T(1024)(128)(4,1)}), s8[2097152]{0:T(1024)(128)(4,1)S(1)}, s32[]{:S(2)}) async-start(s8[6291456]{0:T(1024)(128)(4,1)} %bitcast.48), calls=%async_computation.11 | async-start | bytes 4194304
  823.9 1.2 collective-permute-start.28
  825.1 6.8 collective-permute-start.29
  825.1 6.8 collective-permute-start.30
  825.9 6.0 collective-permute-start.31
  (18 other events, 43.8 us)
Sparse Core Ops, SparseCore 0:
  24.8 38.8 all-gather.6
  65.6 58.5 all-gather.8
  126.1 79.0 all-gather.10
  207.0 82.1 all-gather.12
  290.9 57.4 all-gather.14
  384.9 58.0 all-gather.16
  636.4 48.3 reduce-scatter.6
  688.7 76.4 reduce-scatter.8

commit v2 on v1

v2 whole, which is shorter than its diff:
```python
import functools
import math

import jax
import jax.numpy as jnp
from jax import lax
from jax.experimental import pallas as pl
from jax.experimental.pallas import tpu as pltpu
from jax.sharding import PartitionSpec as P

HEAD_SIZE = 96
PIECE = 256

EPSILON = 1e-05
ROPE_BASE = 100000.0
NEGATIVE = -1e30
F32 = jnp.float32
BF16 = jnp.bfloat16
LANES = 128
VMEM_LIMIT = 56 << 20
COST_SCALE = 3


def nt(left, right):
    return lax.dot_general(left, right, (((1,), (1,)), ((), ())), preferred_element_type=F32)


def nn(left, right):
    return jnp.dot(left, right, preferred_element_type=F32)


def params():
    return pltpu.CompilerParams(vmem_limit_bytes=VMEM_LIMIT)


def cost(flops, bytes_accessed, transcendentals=0):
    return pl.CostEstimate(
        flops=int(flops * COST_SCALE),
        bytes_accessed=int(bytes_accessed * COST_SCALE),
        transcendentals=int(transcendentals * COST_SCALE),
    )


def columns(array, start, size):
    if size % LANES or start % size:
        array, start = array[:, start : start + size], 0
    return array, pl.BlockSpec((array.shape[0], size), lambda r: (0, start // size))


def turn(value, cosine, sine):
    half = HEAD_SIZE // 2
    width = value.shape[-1]
    lane = lax.broadcasted_iota(jnp.int32, (1, width), 1) % HEAD_SIZE
    other = jnp.where(
        jnp.broadcast_to(lane, value.shape) < half, pltpu.roll(value, width - half, 1), pltpu.roll(value, half, 1)
    )
    return value * cosine + other * sine


def project_kernel(q_width, rows_ref, gain_ref, weight_ref, cos_ref, sin_ref, normed_ref, q_ref, kv_ref):
    rows = rows_ref[...].astype(F32)
    inverse = lax.rsqrt(jnp.mean(rows * rows, axis=-1, keepdims=True) + EPSILON)
    normed = (rows * inverse * gain_ref[...]).astype(BF16)
    normed_ref[...] = normed
    turned = turn(nn(normed, weight_ref[...]), cos_ref[...], sin_ref[...]).astype(BF16)
    q_ref[...] = turned[:, :q_width]
    kv_ref[...] = turned[:, q_width:]


def project(inputs, gain, weights, cosine, sine, q_width, row_tile=256):
    rows, width = inputs.shape
    out_width = cosine.shape[1]
    per_seq = cosine.shape[0] // row_tile
    table = pl.BlockSpec((row_tile, out_width), lambda r: (r % per_seq, 0))
    return pl.pallas_call(
        functools.partial(project_kernel, q_width),
        grid=(rows // row_tile,),
        in_specs=[
            pl.BlockSpec((row_tile, width), lambda r: (r, 0)),
            pl.BlockSpec((1, width), lambda r: (0, 0)),
            pl.BlockSpec((width, out_width), lambda r: (0, 0)),
            table,
            table,
        ],
        out_specs=[
            pl.BlockSpec((row_tile, width), lambda r: (r, 0)),
            pl.BlockSpec((row_tile, q_width), lambda r: (r, 0)),
            pl.BlockSpec((row_tile, out_width - q_width), lambda r: (r, 0)),
        ],
        out_shape=[
            jax.ShapeDtypeStruct((rows, width), BF16),
            jax.ShapeDtypeStruct((rows, q_width), BF16),
            jax.ShapeDtypeStruct((rows, out_width - q_width), BF16),
        ],
        compiler_params=params(),
        cost_estimate=cost(2 * rows * width * out_width, 4 * rows * width + 2 * width * out_width),
        name="project",
    )(inputs, gain, weights, cosine, sine)


def stacked(block, group, repeat):
    first = group * repeat
    return jnp.concatenate(
        [
            block[:, (first + r) * HEAD_SIZE : (first + r + 1) * HEAD_SIZE]
            for r in range(repeat)
        ],
        axis=0,
    )


def side_by_side(groups, repeat, tile):
    return jnp.concatenate(
        [g[r * tile : (r + 1) * tile] for g in groups for r in range(repeat)], axis=1
    )


def attend_kernel(n_groups, repeat, n_blocks, bases_ref, q_ref, limit_ref, *refs):
    kv_refs = refs[:n_blocks]
    mixed_ref, lse_ref, k_s, vt_s = refs[n_blocks:]
    tile = q_ref.shape[0]
    block = kv_refs[0].shape[0]
    cols = repeat * tile
    kv_width = n_groups * HEAD_SIZE
    factor = HEAD_SIZE ** (-0.5) * math.log2(math.e)

    @pl.when(pl.program_id(0) == 0)
    def _():
        for j, ref in enumerate(kv_refs):
            for g in range(n_groups):
                first = g * HEAD_SIZE
                k_s[g, j] = ref[:, first : first + HEAD_SIZE]
                vt_s[g, j] = ref[:, kv_width + first : kv_width + first + HEAD_SIZE].T

    limit = jnp.concatenate([limit_ref[0, 0]] * repeat, axis=1)
    offset = lax.broadcasted_iota(jnp.int32, (block, cols), 0)
    results = []
    for g in range(n_groups):
        q = stacked(q_ref[...], g, repeat)
        blocks = []
        for j in range(n_blocks):
            scores = nt(k_s[g, j], q) * factor
            blocks.append(jnp.where(offset <= limit - bases_ref[j], scores, NEGATIVE))
        top = functools.reduce(
            jnp.maximum, [jnp.max(x, axis=0, keepdims=True) for x in blocks]
        )
        total = jnp.zeros((1, cols), F32)
        acc = jnp.zeros((HEAD_SIZE, cols), F32)
        for j in range(n_blocks):
            probs = jnp.exp2(blocks[j] - top)
            total = total + jnp.sum(probs, axis=0, keepdims=True)
            acc = acc + nn(vt_s[g, j], probs.astype(BF16))
        lse_ref[0, g : g + 1, :] = top + jnp.log2(total)
        results.append((acc / total).T)
    mixed_ref[...] = side_by_side(results, repeat, tile).astype(BF16)


def attend(query, kv_pieces, limits, bases, seq):
    _, toks, q_width = query.shape
    n_blocks = len(kv_pieces)
    block, kv_cols = toks, kv_pieces[0].shape[1]
    n_groups = kv_cols // (2 * HEAD_SIZE)
    repeat = q_width // HEAD_SIZE // n_groups
    n_tiles = toks // TILE
    length = block * n_blocks
    return pl.pallas_call(
        functools.partial(attend_kernel, n_groups, repeat, n_blocks),
        grid_spec=pltpu.PrefetchScalarGridSpec(
            num_scalar_prefetch=1,
            grid=(n_tiles,),
            in_specs=[
                pl.BlockSpec((None, TILE, q_width), lambda t, _: (seq, t, 0)),
                pl.BlockSpec((1, 1, 1, TILE), lambda t, _: (seq, t, 0, 0)),
            ]
            + [pl.BlockSpec((block, kv_cols), lambda t, _: (seq, 0))] * n_blocks,
            out_specs=[
                pl.BlockSpec((TILE, q_width), lambda t, _: (t, 0)),
                pl.BlockSpec((1, n_groups, repeat * TILE), lambda t, _: (t, 0, 0)),
            ],
            scratch_shapes=[
                pltpu.VMEM((n_groups, n_blocks, block, HEAD_SIZE), BF16),
                pltpu.VMEM((n_groups, n_blocks, HEAD_SIZE, block), BF16),
            ],
        ),
        out_shape=[
            jax.ShapeDtypeStruct((toks, q_width), BF16),
            jax.ShapeDtypeStruct((n_tiles, n_groups, repeat * TILE), F32),
        ],
        compiler_params=params(),
        cost_estimate=cost(
            4 * toks * length * 256 * n_groups * repeat,
            4 * toks * q_width + 2 * length * kv_cols,
            toks * length * n_groups * repeat,
        ),
        name="attend",
    )(bases, query, limits, *kv_pieces)


def attend_back_kernel(n_groups, repeat, n_blocks, bases_ref, q_ref, limit_ref, lse_ref, mixed_ref, grad_ref, cos_ref, sin_ref, *refs):
    kv_refs, refs = refs[:n_blocks], refs[n_blocks:]
    dq_ref, dkv_ref, k_s, v_s, kt_s, dk_s, dv_s = refs
    tile = q_ref.shape[0]
    block = kv_refs[0].shape[0]
    cols = repeat * tile
    kv_width = n_groups * HEAD_SIZE
    scale = HEAD_SIZE ** (-0.5)
    factor = scale * math.log2(math.e)

    @pl.when(pl.program_id(0) == 0)
    def _():
        for j, ref in enumerate(kv_refs):
            for g in range(n_groups):
                first = g * HEAD_SIZE
                k = ref[:, first : first + HEAD_SIZE]
                k_s[g, j] = k
                kt_s[g, j] = k.T
                v_s[g, j] = ref[:, kv_width + first : kv_width + first + HEAD_SIZE]
        dk_s[...] = jnp.zeros_like(dk_s)
        dv_s[...] = jnp.zeros_like(dv_s)

    limit = jnp.concatenate([limit_ref[0, 0]] * repeat, axis=1)
    offset = lax.broadcasted_iota(jnp.int32, (block, cols), 0)
    ones = jnp.ones((8, HEAD_SIZE), BF16)
    results = []
    for g in range(n_groups):
        q = stacked(q_ref[...], g, repeat)
        grad = stacked(grad_ref[...], g, repeat)
        mixed = stacked(mixed_ref[...], g, repeat)
        product = grad.astype(F32) * mixed.astype(F32)
        high = product.astype(BF16)
        low = (product - high.astype(F32)).astype(BF16)
        delta = (nt(ones, high) + nt(ones, low))[0:1]
        lse = lse_ref[0, g : g + 1, :]
        dqt = jnp.zeros((HEAD_SIZE, cols), F32)
        for j in range(n_blocks):
            scores = nt(k_s[g, j], q) * factor - lse
            probs = jnp.where(offset <= limit - bases_ref[j], jnp.exp2(scores), 0.0)
            grad_soft = nt(v_s[g, j], grad)
            grad_scores = (probs * (grad_soft - delta)).astype(BF16)
            dv_s[g, j] += nn(probs.astype(BF16), grad)
            dk_s[g, j] += nn(grad_scores, q)
            dqt = dqt + nn(kt_s[g, j], grad_scores)
        results.append(dqt.T * scale)
    dq_ref[...] = turn(side_by_side(results, repeat, tile), cos_ref[...], -sin_ref[...]).astype(BF16)

    @pl.when(pl.program_id(0) == pl.num_programs(0) - 1)
    def _():
        for j in range(n_blocks):
            rows = pl.ds(pl.multiple_of(bases_ref[j], block), block)
            dkv_ref[rows, :] = jnp.concatenate(
                [(dk_s[g, j] * scale).astype(BF16) for g in range(n_groups)]
                + [dv_s[g, j].astype(BF16) for g in range(n_groups)],
                axis=1,
            )


def attend_back(query, kv_pieces, limits, lse, mixed, grad, cosine, sine, bases, seq):
    _, toks, q_width = query.shape
    n_blocks = len(kv_pieces)
    block, kv_cols = toks, kv_pieces[0].shape[1]
    n_groups = kv_cols // (2 * HEAD_SIZE)
    repeat = q_width // HEAD_SIZE // n_groups
    n_tiles = toks // TILE
    length = block * n_blocks
    rows = pl.BlockSpec((TILE, q_width), lambda t, _: (t, 0))
    kv_piece = pl.BlockSpec((block, kv_cols), lambda t, _: (seq, 0))
    return pl.pallas_call(
        functools.partial(attend_back_kernel, n_groups, repeat, n_blocks),
        grid_spec=pltpu.PrefetchScalarGridSpec(
            num_scalar_prefetch=1,
            grid=(n_tiles,),
            in_specs=[
                pl.BlockSpec((None, TILE, q_width), lambda t, _: (seq, t, 0)),
                pl.BlockSpec((1, 1, 1, TILE), lambda t, _: (seq, t, 0, 0)),
                pl.BlockSpec((1, n_groups, repeat * TILE), lambda t, _: (t, 0, 0)),
                rows,
                rows,
                rows,
                rows,
            ]
            + [kv_piece] * n_blocks,
            out_specs=[rows, pl.BlockSpec((length, kv_cols), lambda t, _: (0, 0))],
            scratch_shapes=[
                pltpu.VMEM((n_groups, n_blocks, block, HEAD_SIZE), BF16),
                pltpu.VMEM((n_groups, n_blocks, block, HEAD_SIZE), BF16),
                pltpu.VMEM((n_groups, n_blocks, HEAD_SIZE, block), BF16),
                pltpu.VMEM((n_groups, n_blocks, block, HEAD_SIZE), F32),
                pltpu.VMEM((n_groups, n_blocks, block, HEAD_SIZE), F32),
            ],
        ),
        out_shape=[
            jax.ShapeDtypeStruct((toks, q_width), BF16),
            jax.ShapeDtypeStruct((length, kv_cols), BF16),
        ],
        compiler_params=params(),
        cost_estimate=cost(
            10 * toks * length * 256 * n_groups * repeat,
            8 * toks * q_width + 4 * length * kv_cols,
            toks * length * n_groups * repeat,
        ),
        name="attend_back",
    )(bases, query, limits, lse, mixed, grad, cosine, sine, *kv_pieces)


def project_back_kernel(query_ref, cos_ref, sin_ref, weight_ref, terms_ref, kv_ref, part_ref):
    total = jnp.sum(terms_ref[...].astype(F32), axis=0)
    kv = turn(total, cos_ref[...], -sin_ref[...]).astype(BF16)
    kv_ref[...] = kv
    both = jnp.concatenate([query_ref[...], kv], axis=1)
    part_ref[...] = nt(both, weight_ref[...]).astype(BF16)


def project_back(query, terms, cosine, sine, weights):
    toks, kv_cols = cosine.shape
    count = terms.shape[0] // toks
    width, columns = weights.shape[0], query.shape[1] + kv_cols

    def whole(rows, cols):
        return pl.BlockSpec((rows, cols), lambda r: (0, 0))

    return pl.pallas_call(
        project_back_kernel,
        grid=(1,),
        in_specs=[
            whole(*query.shape),
            whole(toks, kv_cols),
            whole(toks, kv_cols),
            whole(width, columns),
            pl.BlockSpec((count, toks, kv_cols), lambda r: (0, 0, 0)),
        ],
        out_specs=[whole(toks, kv_cols), whole(toks, width)],
        out_shape=[
            jax.ShapeDtypeStruct((toks, kv_cols), BF16),
            jax.ShapeDtypeStruct((toks, width), BF16),
        ],
        compiler_params=params(),
        cost_estimate=cost(2 * toks * width * columns, 2 * width * (toks + columns)),
        name="project_back",
    )(query, cosine, sine, weights, terms.reshape(count, toks, kv_cols))


def middle_kernel(count, rows_ref, gain_ref, weight_ref, *refs):
    middle_ref, normed_ref = refs[count:]
    mixed = jnp.concatenate([ref[...] for ref in refs[:count]], axis=1)
    middle = rows_ref[...].astype(F32) + nt(mixed, weight_ref[...])
    inverse = lax.rsqrt(jnp.mean(middle * middle, axis=-1, keepdims=True) + EPSILON)
    middle_ref[...] = middle
    normed_ref[...] = (middle * inverse * gain_ref[...]).astype(BF16)


def middle_of(inputs, gain, weights, start, pieces, seq, row_tile=256):
    width = inputs.shape[1]
    toks, q_width = pieces[0].shape
    steps = toks // row_tile
    rows = pl.BlockSpec((row_tile, width), lambda r: (r, 0))
    weights, weight_spec = columns(weights, start, q_width * len(pieces))
    return pl.pallas_call(
        functools.partial(middle_kernel, len(pieces)),
        grid=(steps,),
        in_specs=[
            pl.BlockSpec((row_tile, width), lambda r: (seq * steps + r, 0)),
            pl.BlockSpec((1, width), lambda r: (0, 0)),
            weight_spec,
        ]
        + [pl.BlockSpec((row_tile, q_width), lambda r: (r, 0))] * len(pieces),
        out_specs=[rows, rows],
        out_shape=[
            jax.ShapeDtypeStruct((toks, width), F32),
            jax.ShapeDtypeStruct((toks, width), BF16),
        ],
        compiler_params=params(),
        cost_estimate=cost(
            2 * toks * width * width, 10 * toks * width + 2 * width * width
        ),
        name="middle_of",
    )(inputs, gain, weights, *pieces)


def ffn_kernel(keep, based, groups, normed_ref, grad_ref, *refs):
    weight_refs, refs = refs[: 3 * groups], refs[3 * groups :]
    normed, grad = normed_ref[...], grad_ref[...]
    out = back = None
    if based:
        out, back = refs[0][...].astype(F32), refs[1][...].astype(F32)
        refs = refs[2:]
    for g in range(groups):
        gate_w, up_w, down_w = [ref[...] for ref in weight_refs[3 * g : 3 * g + 3]]
        gate = nn(normed, gate_w)
        up = nn(normed, up_w)
        grad_hidden = nn(grad, down_w)
        sig = jax.nn.sigmoid(gate)
        silu = gate * sig
        hidden = (silu * up).astype(BF16)
        grad_gate = (grad_hidden * up * (sig + silu * (1.0 - sig))).astype(BF16)
        grad_up = (grad_hidden * silu).astype(BF16)
        out_g = nt(hidden, down_w)
        back_g = nt(grad_gate, gate_w) + nt(grad_up, up_w)
        out = out_g if out is None else out + out_g
        back = back_g if back is None else back + back_g
        if keep and g == 0:
            refs[2][...] = jnp.concatenate([grad_gate, grad_up, hidden], axis=1)
    refs[0][...] = out.astype(BF16)
    refs[1][...] = back.astype(BF16)


def ffn_groups(normed, grad, weights, hidden, seq, base, keep, row_tile=256):
    toks, width = normed.shape
    steps = toks // row_tile
    groups = len(weights)
    rows = pl.BlockSpec((row_tile, width), lambda r: (r, 0))
    kept = pl.BlockSpec((row_tile, 3 * hidden), lambda r: (r, 0))
    wide = jax.ShapeDtypeStruct((toks, width), BF16)
    return pl.pallas_call(
        functools.partial(ffn_kernel, keep, bool(base), groups),
        grid=(steps,),
        in_specs=[rows, pl.BlockSpec((row_tile, width), lambda r: (seq * steps + r, 0))]
        + [
            pl.BlockSpec((width, hidden), lambda r, c=c: (0, c), pipeline_mode=pl.Buffered(1))
            for _ in weights
            for c in range(3)
        ]
        + [rows] * len(base),
        out_specs=[rows, rows] + [kept] * int(keep),
        out_shape=[wide, wide] + [jax.ShapeDtypeStruct((toks, 3 * hidden), BF16)] * int(keep),
        compiler_params=params(),
        cost_estimate=cost(
            12 * groups * toks * width * hidden,
            8 * toks * width + 6 * groups * width * hidden,
            groups * toks * hidden,
        ),
        name="ffn_groups",
    )(normed, grad, *[w for w in weights for _ in range(3)], *base)


def grad_middle_kernel(count, middle_ref, grad_ref, gain_ref, weight_ref, *refs):
    wide_ref, attn_ref, mixed_ref, gain_grad_ref = refs[count:]
    middle = middle_ref[...]
    inverse = lax.rsqrt(jnp.mean(middle * middle, axis=-1, keepdims=True) + EPSILON)
    hat = middle * inverse
    back = refs[0][...].astype(F32)
    for ref in refs[1:count]:
        back = back + ref[...].astype(F32)
    scaled = back * gain_ref[...]
    total = grad_ref[...].astype(F32) + inverse * (
        scaled - hat * jnp.mean(scaled * hat, axis=-1, keepdims=True)
    )
    wide_ref[...] = total
    attn = total.astype(BF16)
    attn_ref[...] = attn
    mixed_ref[...] = nn(attn, weight_ref[...]).astype(BF16)
    part = jnp.sum(back * hat, axis=0, keepdims=True)

    @pl.when(pl.program_id(0) == 0)
    def _():
        gain_grad_ref[...] = part

    @pl.when(pl.program_id(0) > 0)
    def _():
        gain_grad_ref[...] += part


def grad_middle_of(middle, grad, gain, weights, start, backs, q_width, seq, row_tile=256):
    toks, width = middle.shape
    steps = toks // row_tile
    rows = pl.BlockSpec((row_tile, width), lambda r: (r, 0))
    line = pl.BlockSpec((1, width), lambda r: (0, 0))
    weights, weight = columns(weights, start, q_width)
    return pl.pallas_call(
        functools.partial(grad_middle_kernel, len(backs)),
        grid=(steps,),
        in_specs=[
            rows,
            pl.BlockSpec((row_tile, width), lambda r: (seq * steps + r, 0)),
            line,
            weight,
        ]
        + [rows] * len(backs),
        out_specs=[rows, rows, pl.BlockSpec((row_tile, q_width), lambda r: (r, 0)), line],
        out_shape=[
            jax.ShapeDtypeStruct((toks, width), F32),
            jax.ShapeDtypeStruct((toks, width), BF16),
            jax.ShapeDtypeStruct((toks, q_width), BF16),
            jax.ShapeDtypeStruct((1, width), F32),
        ],
        compiler_params=params(),
        cost_estimate=cost(2 * toks * width * q_width, 16 * toks * width),
        name="grad_middle_of",
    )(middle, grad, gain, weights, *backs)


def weight_grad_kernel(n_seqs, tile, split, *refs):
    lefts, others, rights = refs[:n_seqs], refs[n_seqs : 2 * n_seqs], refs[2 * n_seqs : 3 * n_seqs]
    out_ref, left_s, other_s = refs[3 * n_seqs :]
    toks = lefts[0].shape[0]

    @pl.when(pl.program_id(0) == 0)
    def _():
        for s in range(n_seqs):
            left_s[:, s * toks : (s + 1) * toks] = lefts[s][...].T
            other_s[:, s * toks : (s + 1) * toks] = others[s][...].T

    right = jnp.concatenate([ref[...] for ref in rights], axis=0)
    if split % tile:
        out_ref[...] = jnp.concatenate(
            [nn(left_s[...], right[:, :split]), nn(other_s[...], right[:, split:])], axis=1
        ).astype(BF16)
        return
    first = pl.program_id(0) < split // tile

    @pl.when(first)
    def _():
        out_ref[...] = nn(left_s[...], right).astype(BF16)

    @pl.when(jnp.logical_not(first))
    def _():
        out_ref[...] = nn(other_s[...], right).astype(BF16)


def weight_grad(lefts, others, rights, split, tile):
    toks, width = lefts[0].shape
    columns = rights[0].shape[1]
    if tile % LANES or columns % tile or split % tile:
        tile = columns
    n_seqs = len(lefts)
    whole = pl.BlockSpec((toks, width), lambda c: (0, 0))
    return pl.pallas_call(
        functools.partial(weight_grad_kernel, n_seqs, tile, split),
        grid=(columns // tile,),
        in_specs=[whole] * (2 * n_seqs)
        + [pl.BlockSpec((toks, tile), lambda c: (0, c))] * n_seqs,
        out_specs=pl.BlockSpec((width, tile), lambda c: (0, c)),
        out_shape=jax.ShapeDtypeStruct((width, columns), BF16),
        scratch_shapes=[pltpu.VMEM((width, n_seqs * toks), BF16)] * 2,
        compiler_params=params(),
        cost_estimate=cost(
            2 * n_seqs * toks * width * columns,
            2 * n_seqs * toks * (2 * width + columns) + 2 * width * columns,
        ),
        name="weight_grad",
    )(*lefts, *others, *rights)


def grad_inputs_kernel(rows_ref, wide_ref, gain_ref, terms_ref, out_ref, gain_grad_ref):
    rows = rows_ref[...].astype(F32)
    inverse = lax.rsqrt(jnp.mean(rows * rows, axis=-1, keepdims=True) + EPSILON)
    hat = rows * inverse
    back = jnp.sum(terms_ref[...].astype(F32), axis=0)
    scaled = back * gain_ref[...]
    total = wide_ref[...] + inverse * (
        scaled - hat * jnp.mean(scaled * hat, axis=-1, keepdims=True)
    )
    out_ref[...] = total.astype(BF16)
    gain_grad_ref[...] = jnp.sum(back * hat, axis=0, keepdims=True)


def grad_inputs_of(inputs, wide, gain, terms):
    toks, width = inputs.shape
    return pl.pallas_call(
        grad_inputs_kernel,
        out_shape=[
            jax.ShapeDtypeStruct((toks, width), BF16),
            jax.ShapeDtypeStruct((1, width), F32),
        ],
        compiler_params=params(),
        cost_estimate=cost(0, 16 * toks * width),
        name="grad_inputs_of",
    )(inputs, wide, gain, terms.reshape(-1, toks, width))


TILE = 128


def rotation_tables(positions, turned, plain):
    half = HEAD_SIZE // 2
    lane = jnp.arange((turned + plain) * HEAD_SIZE, dtype=jnp.int32)
    inverse = jnp.exp(
        (lane % half).astype(F32) * (-2.0 * math.log(ROPE_BASE) / HEAD_SIZE)
    )
    turns = lane < turned * HEAD_SIZE
    angles = positions.astype(F32)[:, None] * inverse[None, :]
    sign = jnp.where(turns, jnp.where(lane % HEAD_SIZE < half, -1.0, 1.0), 0.0)
    return jnp.where(turns, jnp.cos(angles), 1.0), jnp.sin(angles) * sign


def last_allowed(positions, start_row):
    begin = start_row[:, None, :]
    inside = (positions[None, :, None] >= begin) & (positions[None, :, None] < begin + PIECE)
    ends = jnp.where(inside, begin + PIECE - 1, -1)
    return jnp.maximum(positions[None, :], jnp.max(ends, axis=-1)).astype(jnp.int32)


def swap(value, axis, step):
    count = lax.axis_size(axis)
    return lax.ppermute(value, axis, [(i, i ^ step) for i in range(count)])


def partners(value, axis):
    return [value] + [swap(value, axis, j) for j in range(1, lax.axis_size(axis))]


def place(pieces, axis, dim):
    me = lax.axis_index(axis)
    width = pieces[0].shape[dim]
    shape = list(pieces[0].shape)
    shape[dim] = width * len(pieces)
    whole = jnp.zeros(shape, pieces[0].dtype)
    for j, piece in enumerate(pieces):
        whole = lax.dynamic_update_slice_in_dim(whole, piece, (me ^ j) * width, dim)
    return whole


def after(value, *others):
    return lax.optimization_barrier((value, *others))[0]


def sum_over(value, axis):
    pieces = partners(value, axis)
    return sum(pieces[1:], pieces[0])


def local(
    inputs,
    starts,
    first_gain,
    query_weight,
    key_matrix,
    value_matrix,
    out_weight,
    second_gain,
    gate_weight,
    up_weight,
    down_weight,
    grad_out,
):
    n_seqs, toks, width = inputs.shape
    q_width = query_weight.shape[1]
    kv_width = key_matrix.shape[1]
    qkv_width = q_width + 2 * kv_width
    turned = (q_width + kv_width) // HEAD_SIZE
    own_rows = query_weight.shape[0]
    hidden = gate_weight.shape[1]
    n_ctx = lax.axis_size("ctx")
    n_tp = lax.axis_size("tp")
    ctx = lax.axis_index("ctx")
    tp = lax.axis_index("tp")
    both = ("shard", "ctx")
    seqs = range(n_seqs)
    block = toks // n_tp

    def gather(value):
        return lax.all_gather(value, both, axis=0, tiled=True)

    last = []

    def step(kernel, first, *rest, **kwargs):
        out = kernel(after(first, *last) if last else first, *rest, **kwargs)
        last[:] = [out[0] if isinstance(out, (list, tuple)) else out]
        return out

    gains_own = jnp.concatenate(
        [
            first_gain[:, None],
            second_gain[:, None],
            jnp.zeros((own_rows, LANES - 2), BF16),
        ],
        axis=1,
    )
    qkv_own = jnp.concatenate([query_weight, key_matrix, value_matrix], axis=1)
    attn_own = jnp.concatenate([qkv_own, gains_own], axis=1)
    query_pos = ctx * toks + jnp.arange(toks, dtype=jnp.int32)
    bases = jnp.stack([(ctx ^ j) * toks for j in range(n_ctx)]).astype(jnp.int32)
    limits = last_allowed(query_pos, starts).reshape(n_seqs, toks // TILE, 1, TILE)
    cosine, sine = rotation_tables(query_pos, turned, kv_width // HEAD_SIZE)
    attn_pieces = partners(attn_own, "ctx")
    out_pieces = partners(out_weight.T, "tp")
    attn_part = place(attn_pieces, "ctx", 0)
    attn_part, cosine, sine, *out_pieces = lax.optimization_barrier(
        (attn_part, cosine, sine, *out_pieces)
    )
    attn_full = place(partners(attn_part, "shard"), "shard", 0)
    gain_one = attn_full[:, qkv_width].astype(F32)[None, :]
    gain_two = attn_full[:, qkv_width + 1].astype(F32)[None, :]

    ffn_own = jnp.concatenate([gate_weight, up_weight, down_weight.T], axis=1)
    own_full = gather(jnp.concatenate([ffn_own, *out_pieces], axis=1))
    out_start = 3 * hidden
    ffn_far = [swap(after(ffn_own, *attn_pieces), "tp", j) for j in range(2, n_tp, 2)]

    rows_in = inputs.reshape(n_seqs * toks, width)
    grad_rows = grad_out.reshape(n_seqs * toks, width)
    normed_one, query_low, kv_own = step(
        project, rows_in, gain_one, attn_full, cosine, sine, q_width
    )
    query_low = query_low.reshape(n_seqs, toks, q_width)

    kv_pieces = partners(kv_own, "ctx")
    mixed, lse, mixed_all = [], [], []
    ffn_weights = [own_full]
    for s in seqs:
        mixed_s, lse_s = step(attend, query_low, kv_pieces, limits, bases, s)
        mixed.append(mixed_s)
        lse.append(lse_s)
        mixed_all.append(partners(mixed_s, "tp"))
        if s == 0:
            ffn_weights += [gather(after(far, mixed_s)) for far in ffn_far]

    middle, normed_two, out_terms, backs, kept = [], [], [], [], []
    for s in seqs:
        middle_s, normed_s = step(middle_of, rows_in, gain_two, own_full, out_start, mixed_all[s], s)
        terms = ()
        batches = [ffn_weights] if s else [ffn_weights[:1]] + [[w] for w in ffn_weights[1:]]
        for j, weights in enumerate(batches):
            terms = step(ffn_groups, normed_s, grad_rows, weights, hidden, s, terms, j == 0)
            if j == 0:
                kept.append(terms[2])
                terms = terms[:2]
        middle.append(middle_s)
        normed_two.append(normed_s)
        out_terms.append(terms[0])
        backs.append([terms[1]] + ([swap(terms[1], "tp", 1)] if n_tp > 1 else []))
    out_near = jnp.concatenate(out_terms, axis=0)

    grad_wide, grad_attn, grad_query, grad_kv, gain_two_parts = [], [], [], [], []
    grad_pieces, gain_one_parts = [], []
    q_cos, q_sin = cosine[:, :q_width], sine[:, :q_width]
    kv_cos, kv_sin = cosine[:, q_width:], sine[:, q_width:]

    def through_attention(s):
        wide_s, attn_s, grad_mixed, gain_s = step(
            grad_middle_of, middle[s], grad_rows, gain_two, own_full, out_start, backs[s], q_width, s
        )
        query_s, kv_terms = step(
            attend_back,
            query_low,
            kv_pieces,
            limits,
            lse[s],
            mixed[s],
            grad_mixed,
            q_cos,
            q_sin,
            bases,
            s,
        )
        grad_wide.append(wide_s)
        grad_attn.append(attn_s)
        gain_two_parts.append(gain_s)
        grad_query.append(query_s)
        return lax.all_to_all(kv_terms, "ctx", 0, 0, tiled=True)

    def to_owners(s, parts):
        kv_s, part_s = step(project_back, grad_query[s], parts, kv_cos, kv_sin, attn_full)
        grad_kv.append(kv_s)
        return lax.all_to_all(part_s, "tp", 0, 0, tiled=True)

    def through_norm(s, pieces):
        rows_s = lax.dynamic_slice_in_dim(rows_in, s * toks + tp * block, block, 0)
        wide_s = lax.dynamic_slice_in_dim(grad_wide[s], tp * block, block, 0)
        grad_s, gain_s = step(grad_inputs_of, rows_s, wide_s, gain_one, pieces)
        gain_one_parts.append(gain_s)
        grad_pieces.append(partners(grad_s, "tp"))

    ffn_grads, out_far, pieces = None, out_near, []
    for s in seqs:
        parts = through_attention(s)
        if s == 0:
            if n_tp > 1:
                out_far = swap(after(out_near, grad_query[0]), "tp", 1)
            rights = [after(kept[0], *last), *kept[1:]]
            ffn_grads = weight_grad(
                normed_two,
                [grad_rows[i * toks : (i + 1) * toks] for i in seqs],
                rights,
                2 * hidden,
                256,
            )
            last[:] = [ffn_grads]
            ffn_grads = lax.psum_scatter(ffn_grads, both, scatter_dimension=0, tiled=True)
        else:
            through_norm(s - 1, pieces)
            parts = after(parts, out_far)
        pieces = to_owners(s, parts)
    grad_attn[0] = after(grad_attn[0], ffn_grads, *last)
    attn_grads = weight_grad(
        [normed_one[s * toks : (s + 1) * toks] for s in seqs],
        grad_attn,
        [jnp.concatenate([grad_query[s], grad_kv[s], mixed[s]], axis=1) for s in seqs],
        qkv_width,
        384,
    )
    last[:] = [attn_grads]
    attn_grads = lax.psum_scatter(attn_grads, both, scatter_dimension=0, tiled=True).astype(F32)
    through_norm(n_seqs - 1, pieces)
    grads = [place(pieces, "tp", 0) for pieces in grad_pieces]
    gain_one_parts[0] = after(gain_one_parts[0], grad_pieces[-1][min(1, n_tp - 1)])

    total = jnp.concatenate(middle, axis=0) + out_near.astype(F32)
    if n_tp > 1:
        total = total + out_far.astype(F32)
    result = total.astype(BF16).reshape(n_seqs, toks, width)

    gain_grads = jnp.concatenate(
        [sum_over(sum(gain_one_parts), "tp"), sum(gain_two_parts)], axis=0
    )
    for axis in both:
        gain_grads = sum_over(gain_grads, axis)
    part = lax.axis_index("shard") * n_ctx + ctx
    gain_grads = lax.dynamic_slice_in_dim(gain_grads, part * own_rows, own_rows, 1)
    return (
        result,
        jnp.stack(grads),
        gain_grads[0],
        attn_grads[:, :q_width],
        attn_grads[:, q_width : q_width + kv_width],
        attn_grads[:, q_width + kv_width : qkv_width],
        attn_grads[:, qkv_width:].T,
        gain_grads[1],
        ffn_grads[:, :hidden].astype(F32),
        ffn_grads[:, hidden : 2 * hidden].astype(F32),
        ffn_grads[:, 2 * hidden :].T.astype(F32),
    )


def solution(mesh):
    both = ("shard", "ctx")
    rows = P("shard", "ctx", None)
    return jax.shard_map(
        local,
        mesh=mesh,
        in_specs=(
            rows,
            P("shard", None),
            P(both),
            P(both, "tp"),
            P(both, "tp"),
            P(both, "tp"),
            P("tp", both),
            P(both),
            P(both, "tp"),
            P(both, "tp"),
            P("tp", both),
            rows,
        ),
        out_specs=(
            rows,
            rows,
            P(both),
            P(both, "tp"),
            P(both, "tp"),
            P(both, "tp"),
            P("tp", both),
            P(both),
            P(both, "tp"),
            P(both, "tp"),
            P("tp", both),
        ),
        check_vma=False,
    )
```

time: 863 us -> 572 us (0.66)
  waiting for transfers between devices: 435 us -> 205 us
  matrix products: 48.6 us -> 0 us
  local copies, waits for them, and re-layouts: 83.9 us -> 45.6 us
  Pallas kernels: 180 us -> 217 us
  other arithmetic: 56.8 us -> 20 us
  starting transfers between devices: 33.7 us -> 59.2 us
    ppermute x32 -> x33, waiting for transfers between devices: 435 us -> 152 us  [swap(): return lax.ppermute(value, axis, [(i, i ^ step) for i in range(count)])]
    all_to_all x0 -> x4, waiting for transfers between devices: none -> 53.4 us  [the longest x2 29.7 us: through_attention(): return lax.all_to_all(kv_terms, 'ctx', 0, 0, tiled=True)]
    dot_general x9 -> x0, matrix products: 48.6 us -> none  [the longest x2 23.9 us: nt(): lax.dot_general(left, right, (((1,), (1,)), ((), ())), preferred_element_...]
    pallas_call x5 -> x13, Pallas kernels: 112 us -> 140 us  [the longest x3 62.3 us: ffn_groups(): pl.pallas_call(functools.partial(ffn_kernel, keep, bool(base), groups), g...]
    unnamed x96 -> x89, local copies, waits for them, and re-layouts: 40.8 us -> 14.6 us
    all_to_all x0 -> x4, starting transfers between devices: none -> 21.9 us  [the longest x2 11.9 us: through_attention(): return lax.all_to_all(kv_terms, 'ctx', 0, 0, tiled=True)]
    concatenate x6 -> x2, local copies, waits for them, and re-layouts: 15.9 us -> 0.13 us  [the longest x1 0.1 us: local(): out_near = jnp.concatenate(out_terms, axis=0)]
    add x5 -> x7, other arithmetic: 15.3 us -> 0.13 us  [the longest x3 0.11 us: sum_over(): return sum(pieces[1:], pieces[0])]
  transfers between devices with their start and end apart: 40 -> 41, of which waited for: 22 -> 20; matrix products, arithmetic and copies ran while one was open for 20% -> 8% of each run, Pallas kernels for 21% -> 29%
where the time goes in v2:
time: 572 us; the launch traced here: 562 us
  Pallas kernels  217 us (38%)
  waiting for transfers between devices  205 us (36%)
  starting transfers between devices  59.2 us (10%)
  local copies, waits for them, and re-layouts  45.6 us (8%)
  other arithmetic  20 us (3%)
  between operations  14.9 us (3%)
    ppermute x33, waiting for transfers between devices, swap(): return lax.ppermute(value, axis, [(i, i ^ step) for i in range(count)])  152 us
    pallas_call x3, Pallas kernels, ffn_groups(): pl.pallas_call(functools.partial(ffn_kernel, keep, bool(base), groups), g...  62.3 us
    pallas_call x2, Pallas kernels, attend_back(): pl.pallas_call(functools.partial(attend_back_kernel, n_groups, repeat, n_...  37.9 us
    ppermute x33, starting transfers between devices, swap(): return lax.ppermute(value, axis, [(i, i ^ step) for i in range(count)])  37 us
    pallas_call x2, Pallas kernels, weight_grad(): pl.pallas_call(functools.partial(weight_grad_kernel, n_seqs, tile, split)...  31.6 us
    all_to_all x2, waiting for transfers between devices, through_attention(): return lax.all_to_all(kv_terms, 'ctx', 0, 0, tiled=True)  29.7 us
    pallas_call x2, Pallas kernels, attend(): pl.pallas_call(functools.partial(attend_kernel, n_groups, repeat, n_block...  28.1 us
    all_to_all x2, waiting for transfers between devices, to_owners(): return lax.all_to_all(part_s, 'tp', 0, 0, tiled=True)  23.7 us
  transfers between devices with their start and end apart: 41, of which 20 were waited for; matrix products, arithmetic and copies ran while one was open for 8% of the time, Pallas kernels for 29%

profile of v2, /device:TPU:12, one launch (start us, length us, event | category | flops | bytes accessed | tf_op | source)
XLA Modules:
  0.0 561.6 jit_solution(10866425870717600541)
XLA Ops:
  8.8 1.9 concatenate.25
  10.7 1.5 collective-permute-start
  12.7 1.5 collective-permute-start.2
  14.6 2.6 collective-permute-start.4
  18.3 7.1 %fusion.3 = (f32[512,768]{1,0:T(8,128)}, f32[512,768]{1,0:T(8,128)}) fusion(f32[768]{0:T(1024)S(1)} %get-tuple-element.171, f32[768]{0:T(1024)S(1)} %get-tuple-element.170, f32[512]{0:T(512)S(1)} %get-tuple-element.173, pred[768]{0:T(1024)(128)(4,1)S(1)} %iota_compare_fusion), kind=kLoop, calls=%fused_computation.7 | loop fusion | flops 1179648 | bytes 3154688 | tf_op jit(solution)/shard_map/mul | solution.py:582
  31.5 3.2 collective-permute-done.5
  38.6 2.5 collective-permute-done.6
  42.8 10.2 %project.1 = (bf16[1024,1536]{1,0:T(8,128)(2,1)}, bf16[1024,384]{1,0:T(8,128)(2,1)}, bf16[1024,384]{1,0:T(8,128)(2,1)}) custom-call(bf16[1024,1536]{1,0:T(8,128)(2,1)} %bitcast.53, f32[1,1536]{1,0:T(1,128)} %reshape.160.gain_ref, bf16[1536,896]{1,0:T(8,128)(2,1)} %copy-done.6, f32[512,768]{1,0:T(8,128)} %get-tuple-element.80.cos_ref, ...), custom_call_target="tpu_custom_call" | custom-call | flops 7247757312 | bytes 25952256 | tf_op jit(solution)/shard_map/project/pallas_call | solution.py:75
  53.1 1.5 collective-permute-start.7
  55.1 1.5 collective-permute-start.9
  57.9 26.6 %collective-permute-done.7.refs_1_ = bf16[1024,384]{1,0:T(8,128)(2,1)S(1)} collective-permute-done((bf16[1024,384]{1,0:T(8,128)(2,1)}, bf16[1024,384]{1,0:T(8,128)(2,1)S(1)}, u32[]{:S(2)}, u32[]{:S(2)}) %collective-permute-start.7) | collective-permute-done | bytes 786464 | tf_op jit(solution)/shard_map/ppermute | solution.py:594
  84.5 27.4 %collective-permute-done.9.refs_3_ = bf16[1024,384]{1,0:T(8,128)(2,1)S(1)} collective-permute-done((bf16[1024,384]{1,0:T(8,128)(2,1)}, bf16[1024,384]{1,0:T(8,128)(2,1)S(1)}, u32[]{:S(2)}, u32[]{:S(2)}) %collective-permute-start.9) | collective-permute-done | bytes 786464 | tf_op jit(solution)/shard_map/ppermute | solution.py:594
  112.8 14.2 %attend.2 = (bf16[512,384]{1,0:T(8,128)(2,1)}, f32[4,2,256]{2,1,0:T(2,128)}) custom-call(s32[4]{0:T(128)} %pad_add_fusion.bases_ref, bf16[2,512,384]{2,1,0:T(8,128)(2,1)} %bitcast.63, s32[2,4,1,128]{3,2,1,0:T(1,128)} %broadcast_maximum_fusion.limit_ref, bf16[1024,384]{1,0:T(8,128)(2,1)} %get-tuple-element.85.refs_0_, bf16[1024,384]{1,0:T(8,128)(2,1)} %copy-done.32, ...), custom_call_target="tpu_custom_call" | custom-call | flops 12884901888 | bytes 7077888 | tf_op jit(solution)/shard_map/attend/pallas_call | solution.py:166
  127.3 1.9 slice_bitcast_fusion
  133.8 2.4 collective-permute-start.11
  136.7 13.9 %attend.3 = (bf16[512,384]{1,0:T(8,128)(2,1)}, f32[4,2,256]{2,1,0:T(2,128)}) custom-call(s32[4]{0:T(128)} %pad_add_fusion.bases_ref, bf16[2,512,384]{2,1,0:T(8,128)(2,1)} %bitcast.64, s32[2,4,1,128]{3,2,1,0:T(1,128)} %broadcast_maximum_fusion.limit_ref, bf16[1024,384]{1,0:T(8,128)(2,1)} %get-tuple-element.85.refs_0_, bf16[1024,384]{1,0:T(8,128)(2,1)} %copy-done.32, ...), custom_call_target="tpu_custom_call" | custom-call | flops 12884901888 | bytes 7077888 | tf_op jit(solution)/shard_map/attend/pallas_call | solution.py:166
  152.0 1.9 collective-permute-start.15
  154.5 8.1 %collective-permute-done.11.refs_2_ = bf16[512,384]{1,0:T(8,128)(2,1)S(1)} collective-permute-done((bf16[512,384]{1,0:T(8,128)(2,1)S(1)}, bf16[512,384]{1,0:T(8,128)(2,1)S(1)}, u32[]{:S(2)}, u32[]{:S(2)}) %collective-permute-start.11) | collective-permute-done | bytes 393248 | tf_op jit(solution)/shard_map/ppermute | solution.py:594
  162.6 26.3 %collective-permute-done.12.refs_3_ = bf16[512,384]{1,0:T(8,128)(2,1)S(1)} collective-permute-done((bf16[512,384]{1,0:T(8,128)(2,1)S(1)}, bf16[512,384]{1,0:T(8,128)(2,1)S(1)}, u32[]{:S(2)}, u32[]{:S(2)}) %collective-permute-start.12) | collective-permute-done | bytes 393248 | tf_op jit(solution)/shard_map/ppermute | solution.py:594
  189.7 7.6 %middle_of.2 = (f32[512,1536]{1,0:T(8,128)}, bf16[512,1536]{1,0:T(8,128)(2,1)}) custom-call(bf16[1024,1536]{1,0:T(8,128)(2,1)} %bitcast.54, f32[1,1536]{1,0:T(1,128)} %reshape.161.gain_ref, bf16[1536,4608]{1,0:T(8,128)(2,1)} %all-gather.3.cloned.1.call-done.weight_ref.refs_0_.refs_1_.refs_2_, bf16[512,384]{1,0:T(8,128)(2,1)} %get-tuple-element.86.refs_0_.mixed_ref, ...), custom_call_target="tpu_custom_call" | custom-call | flops 7247757312 | bytes 37748736 | tf_op jit(solution)/shard_map/middle_of/pallas_call | solution.py:357
  197.2 16.5 %ffn_groups.3 = (bf16[512,1536]{1,0:T(8,128)(2,1)}, bf16[512,1536]{1,0:T(8,128)(2,1)}, bf16[512,3072]{1,0:T(8,128)(2,1)}) custom-call(bf16[512,1536]{1,0:T(8,128)(2,1)} %get-tuple-element.98.normed_ref.refs_0_, bf16[1024,1536]{1,0:T(8,128)(2,1)} %bitcast.43, bf16[1536,4608]{1,0:T(8,128)(2,1)} %all-gather.3.cloned.1.call-done.weight_ref.refs_0_.refs_1_.refs_2_, ...), custom_call_target="tpu_custom_call" | custom-call | flops 28991029248 | bytes 47185920 | tf_op jit(solution)/shard_map/ffn_groups/pallas_call | solution.py:413
  213.7 16.9 %ffn_groups.4 = (bf16[512,1536]{1,0:T(8,128)(2,1)}, bf16[512,1536]{1,0:T(8,128)(2,1)}) custom-call(bf16[512,1536]{1,0:T(8,128)(2,1)} %get-tuple-element.98.normed_ref.refs_0_, bf16[1024,1536]{1,0:T(8,128)(2,1)} %bitcast.44, bf16[1536,3072]{1,0:T(8,128)(2,1)} %all-gather.5.cloned.1.call-done.refs_0_.refs_1_.refs_2_.refs_3_.refs_4_.refs_5_, ...), custom_call_target="tpu_custom_call" | custom-call | flops 28991029248 | bytes 47185920 | tf_op jit(solution)/shard_map/ffn_groups/pallas_call | solution.py:413
  232.2 7.5 %middle_of.3 = (f32[512,1536]{1,0:T(8,128)}, bf16[512,1536]{1,0:T(8,128)(2,1)}) custom-call(bf16[1024,1536]{1,0:T(8,128)(2,1)} %bitcast.55, f32[1,1536]{1,0:T(1,128)} %reshape.161.gain_ref, bf16[1536,4608]{1,0:T(8,128)(2,1)} %all-gather.3.cloned.1.call-done.weight_ref.refs_0_.refs_1_.refs_2_, bf16[512,384]{1,0:T(8,128)(2,1)} %get-tuple-element.88.refs_0_.mixed_ref, ...), custom_call_target="tpu_custom_call" | custom-call | flops 7247757312 | bytes 37748736 | tf_op jit(solution)/shard_map/middle_of/pallas_call | solution.py:357
  239.8 28.9 %ffn_groups.5 = (bf16[512,1536]{1,0:T(8,128)(2,1)}, bf16[512,1536]{1,0:T(8,128)(2,1)}, bf16[512,3072]{1,0:T(8,128)(2,1)}) custom-call(bf16[512,1536]{1,0:T(8,128)(2,1)} %get-tuple-element.106.normed_ref.refs_1_, bf16[1024,1536]{1,0:T(8,128)(2,1)} %bitcast.45, bf16[1536,4608]{1,0:T(8,128)(2,1)} %all-gather.3.cloned.1.call-done.weight_ref.refs_0_.refs_1_.refs_2_, ...), custom_call_target="tpu_custom_call" | custom-call | flops 57982058496 | bytes 75497472 | tf_op jit(solution)/shard_map/ffn_groups/pallas_call | solution.py:413
  269.9 7.0 %grad_middle_of.2 = (f32[512,1536]{1,0:T(8,128)}, bf16[512,1536]{1,0:T(8,128)(2,1)}, bf16[512,384]{1,0:T(8,128)(2,1)}, f32[1,1536]{1,0:T(1,128)}) custom-call(f32[512,1536]{1,0:T(8,128)} %get-tuple-element.108.middle_ref, bf16[1024,1536]{1,0:T(8,128)(2,1)} %bitcast.46, f32[1,1536]{1,0:T(1,128)} %reshape.161.gain_ref, ...), custom_call_target="tpu_custom_call" | custom-call | flops 1811939328 | bytes 37748736 | tf_op jit(solution)/shard_map/grad_middle_of/pallas_call | solution.py:468
  276.9 19.0 %attend_back.2 = (bf16[512,384]{1,0:T(8,128)(2,1)}, bf16[2048,384]{1,0:T(8,128)(2,1)}) custom-call(s32[4]{0:T(128)} %pad_add_fusion.bases_ref, bf16[2,512,384]{2,1,0:T(8,128)(2,1)} %bitcast.65, s32[2,4,1,128]{3,2,1,0:T(1,128)} %broadcast_maximum_fusion.limit_ref, f32[4,2,256]{2,1,0:T(2,128)} %get-tuple-element.112.lse_ref, ...), custom_call_target="tpu_custom_call" | custom-call | flops 32212254720 | bytes 14155776 | tf_op jit(solution)/shard_map/attend_back/pallas_call | solution.py:267
  296.0 19.8 %weight_grad.2 = bf16[1536,3072]{1,0:T(8,128)(2,1)} custom-call(bf16[512,1536]{1,0:T(8,128)(2,1)} %get-tuple-element.98.normed_ref.refs_0_, bf16[512,1536]{1,0:T(8,128)(2,1)} %get-tuple-element.106.normed_ref.refs_1_, bf16[512,1536]{1,0:T(8,128)(2,1)} %get-tuple-element.152.refs_2_, bf16[512,1536]{1,0:T(8,128)(2,1)} %get-tuple-element.151.refs_3_, ...), custom_call_target="tpu_custom_call" | custom-call | flops 28991029248 | bytes 66060288 | tf_op jit(solution)/shard_map/weight_grad/pallas_call | solution.py:526
  315.8 2.0 collective-permute-start.19
  317.9 6.0 %all-to-all-start = ((bf16[4,512,384]{2,1,0:T(8,128)(2,1)}), bf16[4,512,384]{2,1,0:T(8,128)(2,1)}, u32[]{:S(2)}, u32[]{:S(2)}) async-start(bf16[4,512,384]{2,1,0:T(8,128)(2,1)} %bitcast.12), calls=%async_computation | async-start | bytes 3145728 | tf_op jit(solution)/shard_map/all_to_all | solution.py:749
  323.9 2.1 constant_dynamic-update-slice_fusion.8
  326.8 8.9 %all-to-all-done.terms_ref = bf16[4,512,384]{2,1,0:T(8,128)(2,1)} async-done(((bf16[4,512,384]{2,1,0:T(8,128)(2,1)}), bf16[4,512,384]{2,1,0:T(8,128)(2,1)}, u32[]{:S(2)}, u32[]{:S(2)}) %all-to-all-start) | async-done | bytes 1572896 | tf_op jit(solution)/shard_map/all_to_all | solution.py:749
  335.7 5.3 project_back.2
  341.0 12.5 %collective-permute-done.19.refs_1_ = bf16[512,1536]{1,0:T(8,128)(2,1)} collective-permute-done((bf16[512,1536]{1,0:T(8,128)(2,1)}, bf16[512,1536]{1,0:T(8,128)(2,1)}, u32[]{:S(2)}, u32[]{:S(2)}) %collective-permute-start.19) | collective-permute-done | bytes 1572896 | tf_op jit(solution)/shard_map/ppermute | solution.py:594
  353.5 7.2 %grad_middle_of.3 = (f32[512,1536]{1,0:T(8,128)}, bf16[512,1536]{1,0:T(8,128)(2,1)}, bf16[512,384]{1,0:T(8,128)(2,1)}, f32[1,1536]{1,0:T(1,128)}) custom-call(f32[512,1536]{1,0:T(8,128)} %get-tuple-element.122.middle_ref, bf16[1024,1536]{1,0:T(8,128)(2,1)} %bitcast.47, f32[1,1536]{1,0:T(1,128)} %reshape.161.gain_ref, ...), custom_call_target="tpu_custom_call" | custom-call | flops 1811939328 | bytes 37748736 | tf_op jit(solution)/shard_map/grad_middle_of/pallas_call | solution.py:468
  360.8 18.9 %attend_back.3 = (bf16[512,384]{1,0:T(8,128)(2,1)}, bf16[2048,384]{1,0:T(8,128)(2,1)}) custom-call(s32[4]{0:T(128)} %pad_add_fusion.bases_ref, bf16[2,512,384]{2,1,0:T(8,128)(2,1)} %bitcast.66, s32[2,4,1,128]{3,2,1,0:T(1,128)} %broadcast_maximum_fusion.limit_ref, f32[4,2,256]{2,1,0:T(2,128)} %get-tuple-element.126.lse_ref, ...), custom_call_target="tpu_custom_call" | custom-call | flops 32212254720 | bytes 14155776 | tf_op jit(solution)/shard_map/attend_back/pallas_call | solution.py:267
  379.6 5.9 %all-to-all-start.2 = ((bf16[4,512,384]{2,1,0:T(8,128)(2,1)}), bf16[4,512,384]{2,1,0:T(8,128)(2,1)}, u32[]{:S(2)}, u32[]{:S(2)}) async-start(bf16[4,512,384]{2,1,0:T(8,128)(2,1)} %bitcast.50), calls=%async_computation.3 | async-start | bytes 3145728 | tf_op jit(solution)/shard_map/all_to_all | solution.py:749
  385.5 20.9 %all-to-all-done.2 = bf16[4,512,384]{2,1,0:T(8,128)(2,1)} async-done(((bf16[4,512,384]{2,1,0:T(8,128)(2,1)}), bf16[4,512,384]{2,1,0:T(8,128)(2,1)}, u32[]{:S(2)}, u32[]{:S(2)}) %all-to-all-start.2) | async-done | bytes 1572896 | tf_op jit(solution)/shard_map/all_to_all | solution.py:749
  406.4 5.4 all-to-all-start.1
  411.8 2.1 constant_dynamic-slice_fusion.7
  413.8 3.9 fusion.20
  417.7 2.2 constant_dynamic-slice_fusion.6.wide_ref
  419.9 2.2 constant_dynamic-slice_fusion.4.wide_ref
  423.3 4.1 fusion.1
  427.4 15.8 %all-to-all-done.1.terms_ref = bf16[4,128,1536]{2,1,0:T(8,128)(2,1)} async-done(((bf16[4,128,1536]{2,1,0:T(8,128)(2,1)}), bf16[4,128,1536]{2,1,0:T(8,128)(2,1)}, u32[]{:S(2)}, u32[]{:S(2)}) %all-to-all-start.1) | async-done | bytes 1572896 | tf_op jit(solution)/shard_map/all_to_all | solution.py:754
  443.2 3.2 grad_inputs_of.2
  446.7 3.2 collective-permute-start.22
  449.9 5.4 project_back.3
  455.3 4.6 all-to-all-start.3
  461.3 11.7 %weight_grad.3 = bf16[1536,1152]{1,0:T(8,128)(2,1)} custom-call(bf16[512,1536]{1,0:T(8,128)(2,1)} %get-tuple-element.154.refs_0_, bf16[512,1536]{1,0:T(8,128)(2,1)} %get-tuple-element.153.refs_1_, bf16[512,1536]{1,0:T(8,128)(2,1)} %get-tuple-element.137.refs_2_, bf16[512,1536]{1,0:T(8,128)(2,1)} %get-tuple-element.138.refs_3_, ...), custom_call_target="tpu_custom_call" | custom-call | flops 10871635968 | bytes 36569088 | tf_op jit(solution)/shard_map/weight_grad/pallas_call | solution.py:526
  475.1 17.7 %collective-permute-done.22 = bf16[128,1536]{1,0:T(8,128)(2,1)} collective-permute-done((bf16[128,1536]{1,0:T(8,128)(2,1)}, bf16[128,1536]{1,0:T(8,128)(2,1)}, u32[]{:S(2)}, u32[]{:S(2)}) %collective-permute-start.22) | collective-permute-done | bytes 393248 | tf_op jit(solution)/shard_map/ppermute | solution.py:594
  493.8 7.9 %all-to-all-done.3.terms_ref = bf16[4,128,1536]{2,1,0:T(8,128)(2,1)S(1)} async-done(((bf16[4,128,1536]{2,1,0:T(8,128)(2,1)}), bf16[4,128,1536]{2,1,0:T(8,128)(2,1)S(1)}, u32[]{:S(2)}, u32[]{:S(2)}) %all-to-all-start.3) | async-done | bytes 1572896 | tf_op jit(solution)/shard_map/all_to_all | solution.py:754
  502.8 3.3 grad_inputs_of.3
  506.1 3.8 collective-permute-start.23
  509.9 1.5 collective-permute-start.25
  511.4 1.5 convert_bitcast_fusion
  514.0 9.4 %collective-permute-done.23 = bf16[128,1536]{1,0:T(8,128)(2,1)S(1)} collective-permute-done((bf16[128,1536]{1,0:T(8,128)(2,1)}, bf16[128,1536]{1,0:T(8,128)(2,1)S(1)}, u32[]{:S(2)}, u32[]{:S(2)}) %collective-permute-start.23) | collective-permute-done | bytes 393248 | tf_op jit(solution)/shard_map/ppermute | solution.py:594
  523.4 2.4 collective-permute-start.26
  525.8 1.5 collective-permute-start.28
  527.4 7.2 %collective-permute-done.24 = bf16[128,1536]{1,0:T(8,128)(2,1)S(1)} collective-permute-done((bf16[128,1536]{1,0:T(8,128)(2,1)}, bf16[128,1536]{1,0:T(8,128)(2,1)S(1)}, u32[]{:S(2)}, u32[]{:S(2)}) %collective-permute-start.24) | collective-permute-done | bytes 393248 | tf_op jit(solution)/shard_map/ppermute | solution.py:594
  534.7 4.3 collective-permute-done.27
  539.0 1.9 collective-permute-done.28
  542.2 2.3 collective-permute-start.30
  546.1 1.9 pad_maximum_fusion
  548.2 2.3 collective-permute-done.32
  (190 shorter events, 45.0 us)
Async XLA Ops:
  7.2 11.1 %copy-start.13 = (bf16[192,1024]{1,0:T(8,128)(2,1)S(1)}, bf16[192,1024]{1,0:T(8,128)(2,1)}, u32[]{:S(2)}) copy-start(bf16[192,1024]{1,0:T(8,128)(2,1)} %param.21) | copy-start | bytes 1179652
  7.2 181.7 %all-gather.3.cloned.1.call-start = ((), (), s32[]{:S(2)}) async-start(), calls=%async_computation.6 | async-start | bytes 15925248 | tf_op jit(solution)/shard_map/all_gather | solution.py:651
  10.7 16.0 %collective-permute-start = (bf16[192,896]{1,0:T(8,128)(2,1)}, bf16[192,896]{1,0:T(8,128)(2,1)}, u32[]{:S(2)}, u32[]{:S(2)}) collective-permute-start(bf16[192,896]{1,0:T(8,128)(2,1)} %concatenate.25), channel_id=1, source_target_pairs={{0,4},{4,0},{8,12},{12,8},{1,5},{5,1},{9,13},{13,9},{2,6},{6,2},{1... | collective-permute-start | bytes 1032200 | tf_op jit(solution)/shard_map/ppermute | solution.py:594
  12.2 17.2 %collective-permute-start.1 = (bf16[192,896]{1,0:T(8,128)(2,1)}, bf16[192,896]{1,0:T(8,128)(2,1)}, u32[]{:S(2)}, u32[]{:S(2)}) collective-permute-start(bf16[192,896]{1,0:T(8,128)(2,1)} %concatenate.25), channel_id=1, source_target_pairs={{0,8},{4,12},{8,0},{12,4},{1,9},{5,13},{9,1},{13,5},{2,10},{6,14},... | collective-permute-start | bytes 1032200 | tf_op jit(solution)/shard_map/ppermute | solution.py:594
  12.7 17.7 %collective-permute-start.2 = (bf16[192,896]{1,0:T(8,128)(2,1)}, bf16[192,896]{1,0:T(8,128)(2,1)}, u32[]{:S(2)}, u32[]{:S(2)}) collective-permute-start(bf16[192,896]{1,0:T(8,128)(2,1)} %concatenate.25), channel_id=1, source_target_pairs={{0,12},{4,8},{8,4},{12,0},{1,13},{5,9},{9,5},{13,1},{2,14},{6,10},... | collective-permute-start | bytes 1032200 | tf_op jit(solution)/shard_map/ppermute | solution.py:594
  14.2 17.3 %collective-permute-start.3 = (bf16[192,384]{1,0:T(8,128)(2,1)}, bf16[192,384]{1,0:T(8,128)(2,1)}, u32[]{:S(2)}, u32[]{:S(2)}) collective-permute-start(bf16[192,384]{1,0:T(8,128)(2,1)} %bitcast.57), channel_id=1, source_target_pairs={{0,1},{1,0},{2,3},{3,2},{4,5},{5,4},{6,7},{7,6},{8,9},{9,8},{10,11... | collective-permute-start | bytes 442376 | tf_op jit(solution)/shard_map/ppermute | solution.py:594
  14.6 16.8 %collective-permute-start.4 = (bf16[192,384]{1,0:T(8,128)(2,1)}, bf16[192,384]{1,0:T(8,128)(2,1)}, u32[]{:S(2)}, u32[]{:S(2)}) collective-permute-start(bf16[192,384]{1,0:T(8,128)(2,1)} %bitcast.58), channel_id=1, source_target_pairs={{0,2},{1,3},{2,0},{3,1},{4,6},{5,7},{6,4},{7,5},{8,10},{9,11},{10,... | collective-permute-start | bytes 442376 | tf_op jit(solution)/shard_map/ppermute | solution.py:594
  18.3 7.1 %copy-start.14 = (bf16[1024,192]{0,1:T(8,128)(2,1)S(1)}, bf16[1024,192]{0,1:T(8,128)(2,1)}, u32[]{:S(2)}) copy-start(bf16[1024,192]{0,1:T(8,128)(2,1)} %param.22) | copy-start | bytes 1179652
  25.6 9.0 %copy-start.26 = (bf16[384,192]{0,1:T(8,128)(2,1)S(1)}, bf16[384,192]{0,1:T(8,128)(2,1)}, u32[]{:S(2)}) copy-start(bf16[384,192]{0,1:T(8,128)(2,1)} %param.18) | copy-start | bytes 442372
  26.7 8.0 %collective-permute-start.5 = (bf16[192,384]{1,0:T(8,128)(2,1)}, bf16[192,384]{1,0:T(8,128)(2,1)S(1)}, u32[]{:S(2)}, u32[]{:S(2)}) collective-permute-start(bf16[192,384]{1,0:T(8,128)(2,1)} %bitcast.59), channel_id=1, source_target_pairs={{0,3},{1,2},{2,1},{3,0},{4,7},{5,6},{6,5},{7,4},{8,11},{9,10},{10,... | collective-permute-start | bytes 442376 | tf_op jit(solution)/shard_map/ppermute | solution.py:594
  31.4 6.5 %copy-start.31 = (s32[2,2]{1,0:T(2,128)S(1)}, s32[2,2]{1,0:T(2,128)}, u32[]{:S(2)}) copy-start(s32[2,2]{1,0:T(2,128)} %param.13) | copy-start | bytes 52
  37.8 175.9 %all-gather.5.cloned.1.call-start = ((), (), s32[]{:S(2)}) async-start(), calls=%async_computation.7 | async-start | bytes 10616832 | tf_op jit(solution)/shard_map/all_gather | solution.py:651
  37.9 3.2 collective-permute-start.6
  42.8 14.9 %copy-start.12 = (bf16[192,1024]{1,0:T(8,128)(2,1)S(1)}, bf16[192,1024]{1,0:T(8,128)(2,1)}, u32[]{:S(2)}) copy-start(bf16[192,1024]{1,0:T(8,128)(2,1)} %param.20) | copy-start | bytes 1179652
  42.8 14.9 %copy-start.15 = (bf16[1024,192]{0,1:T(8,128)(2,1)S(1)}, bf16[1024,192]{0,1:T(8,128)(2,1)}, u32[]{:S(2)}) copy-start(bf16[1024,192]{0,1:T(8,128)(2,1)} %param.22) | copy-start | bytes 1179652
  53.1 31.4 %collective-permute-start.7 = (bf16[1024,384]{1,0:T(8,128)(2,1)}, bf16[1024,384]{1,0:T(8,128)(2,1)S(1)}, u32[]{:S(2)}, u32[]{:S(2)}) collective-permute-start(bf16[1024,384]{1,0:T(8,128)(2,1)} %get-tuple-element.85.refs_0_), channel_id=1, source_target_pairs={{0,4},{4,0},{8,12},{12,8},{1,5},{5,1},{9,13},{13,9},{2,6},{6,2},{1... | collective-permute-start | bytes 2359304 | tf_op jit(solution)/shard_map/ppermute | solution.py:594
  54.5 29.9 %collective-permute-start.8 = (bf16[1024,384]{1,0:T(8,128)(2,1)}, bf16[1024,384]{1,0:T(8,128)(2,1)S(1)}, u32[]{:S(2)}, u32[]{:S(2)}) collective-permute-start(bf16[1024,384]{1,0:T(8,128)(2,1)} %get-tuple-element.85.refs_0_), channel_id=1, source_target_pairs={{0,8},{4,12},{8,0},{12,4},{1,9},{5,13},{9,1},{13,5},{2,10},{6,14},... | collective-permute-start | bytes 2359304 | tf_op jit(solution)/shard_map/ppermute | solution.py:594
  55.1 56.8 %collective-permute-start.9 = (bf16[1024,384]{1,0:T(8,128)(2,1)}, bf16[1024,384]{1,0:T(8,128)(2,1)S(1)}, u32[]{:S(2)}, u32[]{:S(2)}) collective-permute-start(bf16[1024,384]{1,0:T(8,128)(2,1)} %get-tuple-element.85.refs_0_), channel_id=1, source_target_pairs={{0,12},{4,8},{8,4},{12,0},{1,13},{5,9},{9,5},{13,1},{2,14},{6,10},... | collective-permute-start | bytes 2359304 | tf_op jit(solution)/shard_map/ppermute | solution.py:594
  57.8 69.1 %collective-permute-start.13 = (bf16[192,3072]{1,0:T(8,128)(2,1)S(1)}, bf16[192,3072]{1,0:T(8,128)(2,1)}, u32[]{:S(2)}, u32[]{:S(2)}) collective-permute-start(bf16[192,3072]{1,0:T(8,128)(2,1)S(1)} %pad_maximum_fusion.1), channel_id=1, source_target_pairs={{0,2},{1,3},{2,0},{3,1},{4,6},{5,7},{6,4},{7,5},{8,10},{9,11},{10,... | collective-permute-start | bytes 3538952 | tf_op jit(solution)/shard_map/ppermute | solution.py:594
  84.5 27.4 %copy-start.32 = (bf16[1024,384]{1,0:T(8,128)(2,1)}, bf16[1024,384]{1,0:T(8,128)(2,1)S(1)}, u32[]{:S(2)}) copy-start(bf16[1024,384]{1,0:T(8,128)(2,1)S(1)} %collective-permute-done.7.refs_1_) | copy-start | bytes 2359300
  84.5 27.4 %copy-start.33 = (bf16[1024,384]{1,0:T(8,128)(2,1)}, bf16[1024,384]{1,0:T(8,128)(2,1)S(1)}, u32[]{:S(2)}) copy-start(bf16[1024,384]{1,0:T(8,128)(2,1)S(1)} %collective-permute-done.8.refs_2_) | copy-start | bytes 2359300
  112.8 14.5 %copy-start = (bf16[2,512,1536]{2,1,0:T(8,128)(2,1)S(1)}, bf16[2,512,1536]{2,1,0:T(8,128)(2,1)}, u32[]{:S(2)}) copy-start(bf16[2,512,1536]{2,1,0:T(8,128)(2,1)} %param.23) | copy-start | bytes 9437188
  127.0 334.3 %reduce-scatter.3.cloned.1.call-start = ((), (), s32[]{:S(2)}) async-start(), calls=%async_computation.8 | async-start | bytes 10616832 | tf_op jit(solution)/shard_map/reduce_scatter | solution.py:778
  133.2 20.7 %collective-permute-start.10 = (bf16[512,384]{1,0:T(8,128)(2,1)S(1)}, bf16[512,384]{1,0:T(8,128)(2,1)S(1)}, u32[]{:S(2)}, u32[]{:S(2)}) collective-permute-start(bf16[512,384]{1,0:T(8,128)(2,1)S(1)} %copy-done.18), channel_id=1, source_target_pairs={{0,1},{1,0},{2,3},{3,2},{4,5},{5,4},{6,7},{7,6},{8,9},{9,8},{10,11... | collective-permute-start | bytes 1179656 | tf_op jit(solution)/shard_map/ppermute | solution.py:594
  133.8 28.9 %collective-permute-start.11 = (bf16[512,384]{1,0:T(8,128)(2,1)S(1)}, bf16[512,384]{1,0:T(8,128)(2,1)S(1)}, u32[]{:S(2)}, u32[]{:S(2)}) collective-permute-start(bf16[512,384]{1,0:T(8,128)(2,1)S(1)} %copy-done.18), channel_id=1, source_target_pairs={{0,2},{1,3},{2,0},{3,1},{4,6},{5,7},{6,4},{7,5},{8,10},{9,11},{10,... | collective-permute-start | bytes 1179656 | tf_op jit(solution)/shard_map/ppermute | solution.py:594
  136.2 52.7 %collective-permute-start.12 = (bf16[512,384]{1,0:T(8,128)(2,1)S(1)}, bf16[512,384]{1,0:T(8,128)(2,1)S(1)}, u32[]{:S(2)}, u32[]{:S(2)}) collective-permute-start(bf16[512,384]{1,0:T(8,128)(2,1)S(1)} %copy-done.18), channel_id=1, source_target_pairs={{0,3},{1,2},{2,1},{3,0},{4,7},{5,6},{6,5},{7,4},{8,11},{9,10},{10,... | collective-permute-start | bytes 1179656 | tf_op jit(solution)/shard_map/ppermute | solution.py:594
  150.6 80.0 %collective-permute-start.14 = (bf16[512,384]{1,0:T(8,128)(2,1)}, bf16[512,384]{1,0:T(8,128)(2,1)S(1)}, u32[]{:S(2)}, u32[]{:S(2)}) collective-permute-start(bf16[512,384]{1,0:T(8,128)(2,1)} %get-tuple-element.88.refs_0_.mixed_ref), channel_id=1, source_target_pairs={{0,1},{1,0},{2,3},{3,2},{4,5},{5,4},{6,7},{7,6},{8,9},{9,8},{10,11... | collective-permute-start | bytes 1179656 | tf_op jit(solution)/shard_map/ppermute | solution.py:594
  152.0 78.6 %collective-permute-start.15 = (bf16[512,384]{1,0:T(8,128)(2,1)}, bf16[512,384]{1,0:T(8,128)(2,1)S(1)}, u32[]{:S(2)}, u32[]{:S(2)}) collective-permute-start(bf16[512,384]{1,0:T(8,128)(2,1)} %get-tuple-element.88.refs_0_.mixed_ref), channel_id=1, source_target_pairs={{0,2},{1,3},{2,0},{3,1},{4,6},{5,7},{6,4},{7,5},{8,10},{9,11},{10,... | collective-permute-start | bytes 1179656 | tf_op jit(solution)/shard_map/ppermute | solution.py:594
  154.0 34.9 %copy-start.38 = (bf16[512,384]{1,0:T(8,128)(2,1)}, bf16[512,384]{1,0:T(8,128)(2,1)S(1)}, u32[]{:S(2)}) copy-start(bf16[512,384]{1,0:T(8,128)(2,1)S(1)} %collective-permute-done.10.refs_1_) | copy-start | bytes 1179652
  154.0 76.7 %collective-permute-start.16 = (bf16[512,384]{1,0:T(8,128)(2,1)}, bf16[512,384]{1,0:T(8,128)(2,1)S(1)}, u32[]{:S(2)}, u32[]{:S(2)}) collective-permute-start(bf16[512,384]{1,0:T(8,128)(2,1)} %get-tuple-element.88.refs_0_.mixed_ref), channel_id=1, source_target_pairs={{0,3},{1,2},{2,1},{3,0},{4,7},{5,6},{6,5},{7,4},{8,11},{9,10},{10,... | collective-permute-start | bytes 1179656 | tf_op jit(solution)/shard_map/ppermute | solution.py:594
  162.6 26.3 %copy-start.39 = (bf16[512,384]{1,0:T(8,128)(2,1)}, bf16[512,384]{1,0:T(8,128)(2,1)S(1)}, u32[]{:S(2)}) copy-start(bf16[512,384]{1,0:T(8,128)(2,1)S(1)} %collective-permute-done.11.refs_2_) | copy-start | bytes 1179652
  230.6 9.2 %copy-start.9 = (bf16[512,1536]{1,0:T(8,128)(2,1)S(1)}, bf16[512,1536]{1,0:T(8,128)(2,1)}, u32[]{:S(2)}) copy-start(bf16[512,1536]{1,0:T(8,128)(2,1)} %get-tuple-element.109.refs_0_) | copy-start | bytes 4718596
  239.8 29.0 %collective-permute-start.17 = (bf16[512,1536]{1,0:T(8,128)(2,1)S(1)}, bf16[512,1536]{1,0:T(8,128)(2,1)S(1)}, u32[]{:S(2)}, u32[]{:S(2)}) collective-permute-start(bf16[512,1536]{1,0:T(8,128)(2,1)S(1)} %copy-done.9), channel_id=1, source_target_pairs={{0,1},{1,0},{2,3},{3,2},{4,5},{5,4},{6,7},{7,6},{8,9},{9,8},{10,11... | collective-permute-start | bytes 4718600 | tf_op jit(solution)/shard_map/ppermute | solution.py:594
  315.8 37.7 %collective-permute-start.19 = (bf16[512,1536]{1,0:T(8,128)(2,1)}, bf16[512,1536]{1,0:T(8,128)(2,1)}, u32[]{:S(2)}, u32[]{:S(2)}) collective-permute-start(bf16[512,1536]{1,0:T(8,128)(2,1)} %get-tuple-element.123.refs_0_), channel_id=1, source_target_pairs={{0,1},{1,0},{2,3},{3,2},{4,5},{5,4},{6,7},{7,6},{8,9},{9,8},{10,11... | collective-permute-start | bytes 4718600 | tf_op jit(solution)/shard_map/ppermute | solution.py:594
  317.9 17.8 %all-to-all-start = ((bf16[4,512,384]{2,1,0:T(8,128)(2,1)}), bf16[4,512,384]{2,1,0:T(8,128)(2,1)}, u32[]{:S(2)}, u32[]{:S(2)}) async-start(bf16[4,512,384]{2,1,0:T(8,128)(2,1)} %bitcast.12), calls=%async_computation | async-start | bytes 3145728 | tf_op jit(solution)/shard_map/all_to_all | solution.py:749
  326.7 96.6 %collective-permute-start.18 = (bf16[1024,1536]{1,0:T(8,128)(2,1)S(1)}, bf16[1024,1536]{1,0:T(8,128)(2,1)}, u32[]{:S(2)}, u32[]{:S(2)}) collective-permute-start(bf16[1024,1536]{1,0:T(8,128)(2,1)S(1)} %constant_dynamic-update-slice_fusion.7), channel_id=1, source_target_pairs={{0,1},{1,0},{2,3},{3,2},{4,5},{5,4},{6,7},{7,6},{8,9},{9,8},{10,11... | collective-permute-start | bytes 9437192 | tf_op jit(solution)/shard_map/ppermute | solution.py:594
  379.6 26.7 %all-to-all-start.2 = ((bf16[4,512,384]{2,1,0:T(8,128)(2,1)}), bf16[4,512,384]{2,1,0:T(8,128)(2,1)}, u32[]{:S(2)}, u32[]{:S(2)}) async-start(bf16[4,512,384]{2,1,0:T(8,128)(2,1)} %bitcast.50), calls=%async_computation.3 | async-start | bytes 3145728 | tf_op jit(solution)/shard_map/all_to_all | solution.py:749
  406.4 36.9 %all-to-all-start.1 = ((bf16[4,128,1536]{2,1,0:T(8,128)(2,1)}), bf16[4,128,1536]{2,1,0:T(8,128)(2,1)}, u32[]{:S(2)}, u32[]{:S(2)}) async-start(bf16[4,128,1536]{2,1,0:T(8,128)(2,1)} %bitcast.49), calls=%async_computation.1 | async-start | bytes 3145728 | tf_op jit(solution)/shard_map/all_to_all | solution.py:754
  413.8 9.5 %copy-start.2 = (f32[512,1536]{1,0:T(8,128)S(1)}, f32[512,1536]{1,0:T(8,128)}, u32[]{:S(2)}) copy-start(f32[512,1536]{1,0:T(8,128)} %get-tuple-element.122.middle_ref) | copy-start | bytes 9437188
  417.7 4.4 copy-start.19
  417.7 4.4 copy-start.20
  417.7 4.4 copy-start.22
  419.9 3.4 copy-start.1
  446.4 26.6 %collective-permute-start.20 = (bf16[128,1536]{1,0:T(8,128)(2,1)}, bf16[128,1536]{1,0:T(8,128)(2,1)}, u32[]{:S(2)}, u32[]{:S(2)}) collective-permute-start(bf16[128,1536]{1,0:T(8,128)(2,1)} %get-tuple-element.131), channel_id=1, source_target_pairs={{0,1},{1,0},{2,3},{3,2},{4,5},{5,4},{6,7},{7,6},{8,9},{9,8},{10,11... | collective-permute-start | bytes 1179656 | tf_op jit(solution)/shard_map/ppermute | solution.py:594
  446.4 27.7 %collective-permute-start.21 = (bf16[128,1536]{1,0:T(8,128)(2,1)}, bf16[128,1536]{1,0:T(8,128)(2,1)}, u32[]{:S(2)}, u32[]{:S(2)}) collective-permute-start(bf16[128,1536]{1,0:T(8,128)(2,1)} %get-tuple-element.131), channel_id=1, source_target_pairs={{0,2},{1,3},{2,0},{3,1},{4,6},{5,7},{6,4},{7,5},{8,10},{9,11},{10,... | collective-permute-start | bytes 1179656 | tf_op jit(solution)/shard_map/ppermute | solution.py:594
  446.7 46.1 %collective-permute-start.22 = (bf16[128,1536]{1,0:T(8,128)(2,1)}, bf16[128,1536]{1,0:T(8,128)(2,1)}, u32[]{:S(2)}, u32[]{:S(2)}) collective-permute-start(bf16[128,1536]{1,0:T(8,128)(2,1)} %get-tuple-element.131), channel_id=1, source_target_pairs={{0,3},{1,2},{2,1},{3,0},{4,7},{5,6},{6,5},{7,4},{8,11},{9,10},{10,... | collective-permute-start | bytes 1179656 | tf_op jit(solution)/shard_map/ppermute | solution.py:594
  455.3 4.6 copy-start.17
  455.3 4.6 copy-start.21
  455.3 4.6 copy-start.23
  455.3 46.4 %all-to-all-start.3 = ((bf16[4,128,1536]{2,1,0:T(8,128)(2,1)}), bf16[4,128,1536]{2,1,0:T(8,128)(2,1)S(1)}, u32[]{:S(2)}, u32[]{:S(2)}) async-start(bf16[4,128,1536]{2,1,0:T(8,128)(2,1)} %bitcast.51), calls=%async_computation.4 | async-start | bytes 3145728 | tf_op jit(solution)/shard_map/all_to_all | solution.py:754
  459.8 91.4 %reduce-scatter.5.cloned.1.call-start = ((), (), s32[]{:S(2)}) async-start(), calls=%async_computation.9 | async-start | bytes 3981312 | tf_op jit(solution)/shard_map/reduce_scatter | solution.py:792
  502.8 8.6 %copy-start.16 = (bf16[192,3072]{1,0:T(8,128)(2,1)S(1)}, bf16[192,3072]{1,0:T(8,128)(2,1)}, u32[]{:S(2)}) copy-start(bf16[192,3072]{1,0:T(8,128)(2,1)} %reduce-scatter.3.cloned.1.call-done) | copy-start | bytes 3538948
  506.1 17.2 %collective-permute-start.23 = (bf16[128,1536]{1,0:T(8,128)(2,1)}, bf16[128,1536]{1,0:T(8,128)(2,1)S(1)}, u32[]{:S(2)}, u32[]{:S(2)}) collective-permute-start(bf16[128,1536]{1,0:T(8,128)(2,1)} %get-tuple-element.141), channel_id=1, source_target_pairs={{0,1},{1,0},{2,3},{3,2},{4,5},{5,4},{6,7},{7,6},{8,9},{9,8},{10,11... | collective-permute-start | bytes 1179656 | tf_op jit(solution)/shard_map/ppermute | solution.py:594
  509.9 24.7 %collective-permute-start.24 = (bf16[128,1536]{1,0:T(8,128)(2,1)}, bf16[128,1536]{1,0:T(8,128)(2,1)S(1)}, u32[]{:S(2)}, u32[]{:S(2)}) collective-permute-start(bf16[128,1536]{1,0:T(8,128)(2,1)} %get-tuple-element.141), channel_id=1, source_target_pairs={{0,2},{1,3},{2,0},{3,1},{4,6},{5,7},{6,4},{7,5},{8,10},{9,11},{10,... | collective-permute-start | bytes 1179656 | tf_op jit(solution)/shard_map/ppermute | solution.py:594
  509.9 31.1 %collective-permute-start.25 = (bf16[128,1536]{1,0:T(8,128)(2,1)}, bf16[128,1536]{1,0:T(8,128)(2,1)S(1)}, u32[]{:S(2)}, u32[]{:S(2)}) collective-permute-start(bf16[128,1536]{1,0:T(8,128)(2,1)} %get-tuple-element.141), channel_id=1, source_target_pairs={{0,3},{1,2},{2,1},{3,0},{4,7},{5,6},{6,5},{7,4},{8,11},{9,10},{10,... | collective-permute-start | bytes 1179656 | tf_op jit(solution)/shard_map/ppermute | solution.py:594
  512.9 10.5 %copy-start.29 = (f32[1,1536]{1,0:T(1,128)S(1)}, f32[1,1536]{1,0:T(1,128)}, u32[]{:S(2)}) copy-start(f32[1,1536]{1,0:T(1,128)} %get-tuple-element.143) | copy-start | bytes 18436
  512.9 10.5 %copy-start.30 = (f32[1,1536]{1,0:T(1,128)S(1)}, f32[1,1536]{1,0:T(1,128)}, u32[]{:S(2)}) copy-start(f32[1,1536]{1,0:T(1,128)} %get-tuple-element.144) | copy-start | bytes 18436
  523.4 11.3 %collective-permute-start.26 = (f32[1,1536]{1,0:T(1,128)S(1)}, f32[1,1536]{1,0:T(1,128)S(1)}, u32[]{:S(2)}, u32[]{:S(2)}) collective-permute-start(f32[1,1536]{1,0:T(1,128)S(1)} %add.159), channel_id=1, source_target_pairs={{0,1},{1,0},{2,3},{3,2},{4,5},{5,4},{6,7},{7,6},{8,9},{9,8},{10,11... | collective-permute-start | bytes 18440 | tf_op jit(solution)/shard_map/ppermute | solution.py:594
  525.8 13.1 %collective-permute-start.27 = (f32[1,1536]{1,0:T(1,128)S(1)}, f32[1,1536]{1,0:T(1,128)S(1)}, u32[]{:S(2)}, u32[]{:S(2)}) collective-permute-start(f32[1,1536]{1,0:T(1,128)S(1)} %add.159), channel_id=1, source_target_pairs={{0,2},{1,3},{2,0},{3,1},{4,6},{5,7},{6,4},{7,5},{8,10},{9,11},{10,... | collective-permute-start | bytes 18440 | tf_op jit(solution)/shard_map/ppermute | solution.py:594
  525.8 15.1 %collective-permute-start.28 = (f32[1,1536]{1,0:T(1,128)S(1)}, f32[1,1536]{1,0:T(1,128)S(1)}, u32[]{:S(2)}, u32[]{:S(2)}) collective-permute-start(f32[1,1536]{1,0:T(1,128)S(1)} %add.159), channel_id=1, source_target_pairs={{0,3},{1,2},{2,1},{3,0},{4,7},{5,6},{6,5},{7,4},{8,11},{9,10},{10,... | collective-permute-start | bytes 18440 | tf_op jit(solution)/shard_map/ppermute | solution.py:594
  540.9 1.2 collective-permute-start.29
  542.2 5.8 %collective-permute-start.30 = (f32[2,1536]{1,0:T(2,128)S(1)}, f32[2,1536]{1,0:T(2,128)S(1)}, u32[]{:S(2)}, u32[]{:S(2)}) collective-permute-start(f32[2,1536]{1,0:T(2,128)S(1)} %fusion.19), channel_id=1, source_target_pairs={{0,4},{4,0},{8,12},{12,8},{1,5},{5,1},{9,13},{13,9},{2,6},{6,2},{1... | collective-permute-start | bytes 36872 | tf_op jit(solution)/shard_map/ppermute | solution.py:594
  544.5 3.7 collective-permute-start.31
  546.0 4.6 collective-permute-start.32
  (18 other events, 26.4 us)
Sparse Core Ops, SparseCore 0:
  37.9 103.3 all-gather.2
  143.3 59.1 all-gather.4
  315.9 90.8 reduce-scatter.2
  473.1 48.0 reduce-scatter.4

commit v3 on v2

--- a/solution.py
+++ b/solution.py
@@ -18,7 +18,8 @@
 BF16 = jnp.bfloat16
 LANES = 128
 VMEM_LIMIT = 56 << 20
-COST_SCALE = 3
+TAIL = 30.0
+COST_SCALE = 10
 
 
 def nt(left, right):
@@ -33,12 +34,16 @@
     return pltpu.CompilerParams(vmem_limit_bytes=VMEM_LIMIT)
 
 
-def cost(flops, bytes_accessed, transcendentals=0):
+def cost(flops, bytes_accessed, transcendentals=0, weight=1.0):
     return pl.CostEstimate(
-        flops=int(flops * COST_SCALE),
-        bytes_accessed=int(bytes_accessed * COST_SCALE),
-        transcendentals=int(transcendentals * COST_SCALE),
-    )
+        flops=int(flops * COST_SCALE * weight),
+        bytes_accessed=int(bytes_accessed * COST_SCALE * weight),
+        transcendentals=int(transcendentals * COST_SCALE * weight),
+    )
+
+
+def tail_cost(*args, **kwargs):
+    return cost(*args, **kwargs, weight=TAIL)
 
 
 def columns(array, start, size):
@@ -293,7 +298,7 @@
             jax.ShapeDtypeStruct((length, kv_cols), BF16),
         ],
         compiler_params=params(),
-        cost_estimate=cost(
+        cost_estimate=tail_cost(
             10 * toks * length * 256 * n_groups * repeat,
             8 * toks * q_width + 4 * length * kv_cols,
             toks * length * n_groups * repeat,
@@ -334,7 +339,9 @@
             jax.ShapeDtypeStruct((toks, width), BF16),
         ],
         compiler_params=params(),
-        cost_estimate=cost(2 * toks * width * columns, 2 * width * (toks + columns)),
+        cost_estimate=tail_cost(
+            2 * toks * width * columns, 2 * width * (toks + columns)
+        ),
         name="project_back",
     )(query, cosine, sine, weights, terms.reshape(count, toks, kv_cols))
 
@@ -483,7 +490,7 @@
             jax.ShapeDtypeStruct((1, width), F32),
         ],
         compiler_params=params(),
-        cost_estimate=cost(2 * toks * width * q_width, 16 * toks * width),
+        cost_estimate=tail_cost(2 * toks * width * q_width, 16 * toks * width),
         name="grad_middle_of",
     )(middle, grad, gain, weights, *backs)
 
@@ -532,7 +539,7 @@
         out_shape=jax.ShapeDtypeStruct((width, columns), BF16),
         scratch_shapes=[pltpu.VMEM((width, n_seqs * toks), BF16)] * 2,
         compiler_params=params(),
-        cost_estimate=cost(
+        cost_estimate=tail_cost(
             2 * n_seqs * toks * width * columns,
             2 * n_seqs * toks * (2 * width + columns) + 2 * width * columns,
         ),
@@ -540,11 +547,14 @@
     )(*lefts, *others, *rights)
 
 
-def grad_inputs_kernel(rows_ref, wide_ref, gain_ref, terms_ref, out_ref, gain_grad_ref):
+def grad_inputs_kernel(rows_ref, wide_ref, gain_ref, *refs):
+    *term_refs, out_ref, gain_grad_ref = refs
     rows = rows_ref[...].astype(F32)
     inverse = lax.rsqrt(jnp.mean(rows * rows, axis=-1, keepdims=True) + EPSILON)
     hat = rows * inverse
-    back = jnp.sum(terms_ref[...].astype(F32), axis=0)
+    back = term_refs[0][...].astype(F32)
+    for ref in term_refs[1:]:
+        back = back + ref[...].astype(F32)
     scaled = back * gain_ref[...]
     total = wide_ref[...] + inverse * (
         scaled - hat * jnp.mean(scaled * hat, axis=-1, keepdims=True)
@@ -562,9 +572,9 @@
             jax.ShapeDtypeStruct((1, width), F32),
         ],
         compiler_params=params(),
-        cost_estimate=cost(0, 16 * toks * width),
+        cost_estimate=tail_cost(0, 16 * toks * width),
         name="grad_inputs_of",
-    )(inputs, wide, gain, terms.reshape(-1, toks, width))
+    )(inputs, wide, gain, *terms)
 
 
 TILE = 128
@@ -607,6 +617,14 @@
     for j, piece in enumerate(pieces):
         whole = lax.dynamic_update_slice_in_dim(whole, piece, (me ^ j) * width, dim)
     return whole
+
+
+def exchange(value, axis):
+    me = lax.axis_index(axis)
+    count = lax.axis_size(axis)
+    size = value.shape[0] // count
+    blocks = [lax.dynamic_slice_in_dim(value, (me ^ j) * size, size, 0) for j in range(count)]
+    return [blocks[0]] + [swap(blocks[j], axis, j) for j in range(1, count)]
 
 
 def after(value, *others):
@@ -725,10 +743,16 @@
     q_cos, q_sin = cosine[:, :q_width], sine[:, :q_width]
     kv_cos, kv_sin = cosine[:, q_width:], sine[:, q_width:]
 
-    def through_attention(s):
+    def through_middle(s):
         wide_s, attn_s, grad_mixed, gain_s = step(
             grad_middle_of, middle[s], grad_rows, gain_two, own_full, out_start, backs[s], q_width, s
         )
+        grad_wide.append(wide_s)
+        grad_attn.append(attn_s)
+        gain_two_parts.append(gain_s)
+        return grad_mixed
+
+    def through_attention(s, grad_mixed):
         query_s, kv_terms = step(
             attend_back,
             query_low,
@@ -742,16 +766,13 @@
             bases,
             s,
         )
-        grad_wide.append(wide_s)
-        grad_attn.append(attn_s)
-        gain_two_parts.append(gain_s)
         grad_query.append(query_s)
         return lax.all_to_all(kv_terms, "ctx", 0, 0, tiled=True)
 
     def to_owners(s, parts):
         kv_s, part_s = step(project_back, grad_query[s], parts, kv_cos, kv_sin, attn_full)
         grad_kv.append(kv_s)
-        return lax.all_to_all(part_s, "tp", 0, 0, tiled=True)
+        return exchange(part_s, "tp")
 
     def through_norm(s, pieces):
         rows_s = lax.dynamic_slice_in_dim(rows_in, s * toks + tp * block, block, 0)
@@ -760,27 +781,29 @@
         gain_one_parts.append(gain_s)
         grad_pieces.append(partners(grad_s, "tp"))
 
-    ffn_grads, out_far, pieces = None, out_near, []
+    out_far, terms, pieces = out_near, None, None
     for s in seqs:
-        parts = through_attention(s)
-        if s == 0:
-            if n_tp > 1:
-                out_far = swap(after(out_near, grad_query[0]), "tp", 1)
-            rights = [after(kept[0], *last), *kept[1:]]
-            ffn_grads = weight_grad(
-                normed_two,
-                [grad_rows[i * toks : (i + 1) * toks] for i in seqs],
-                rights,
-                2 * hidden,
-                256,
-            )
-            last[:] = [ffn_grads]
-            ffn_grads = lax.psum_scatter(ffn_grads, both, scatter_dimension=0, tiled=True)
-        else:
+        grad_mixed = through_middle(s)
+        if s > 0:
+            pieces = to_owners(s - 1, terms)
+        terms = through_attention(s, grad_mixed)
+        if s == 0 and n_tp > 1:
+            out_far = swap(after(out_near, grad_query[0]), "tp", 1)
+        if 0 < s < n_seqs - 1:
             through_norm(s - 1, pieces)
-            parts = after(parts, out_far)
-        pieces = to_owners(s, parts)
-    grad_attn[0] = after(grad_attn[0], ffn_grads, *last)
+    ffn_grads = weight_grad(
+        normed_two,
+        [grad_rows[i * toks : (i + 1) * toks] for i in seqs],
+        [after(kept[0], *last), *kept[1:]],
+        2 * hidden,
+        256,
+    )
+    last[:] = [ffn_grads]
+    ffn_grads = lax.psum_scatter(ffn_grads, both, scatter_dimension=0, tiled=True)
+    held, pieces = pieces, to_owners(n_seqs - 1, terms)
+    if n_seqs > 1:
+        through_norm(n_seqs - 2, held)
+    grad_attn[0] = after(grad_attn[0], out_far, *last)
     attn_grads = weight_grad(
         [normed_one[s * toks : (s + 1) * toks] for s in seqs],
         grad_attn,
@@ -789,7 +812,9 @@
         384,
     )
     last[:] = [attn_grads]
-    attn_grads = lax.psum_scatter(attn_grads, both, scatter_dimension=0, tiled=True).astype(F32)
+    attn_grads = lax.psum_scatter(
+        after(attn_grads, ffn_grads), both, scatter_dimension=0, tiled=True
+    ).astype(F32)
     through_norm(n_seqs - 1, pieces)
     grads = [place(pieces, "tp", 0) for pieces in grad_pieces]
     gain_one_parts[0] = after(gain_one_parts[0], grad_pieces[-1][min(1, n_tp - 1)])

time: 572 us -> 530 us (0.927)
  waiting for transfers between devices: 205 us -> 163 us
    all_to_all x2, waiting for transfers between devices: 29.7 us -> 0.01 us  [through_attention(): return lax.all_to_all(kv_terms, 'ctx', 0, 0, tiled=True)]
    all_to_all x2 -> x0, waiting for transfers between devices: 23.7 us -> none  [to_owners(): return lax.all_to_all(part_s, 'tp', 0, 0, tiled=True)]
    all_to_all x2 -> x0, starting transfers between devices: 9.97 us -> none  [to_owners(): return lax.all_to_all(part_s, 'tp', 0, 0, tiled=True)]
    ppermute x33 -> x39, starting transfers between devices: 37 us -> 44.2 us  [swap(): return lax.ppermute(value, axis, [(i, i ^ step) for i in range(count)])]
    ppermute x33 -> x39, waiting for transfers between devices: 152 us -> 157 us  [swap(): return lax.ppermute(value, axis, [(i, i ^ step) for i in range(count)])]
    unnamed x89 -> x91, local copies, waits for them, and re-layouts: 14.6 us -> 11.8 us
  transfers between devices with their start and end apart: 41 -> 45, of which waited for: 20 -> 19; matrix products, arithmetic and copies ran while one was open for 8% -> 11% of each run, Pallas kernels for 29% -> 40%
where the time goes in v3:
time: 530 us; the launch traced here: 522 us
  Pallas kernels  218 us (41%)
  waiting for transfers between devices  163 us (31%)
  starting transfers between devices  54.8 us (10%)
  local copies, waits for them, and re-layouts  47.1 us (9%)
  other arithmetic  24.9 us (5%)
  between operations  14.6 us (3%)
    ppermute x39, waiting for transfers between devices, swap(): return lax.ppermute(value, axis, [(i, i ^ step) for i in range(count)])  157 us
    pallas_call x3, Pallas kernels, ffn_groups(): pl.pallas_call(functools.partial(ffn_kernel, keep, bool(base), groups), g...  62.4 us
    ppermute x39, starting transfers between devices, swap(): return lax.ppermute(value, axis, [(i, i ^ step) for i in range(count)])  44.2 us
    pallas_call x2, Pallas kernels, attend_back(): pl.pallas_call(functools.partial(attend_back_kernel, n_groups, repeat, n_...  37.7 us
    pallas_call x2, Pallas kernels, weight_grad(): pl.pallas_call(functools.partial(weight_grad_kernel, n_seqs, tile, split)...  32.3 us
    pallas_call x2, Pallas kernels, attend(): pl.pallas_call(functools.partial(attend_kernel, n_groups, repeat, n_block...  27.9 us
    pallas_call x2, Pallas kernels, middle_of(): pl.pallas_call(functools.partial(middle_kernel, len(pieces)), grid=(steps...  15.1 us
    pallas_call x2, Pallas kernels, grad_middle_of(): pl.pallas_call(functools.partial(grad_middle_kernel, len(backs)), grid=(s...  14 us
  transfers between devices with their start and end apart: 45, of which 19 were waited for; matrix products, arithmetic and copies ran while one was open for 11% of the time, Pallas kernels for 40%

profile of v3, /device:TPU:12, one launch (start us, length us, event | category | flops | bytes accessed | tf_op | source)
XLA Modules:
  0.0 521.6 jit_solution(4104667094907070659)
XLA Ops:
  10.0 1.6 collective-permute-start
  12.0 1.5 collective-permute-start.2
  14.0 2.6 collective-permute-start.4
  17.7 7.1 %fusion.3 = (f32[512,768]{1,0:T(8,128)}, f32[512,768]{1,0:T(8,128)}) fusion(f32[768]{0:T(1024)S(1)} %get-tuple-element.179, f32[768]{0:T(1024)S(1)} %get-tuple-element.178, f32[512]{0:T(512)S(1)} %get-tuple-element.181, pred[768]{0:T(1024)(128)(4,1)S(1)} %iota_compare_fusion), kind=kLoop, calls=%fused_computation.7 | loop fusion | flops 1179648 | bytes 3154688 | tf_op jit(solution)/shard_map/mul | solution.py:592
  26.6 2.0 collective-permute-done.1
  30.6 2.4 collective-permute-done.5
  37.1 2.1 constant_dynamic-slice_fusion.15
  40.8 1.6 constant_dynamic-update-slice_fusion.9.weight_ref
  44.0 10.2 %project.1 = (bf16[1024,1536]{1,0:T(8,128)(2,1)}, bf16[1024,384]{1,0:T(8,128)(2,1)}, bf16[1024,384]{1,0:T(8,128)(2,1)}) custom-call(bf16[1024,1536]{1,0:T(8,128)(2,1)} %bitcast.49, f32[1,1536]{1,0:T(1,128)} %reshape.150.gain_ref, bf16[1536,896]{1,0:T(8,128)(2,1)} %copy-done.2, f32[512,768]{1,0:T(8,128)} %get-tuple-element.80.cos_ref, ...), custom_call_target="tpu_custom_call" | custom-call | flops 24159191040 | bytes 86507520 | tf_op jit(solution)/shard_map/project/pallas_call | solution.py:80
  54.2 1.5 collective-permute-start.7
  56.2 1.5 collective-permute-start.9
  58.3 1.9 slice_bitcast_fusion
  60.5 22.2 %collective-permute-done.7.refs_1_ = bf16[1024,384]{1,0:T(8,128)(2,1)S(1)} collective-permute-done((bf16[1024,384]{1,0:T(8,128)(2,1)}, bf16[1024,384]{1,0:T(8,128)(2,1)S(1)}, u32[]{:S(2)}, u32[]{:S(2)}) %collective-permute-start.7) | collective-permute-done | bytes 786464 | tf_op jit(solution)/shard_map/ppermute | solution.py:604
  82.7 31.7 %collective-permute-done.9.refs_3_ = bf16[1024,384]{1,0:T(8,128)(2,1)S(1)} collective-permute-done((bf16[1024,384]{1,0:T(8,128)(2,1)}, bf16[1024,384]{1,0:T(8,128)(2,1)S(1)}, u32[]{:S(2)}, u32[]{:S(2)}) %collective-permute-start.9) | collective-permute-done | bytes 786464 | tf_op jit(solution)/shard_map/ppermute | solution.py:604
  115.3 14.0 %attend.2 = (bf16[512,384]{1,0:T(8,128)(2,1)}, f32[4,2,256]{2,1,0:T(2,128)}) custom-call(s32[4]{0:T(128)} %pad_add_fusion.bases_ref, bf16[2,512,384]{2,1,0:T(8,128)(2,1)} %bitcast.58, s32[2,4,1,128]{3,2,1,0:T(1,128)} %broadcast_maximum_fusion.limit_ref, bf16[1024,384]{1,0:T(8,128)(2,1)} %get-tuple-element.85.refs_0_, bf16[1024,384]{1,0:T(8,128)(2,1)} %copy-done.36, ...), custom_call_target="tpu_custom_call" | custom-call | flops 42949672960 | bytes 23592960 | tf_op jit(solution)/shard_map/attend/pallas_call | solution.py:171
  134.9 1.8 fusion.20
  137.3 2.4 collective-permute-start.11
  140.2 13.9 %attend.3 = (bf16[512,384]{1,0:T(8,128)(2,1)}, f32[4,2,256]{2,1,0:T(2,128)}) custom-call(s32[4]{0:T(128)} %pad_add_fusion.bases_ref, bf16[2,512,384]{2,1,0:T(8,128)(2,1)} %bitcast.59, s32[2,4,1,128]{3,2,1,0:T(1,128)} %broadcast_maximum_fusion.limit_ref, bf16[1024,384]{1,0:T(8,128)(2,1)} %get-tuple-element.85.refs_0_, bf16[1024,384]{1,0:T(8,128)(2,1)} %copy-done.36, ...), custom_call_target="tpu_custom_call" | custom-call | flops 42949672960 | bytes 23592960 | tf_op jit(solution)/shard_map/attend/pallas_call | solution.py:171
  155.5 1.9 collective-permute-start.15
  158.0 8.1 %collective-permute-done.11.refs_2_ = bf16[512,384]{1,0:T(8,128)(2,1)S(1)} collective-permute-done((bf16[512,384]{1,0:T(8,128)(2,1)S(1)}, bf16[512,384]{1,0:T(8,128)(2,1)S(1)}, u32[]{:S(2)}, u32[]{:S(2)}) %collective-permute-start.11) | collective-permute-done | bytes 393248 | tf_op jit(solution)/shard_map/ppermute | solution.py:604
  166.1 26.3 %collective-permute-done.12.refs_3_ = bf16[512,384]{1,0:T(8,128)(2,1)S(1)} collective-permute-done((bf16[512,384]{1,0:T(8,128)(2,1)S(1)}, bf16[512,384]{1,0:T(8,128)(2,1)S(1)}, u32[]{:S(2)}, u32[]{:S(2)}) %collective-permute-start.12) | collective-permute-done | bytes 393248 | tf_op jit(solution)/shard_map/ppermute | solution.py:604
  193.2 7.6 %middle_of.2 = (f32[512,1536]{1,0:T(8,128)}, bf16[512,1536]{1,0:T(8,128)(2,1)}) custom-call(bf16[1024,1536]{1,0:T(8,128)(2,1)} %bitcast.50, f32[1,1536]{1,0:T(1,128)} %reshape.151.gain_ref, bf16[1536,4608]{1,0:T(8,128)(2,1)} %all-gather.3.cloned.1.call-done.weight_ref.refs_0_.refs_1_.refs_2_, bf16[512,384]{1,0:T(8,128)(2,1)} %get-tuple-element.86.refs_0_.mixed_ref, ...), custom_call_target="tpu_custom_call" | custom-call | flops 24159191040 | bytes 125829120 | tf_op jit(solution)/shard_map/middle_of/pallas_call | solution.py:364
  200.7 16.5 %ffn_groups.3 = (bf16[512,1536]{1,0:T(8,128)(2,1)}, bf16[512,1536]{1,0:T(8,128)(2,1)}, bf16[512,3072]{1,0:T(8,128)(2,1)}) custom-call(bf16[512,1536]{1,0:T(8,128)(2,1)} %get-tuple-element.98.normed_ref.refs_0_, bf16[1024,1536]{1,0:T(8,128)(2,1)} %bitcast.39, bf16[1536,4608]{1,0:T(8,128)(2,1)} %all-gather.3.cloned.1.call-done.weight_ref.refs_0_.refs_1_.refs_2_, ...), custom_call_target="tpu_custom_call" | custom-call | flops 96636764160 | bytes 157286400 | tf_op jit(solution)/shard_map/ffn_groups/pallas_call | solution.py:420
  217.3 16.5 %ffn_groups.4 = (bf16[512,1536]{1,0:T(8,128)(2,1)}, bf16[512,1536]{1,0:T(8,128)(2,1)}) custom-call(bf16[512,1536]{1,0:T(8,128)(2,1)} %get-tuple-element.98.normed_ref.refs_0_, bf16[1024,1536]{1,0:T(8,128)(2,1)} %bitcast.40, bf16[1536,3072]{1,0:T(8,128)(2,1)} %all-gather.5.cloned.1.call-done.refs_0_.refs_1_.refs_2_.refs_3_.refs_4_.refs_5_, ...), custom_call_target="tpu_custom_call" | custom-call | flops 96636764160 | bytes 157286400 | tf_op jit(solution)/shard_map/ffn_groups/pallas_call | solution.py:420
  233.8 7.6 %middle_of.3 = (f32[512,1536]{1,0:T(8,128)}, bf16[512,1536]{1,0:T(8,128)(2,1)}) custom-call(bf16[1024,1536]{1,0:T(8,128)(2,1)} %bitcast.51, f32[1,1536]{1,0:T(1,128)} %reshape.151.gain_ref, bf16[1536,4608]{1,0:T(8,128)(2,1)} %all-gather.3.cloned.1.call-done.weight_ref.refs_0_.refs_1_.refs_2_, bf16[512,384]{1,0:T(8,128)(2,1)} %get-tuple-element.88.refs_0_.mixed_ref, ...), custom_call_target="tpu_custom_call" | custom-call | flops 24159191040 | bytes 125829120 | tf_op jit(solution)/shard_map/middle_of/pallas_call | solution.py:364
  241.4 29.4 %ffn_groups.5 = (bf16[512,1536]{1,0:T(8,128)(2,1)}, bf16[512,1536]{1,0:T(8,128)(2,1)}, bf16[512,3072]{1,0:T(8,128)(2,1)}) custom-call(bf16[512,1536]{1,0:T(8,128)(2,1)} %get-tuple-element.106.normed_ref.refs_1_, bf16[1024,1536]{1,0:T(8,128)(2,1)} %bitcast.41, bf16[1536,4608]{1,0:T(8,128)(2,1)} %all-gather.3.cloned.1.call-done.weight_ref.refs_0_.refs_1_.refs_2_, ...), custom_call_target="tpu_custom_call" | custom-call | flops 193273528320 | bytes 251658240 | tf_op jit(solution)/shard_map/ffn_groups/pallas_call | solution.py:420
  270.7 2.1 collective-permute-start.19
  275.3 7.0 %grad_middle_of.2 = (f32[512,1536]{1,0:T(8,128)}, bf16[512,1536]{1,0:T(8,128)(2,1)}, bf16[512,384]{1,0:T(8,128)(2,1)}, f32[1,1536]{1,0:T(1,128)}) custom-call(f32[512,1536]{1,0:T(8,128)} %get-tuple-element.108.middle_ref, bf16[1024,1536]{1,0:T(8,128)(2,1)} %bitcast.42, f32[1,1536]{1,0:T(1,128)} %reshape.151.gain_ref, ...), custom_call_target="tpu_custom_call" | custom-call | flops 181193932800 | bytes 3774873600 | tf_op jit(solution)/shard_map/grad_middle_of/pallas_call | solution.py:475
  282.3 18.9 %attend_back.2 = (bf16[512,384]{1,0:T(8,128)(2,1)}, bf16[2048,384]{1,0:T(8,128)(2,1)}) custom-call(s32[4]{0:T(128)} %pad_add_fusion.bases_ref, bf16[2,512,384]{2,1,0:T(8,128)(2,1)} %bitcast.60, s32[2,4,1,128]{3,2,1,0:T(1,128)} %broadcast_maximum_fusion.limit_ref, f32[4,2,256]{2,1,0:T(2,128)} %get-tuple-element.112.lse_ref, ...), custom_call_target="tpu_custom_call" | custom-call | flops 3221225472000 | bytes 1415577600 | tf_op jit(solution)/shard_map/attend_back/pallas_call | solution.py:272
  301.2 5.9 %all-to-all-start = ((bf16[4,512,384]{2,1,0:T(8,128)(2,1)}), bf16[4,512,384]{2,1,0:T(8,128)(2,1)}, u32[]{:S(2)}, u32[]{:S(2)}) async-start(bf16[4,512,384]{2,1,0:T(8,128)(2,1)} %bitcast.46), calls=%async_computation | async-start | bytes 3145728 | tf_op jit(solution)/shard_map/all_to_all | solution.py:770
  307.1 7.0 %grad_middle_of.3 = (f32[512,1536]{1,0:T(8,128)}, bf16[512,1536]{1,0:T(8,128)(2,1)}, bf16[512,384]{1,0:T(8,128)(2,1)}, f32[1,1536]{1,0:T(1,128)}) custom-call(f32[512,1536]{1,0:T(8,128)} %get-tuple-element.116.middle_ref, bf16[1024,1536]{1,0:T(8,128)(2,1)} %bitcast.43, f32[1,1536]{1,0:T(1,128)} %reshape.151.gain_ref, ...), custom_call_target="tpu_custom_call" | custom-call | flops 181193932800 | bytes 3774873600 | tf_op jit(solution)/shard_map/grad_middle_of/pallas_call | solution.py:475
  316.1 2.1 constant_dynamic-slice_fusion.14.wide_ref
  318.2 2.1 constant_dynamic-slice_fusion.8.wide_ref
  320.2 5.4 %project_back.2 = (bf16[512,384]{1,0:T(8,128)(2,1)}, bf16[512,1536]{1,0:T(8,128)(2,1)}) custom-call(bf16[512,384]{1,0:T(8,128)(2,1)} %get-tuple-element.119.query_ref, f32[512,384]{1,0:T(8,128)} %get-tuple-element.165.cos_ref, f32[512,384]{1,0:T(8,128)} %get-tuple-element.163.sin_ref, bf16[1536,896]{1,0:T(8,128)(2,1)} %copy-done.2, ...), custom_call_target="tpu_custom_call" | custom-call | flops 362387865600 | bytes 1179648000 | tf_op jit(solution)/shard_map/project_back/pallas_call | solution.py:326
  325.6 18.8 %attend_back.3 = (bf16[512,384]{1,0:T(8,128)(2,1)}, bf16[2048,384]{1,0:T(8,128)(2,1)}) custom-call(s32[4]{0:T(128)} %pad_add_fusion.bases_ref, bf16[2,512,384]{2,1,0:T(8,128)(2,1)} %bitcast.61, s32[2,4,1,128]{3,2,1,0:T(1,128)} %broadcast_maximum_fusion.limit_ref, f32[4,2,256]{2,1,0:T(2,128)} %get-tuple-element.123.lse_ref, ...), custom_call_target="tpu_custom_call" | custom-call | flops 3221225472000 | bytes 1415577600 | tf_op jit(solution)/shard_map/attend_back/pallas_call | solution.py:272
  344.5 4.4 all-to-all-start.1
  348.9 19.9 %weight_grad.2 = bf16[1536,3072]{1,0:T(8,128)(2,1)} custom-call(bf16[512,1536]{1,0:T(8,128)(2,1)} %get-tuple-element.98.normed_ref.refs_0_, bf16[512,1536]{1,0:T(8,128)(2,1)} %get-tuple-element.106.normed_ref.refs_1_, bf16[512,1536]{1,0:T(8,128)(2,1)} %get-tuple-element.150.refs_2_, bf16[512,1536]{1,0:T(8,128)(2,1)} %get-tuple-element.149.refs_3_, ...), custom_call_target="tpu_custom_call" | custom-call | flops 2899102924800 | bytes 6606028800 | tf_op jit(solution)/shard_map/weight_grad/pallas_call | solution.py:533
  372.8 1.6 collective-permute-start.21
  376.0 6.1 %project_back.3 = (bf16[512,384]{1,0:T(8,128)(2,1)}, bf16[512,1536]{1,0:T(8,128)(2,1)}) custom-call(bf16[512,384]{1,0:T(8,128)(2,1)} %get-tuple-element.129.query_ref, f32[512,384]{1,0:T(8,128)} %get-tuple-element.165.cos_ref, f32[512,384]{1,0:T(8,128)} %get-tuple-element.163.sin_ref, bf16[1536,896]{1,0:T(8,128)(2,1)} %copy-done.2, ...), custom_call_target="tpu_custom_call" | custom-call | flops 362387865600 | bytes 1179648000 | tf_op jit(solution)/shard_map/project_back/pallas_call | solution.py:326
  382.1 4.6 collective-permute-done.20.refs_1_
  386.7 2.2 collective-permute-done.21.refs_2_
  388.9 19.3 %collective-permute-done.22.refs_3_ = bf16[128,1536]{1,0:T(8,128)(2,1)} collective-permute-done((bf16[128,1536]{1,0:T(8,128)(2,1)}, bf16[128,1536]{1,0:T(8,128)(2,1)}, u32[]{:S(2)}, u32[]{:S(2)}) %collective-permute-start.22) | collective-permute-done | bytes 393248 | tf_op jit(solution)/shard_map/ppermute | solution.py:604
  408.3 3.3 grad_inputs_of.2
  411.6 2.9 collective-permute-start.24
  420.4 3.0 collective-permute-done.23
  423.4 2.4 collective-permute-start.27
  428.1 12.4 %weight_grad.3 = bf16[1536,1152]{1,0:T(8,128)(2,1)} custom-call(bf16[512,1536]{1,0:T(8,128)(2,1)} %get-tuple-element.154.refs_0_, bf16[512,1536]{1,0:T(8,128)(2,1)} %get-tuple-element.153.refs_1_, bf16[512,1536]{1,0:T(8,128)(2,1)} %get-tuple-element.136.refs_2_, bf16[512,1536]{1,0:T(8,128)(2,1)} %get-tuple-element.137.refs_3_, ...), custom_call_target="tpu_custom_call" | custom-call | flops 1087163596800 | bytes 3656908800 | tf_op jit(solution)/shard_map/weight_grad/pallas_call | solution.py:533
  440.5 5.7 %reduce-scatter.3.cloned.1.call-done = bf16[192,3072]{1,0:T(8,128)(2,1)} async-done(((bf16[1536,3072]{1,0:T(8,128)(2,1)}), bf16[192,3072]{1,0:T(8,128)(2,1)}) %reduce-scatter.3.cloned.1.call-update) | async-done | bytes 1179664 | tf_op jit(solution)/shard_map/reduce_scatter | solution.py:802
  446.2 1.9 bitcast_dynamic-update-slice_fusion.5
  448.1 4.4 collective-permute-done.25
  452.5 1.9 bitcast_dynamic-update-slice_fusion.4
  454.5 3.9 collective-permute-done.27.refs_2_
  458.3 6.2 %collective-permute-done.28.refs_3_ = bf16[128,1536]{1,0:T(8,128)(2,1)} collective-permute-done((bf16[128,1536]{1,0:T(8,128)(2,1)}, bf16[128,1536]{1,0:T(8,128)(2,1)}, u32[]{:S(2)}, u32[]{:S(2)}) %collective-permute-start.28) | collective-permute-done | bytes 393248 | tf_op jit(solution)/shard_map/ppermute | solution.py:604
  464.5 3.1 grad_inputs_of.3
  467.6 2.0 collective-permute-start.30
  471.1 5.3 %fusion.1 = bf16[1024,1536]{1,0:T(8,128)(2,1)} fusion(f32[512,1536]{1,0:T(8,128)S(1)} %copy-done.6, f32[512,1536]{1,0:T(8,128)S(1)} %copy-done.5, bf16[1024,1536]{1,0:T(8,128)(2,1)} %collective-permute-done.18, bf16[1024,1536]{1,0:T(8,128)(2,1)} %constant_dynamic-update-slice_fusion.7), kind=kLoop, calls=%fused_computation.2 | loop fusion | flops 9437184 | bytes 15728640 | tf_op jit(solution)/shard_map/convert_element_type | solution.py:825
  477.4 3.5 collective-permute-done.29
  480.9 2.6 collective-permute-start.32
  483.5 1.5 collective-permute-start.34
  485.1 9.3 %collective-permute-done.30 = bf16[128,1536]{1,0:T(8,128)(2,1)S(1)} collective-permute-done((bf16[128,1536]{1,0:T(8,128)(2,1)}, bf16[128,1536]{1,0:T(8,128)(2,1)S(1)}, u32[]{:S(2)}, u32[]{:S(2)}) %collective-permute-start.30) | collective-permute-done | bytes 393248 | tf_op jit(solution)/shard_map/ppermute | solution.py:604
  494.5 4.2 collective-permute-done.33
  498.6 2.4 collective-permute-done.34
  502.4 1.6 collective-permute-start.36
  505.9 3.4 pad_maximum_fusion
  (202 shorter events, 57.1 us)
Async XLA Ops:
  7.2 10.5 %copy-start.12 = (bf16[192,1024]{1,0:T(8,128)(2,1)S(1)}, bf16[192,1024]{1,0:T(8,128)(2,1)}, u32[]{:S(2)}) copy-start(bf16[192,1024]{1,0:T(8,128)(2,1)} %param.21) | copy-start | bytes 1179652
  7.2 185.2 %all-gather.3.cloned.1.call-start = ((), (), s32[]{:S(2)}) async-start(), calls=%async_computation.4 | async-start | bytes 15925248 | tf_op jit(solution)/shard_map/all_gather | solution.py:669
  10.0 15.0 %collective-permute-start = (bf16[192,896]{1,0:T(8,128)(2,1)S(1)}, bf16[192,896]{1,0:T(8,128)(2,1)}, u32[]{:S(2)}, u32[]{:S(2)}) collective-permute-start(bf16[192,896]{1,0:T(8,128)(2,1)S(1)} %concatenate.25), channel_id=1, source_target_pairs={{0,4},{4,0},{8,12},{12,8},{1,5},{5,1},{9,13},{13,9},{2,6},{6,2},{1... | collective-permute-start | bytes 1032200 | tf_op jit(solution)/shard_map/ppermute | solution.py:604
  11.5 17.0 %collective-permute-start.1 = (bf16[192,896]{1,0:T(8,128)(2,1)S(1)}, bf16[192,896]{1,0:T(8,128)(2,1)}, u32[]{:S(2)}, u32[]{:S(2)}) collective-permute-start(bf16[192,896]{1,0:T(8,128)(2,1)S(1)} %concatenate.25), channel_id=1, source_target_pairs={{0,8},{4,12},{8,0},{12,4},{1,9},{5,13},{9,1},{13,5},{2,10},{6,14},... | collective-permute-start | bytes 1032200 | tf_op jit(solution)/shard_map/ppermute | solution.py:604
  12.0 17.5 %collective-permute-start.2 = (bf16[192,896]{1,0:T(8,128)(2,1)S(1)}, bf16[192,896]{1,0:T(8,128)(2,1)}, u32[]{:S(2)}, u32[]{:S(2)}) collective-permute-start(bf16[192,896]{1,0:T(8,128)(2,1)S(1)} %concatenate.25), channel_id=1, source_target_pairs={{0,12},{4,8},{8,4},{12,0},{1,13},{5,9},{9,5},{13,1},{2,14},{6,10},... | collective-permute-start | bytes 1032200 | tf_op jit(solution)/shard_map/ppermute | solution.py:604
  13.5 17.1 %collective-permute-start.3 = (bf16[192,384]{1,0:T(8,128)(2,1)}, bf16[192,384]{1,0:T(8,128)(2,1)}, u32[]{:S(2)}, u32[]{:S(2)}) collective-permute-start(bf16[192,384]{1,0:T(8,128)(2,1)} %bitcast.52), channel_id=1, source_target_pairs={{0,1},{1,0},{2,3},{3,2},{4,5},{5,4},{6,7},{7,6},{8,9},{9,8},{10,11... | collective-permute-start | bytes 442376 | tf_op jit(solution)/shard_map/ppermute | solution.py:604
  14.0 16.6 %collective-permute-start.4 = (bf16[192,384]{1,0:T(8,128)(2,1)}, bf16[192,384]{1,0:T(8,128)(2,1)}, u32[]{:S(2)}, u32[]{:S(2)}) collective-permute-start(bf16[192,384]{1,0:T(8,128)(2,1)} %bitcast.53), channel_id=1, source_target_pairs={{0,2},{1,3},{2,0},{3,1},{4,6},{5,7},{6,4},{7,5},{8,10},{9,11},{10,... | collective-permute-start | bytes 442376 | tf_op jit(solution)/shard_map/ppermute | solution.py:604
  17.7 7.1 %copy-start.14 = (bf16[1024,192]{0,1:T(8,128)(2,1)S(1)}, bf16[1024,192]{0,1:T(8,128)(2,1)}, u32[]{:S(2)}) copy-start(bf16[1024,192]{0,1:T(8,128)(2,1)} %param.22) | copy-start | bytes 1179652
  25.0 8.0 %copy-start.30 = (bf16[384,192]{0,1:T(8,128)(2,1)S(1)}, bf16[384,192]{0,1:T(8,128)(2,1)}, u32[]{:S(2)}) copy-start(bf16[384,192]{0,1:T(8,128)(2,1)} %param.18) | copy-start | bytes 442372
  25.0 8.0 %collective-permute-start.5 = (bf16[192,384]{1,0:T(8,128)(2,1)}, bf16[192,384]{1,0:T(8,128)(2,1)S(1)}, u32[]{:S(2)}, u32[]{:S(2)}) collective-permute-start(bf16[192,384]{1,0:T(8,128)(2,1)} %bitcast.54), channel_id=1, source_target_pairs={{0,3},{1,2},{2,1},{3,0},{4,7},{5,6},{6,5},{7,4},{8,11},{9,10},{10,... | collective-permute-start | bytes 442376 | tf_op jit(solution)/shard_map/ppermute | solution.py:604
  30.6 5.8 %copy-start.35 = (s32[2,2]{1,0:T(2,128)S(1)}, s32[2,2]{1,0:T(2,128)}, u32[]{:S(2)}) copy-start(s32[2,2]{1,0:T(2,128)} %param.13) | copy-start | bytes 52
  36.2 181.1 %all-gather.5.cloned.1.call-start = ((), (), s32[]{:S(2)}) async-start(), calls=%async_computation.5 | async-start | bytes 10616832 | tf_op jit(solution)/shard_map/all_gather | solution.py:669
  36.2 4.5 collective-permute-start.6
  44.0 14.3 %copy-start.3 = (bf16[2,512,1536]{2,1,0:T(8,128)(2,1)S(1)}, bf16[2,512,1536]{2,1,0:T(8,128)(2,1)}, u32[]{:S(2)}) copy-start(bf16[2,512,1536]{2,1,0:T(8,128)(2,1)} %param.23) | copy-start | bytes 9437188
  54.2 28.5 %collective-permute-start.7 = (bf16[1024,384]{1,0:T(8,128)(2,1)}, bf16[1024,384]{1,0:T(8,128)(2,1)S(1)}, u32[]{:S(2)}, u32[]{:S(2)}) collective-permute-start(bf16[1024,384]{1,0:T(8,128)(2,1)} %get-tuple-element.85.refs_0_), channel_id=1, source_target_pairs={{0,4},{4,0},{8,12},{12,8},{1,5},{5,1},{9,13},{13,9},{2,6},{6,2},{1... | collective-permute-start | bytes 2359304 | tf_op jit(solution)/shard_map/ppermute | solution.py:604
  55.7 27.0 %collective-permute-start.8 = (bf16[1024,384]{1,0:T(8,128)(2,1)}, bf16[1024,384]{1,0:T(8,128)(2,1)S(1)}, u32[]{:S(2)}, u32[]{:S(2)}) collective-permute-start(bf16[1024,384]{1,0:T(8,128)(2,1)} %get-tuple-element.85.refs_0_), channel_id=1, source_target_pairs={{0,8},{4,12},{8,0},{12,4},{1,9},{5,13},{9,1},{13,5},{2,10},{6,14},... | collective-permute-start | bytes 2359304 | tf_op jit(solution)/shard_map/ppermute | solution.py:604
  56.2 58.2 %collective-permute-start.9 = (bf16[1024,384]{1,0:T(8,128)(2,1)}, bf16[1024,384]{1,0:T(8,128)(2,1)S(1)}, u32[]{:S(2)}, u32[]{:S(2)}) collective-permute-start(bf16[1024,384]{1,0:T(8,128)(2,1)} %get-tuple-element.85.refs_0_), channel_id=1, source_target_pairs={{0,12},{4,8},{8,4},{12,0},{1,13},{5,9},{9,5},{13,1},{2,14},{6,10},... | collective-permute-start | bytes 2359304 | tf_op jit(solution)/shard_map/ppermute | solution.py:604
  60.1 69.2 %collective-permute-start.13 = (bf16[192,3072]{1,0:T(8,128)(2,1)S(1)}, bf16[192,3072]{1,0:T(8,128)(2,1)S(1)}, u32[]{:S(2)}, u32[]{:S(2)}) collective-permute-start(bf16[192,3072]{1,0:T(8,128)(2,1)S(1)} %copy-done.20), channel_id=1, source_target_pairs={{0,2},{1,3},{2,0},{3,1},{4,6},{5,7},{6,4},{7,5},{8,10},{9,11},{10,... | collective-permute-start | bytes 3538952 | tf_op jit(solution)/shard_map/ppermute | solution.py:604
  82.7 31.7 %copy-start.36 = (bf16[1024,384]{1,0:T(8,128)(2,1)}, bf16[1024,384]{1,0:T(8,128)(2,1)S(1)}, u32[]{:S(2)}) copy-start(bf16[1024,384]{1,0:T(8,128)(2,1)S(1)} %collective-permute-done.7.refs_1_) | copy-start | bytes 2359300
  82.7 31.7 %copy-start.37 = (bf16[1024,384]{1,0:T(8,128)(2,1)}, bf16[1024,384]{1,0:T(8,128)(2,1)S(1)}, u32[]{:S(2)}) copy-start(bf16[1024,384]{1,0:T(8,128)(2,1)S(1)} %collective-permute-done.8.refs_2_) | copy-start | bytes 2359300
  115.3 15.1 %copy-start.1 = (f32[512,768]{1,0:T(8,128)S(1)}, f32[512,768]{1,0:T(8,128)}, u32[]{:S(2)}) copy-start(f32[512,768]{1,0:T(8,128)} %get-tuple-element.81.sin_ref) | copy-start | bytes 4718596
  136.7 20.8 %collective-permute-start.10 = (bf16[512,384]{1,0:T(8,128)(2,1)S(1)}, bf16[512,384]{1,0:T(8,128)(2,1)S(1)}, u32[]{:S(2)}, u32[]{:S(2)}) collective-permute-start(bf16[512,384]{1,0:T(8,128)(2,1)S(1)} %copy-done.22), channel_id=1, source_target_pairs={{0,1},{1,0},{2,3},{3,2},{4,5},{5,4},{6,7},{7,6},{8,9},{9,8},{10,11... | collective-permute-start | bytes 1179656 | tf_op jit(solution)/shard_map/ppermute | solution.py:604
  137.3 28.9 %collective-permute-start.11 = (bf16[512,384]{1,0:T(8,128)(2,1)S(1)}, bf16[512,384]{1,0:T(8,128)(2,1)S(1)}, u32[]{:S(2)}, u32[]{:S(2)}) collective-permute-start(bf16[512,384]{1,0:T(8,128)(2,1)S(1)} %copy-done.22), channel_id=1, source_target_pairs={{0,2},{1,3},{2,0},{3,1},{4,6},{5,7},{6,4},{7,5},{8,10},{9,11},{10,... | collective-permute-start | bytes 1179656 | tf_op jit(solution)/shard_map/ppermute | solution.py:604
  139.7 52.7 %collective-permute-start.12 = (bf16[512,384]{1,0:T(8,128)(2,1)S(1)}, bf16[512,384]{1,0:T(8,128)(2,1)S(1)}, u32[]{:S(2)}, u32[]{:S(2)}) collective-permute-start(bf16[512,384]{1,0:T(8,128)(2,1)S(1)} %copy-done.22), channel_id=1, source_target_pairs={{0,3},{1,2},{2,1},{3,0},{4,7},{5,6},{6,5},{7,4},{8,11},{9,10},{10,... | collective-permute-start | bytes 1179656 | tf_op jit(solution)/shard_map/ppermute | solution.py:604
  154.1 79.7 %collective-permute-start.14 = (bf16[512,384]{1,0:T(8,128)(2,1)}, bf16[512,384]{1,0:T(8,128)(2,1)}, u32[]{:S(2)}, u32[]{:S(2)}) collective-permute-start(bf16[512,384]{1,0:T(8,128)(2,1)} %get-tuple-element.88.refs_0_.mixed_ref), channel_id=1, source_target_pairs={{0,1},{1,0},{2,3},{3,2},{4,5},{5,4},{6,7},{7,6},{8,9},{9,8},{10,11... | collective-permute-start | bytes 1179656 | tf_op jit(solution)/shard_map/ppermute | solution.py:604
  155.5 78.2 %collective-permute-start.15 = (bf16[512,384]{1,0:T(8,128)(2,1)}, bf16[512,384]{1,0:T(8,128)(2,1)}, u32[]{:S(2)}, u32[]{:S(2)}) collective-permute-start(bf16[512,384]{1,0:T(8,128)(2,1)} %get-tuple-element.88.refs_0_.mixed_ref), channel_id=1, source_target_pairs={{0,2},{1,3},{2,0},{3,1},{4,6},{5,7},{6,4},{7,5},{8,10},{9,11},{10,... | collective-permute-start | bytes 1179656 | tf_op jit(solution)/shard_map/ppermute | solution.py:604
  157.5 34.9 %copy-start.39 = (bf16[512,384]{1,0:T(8,128)(2,1)}, bf16[512,384]{1,0:T(8,128)(2,1)S(1)}, u32[]{:S(2)}) copy-start(bf16[512,384]{1,0:T(8,128)(2,1)S(1)} %collective-permute-done.10.refs_1_) | copy-start | bytes 1179652
  157.5 76.3 %collective-permute-start.16 = (bf16[512,384]{1,0:T(8,128)(2,1)}, bf16[512,384]{1,0:T(8,128)(2,1)}, u32[]{:S(2)}, u32[]{:S(2)}) collective-permute-start(bf16[512,384]{1,0:T(8,128)(2,1)} %get-tuple-element.88.refs_0_.mixed_ref), channel_id=1, source_target_pairs={{0,3},{1,2},{2,1},{3,0},{4,7},{5,6},{6,5},{7,4},{8,11},{9,10},{10,... | collective-permute-start | bytes 1179656 | tf_op jit(solution)/shard_map/ppermute | solution.py:604
  166.1 26.3 %copy-start.40 = (bf16[512,384]{1,0:T(8,128)(2,1)}, bf16[512,384]{1,0:T(8,128)(2,1)S(1)}, u32[]{:S(2)}) copy-start(bf16[512,384]{1,0:T(8,128)(2,1)S(1)} %collective-permute-done.11.refs_2_) | copy-start | bytes 1179652
  241.3 34.0 %collective-permute-start.17 = (bf16[512,1536]{1,0:T(8,128)(2,1)}, bf16[512,1536]{1,0:T(8,128)(2,1)}, u32[]{:S(2)}, u32[]{:S(2)}) collective-permute-start(bf16[512,1536]{1,0:T(8,128)(2,1)} %get-tuple-element.109.refs_0_), channel_id=1, source_target_pairs={{0,1},{1,0},{2,3},{3,2},{4,5},{5,4},{6,7},{7,6},{8,9},{9,8},{10,11... | collective-permute-start | bytes 4718600 | tf_op jit(solution)/shard_map/ppermute | solution.py:604
  241.3 31.5 %copy-start.9 = (bf16[512,1536]{1,0:T(8,128)(2,1)S(1)}, bf16[512,1536]{1,0:T(8,128)(2,1)}, u32[]{:S(2)}) copy-start(bf16[512,1536]{1,0:T(8,128)(2,1)} %get-tuple-element.102) | copy-start | bytes 4718596
  270.7 36.4 %collective-permute-start.19 = (bf16[512,1536]{1,0:T(8,128)(2,1)}, bf16[512,1536]{1,0:T(8,128)(2,1)}, u32[]{:S(2)}, u32[]{:S(2)}) collective-permute-start(bf16[512,1536]{1,0:T(8,128)(2,1)} %get-tuple-element.117.refs_0_), channel_id=1, source_target_pairs={{0,1},{1,0},{2,3},{3,2},{4,5},{5,4},{6,7},{7,6},{8,9},{9,8},{10,11... | collective-permute-start | bytes 4718600 | tf_op jit(solution)/shard_map/ppermute | solution.py:604
  301.2 19.1 %all-to-all-start = ((bf16[4,512,384]{2,1,0:T(8,128)(2,1)}), bf16[4,512,384]{2,1,0:T(8,128)(2,1)}, u32[]{:S(2)}, u32[]{:S(2)}) async-start(bf16[4,512,384]{2,1,0:T(8,128)(2,1)} %bitcast.46), calls=%async_computation | async-start | bytes 3145728 | tf_op jit(solution)/shard_map/all_to_all | solution.py:770
  307.1 7.7 %copy-start.34 = (f32[1,1536]{1,0:T(1,128)S(1)}, f32[1,1536]{1,0:T(1,128)}, u32[]{:S(2)}) copy-start(f32[1,1536]{1,0:T(1,128)} %get-tuple-element.144) | copy-start | bytes 18436
  314.1 112.6 %collective-permute-start.18 = (bf16[1024,1536]{1,0:T(8,128)(2,1)}, bf16[1024,1536]{1,0:T(8,128)(2,1)}, u32[]{:S(2)}, u32[]{:S(2)}) collective-permute-start(bf16[1024,1536]{1,0:T(8,128)(2,1)} %constant_dynamic-update-slice_fusion.7), channel_id=1, source_target_pairs={{0,1},{1,0},{2,3},{3,2},{4,5},{5,4},{6,7},{7,6},{8,9},{9,8},{10,11... | collective-permute-start | bytes 9437192 | tf_op jit(solution)/shard_map/ppermute | solution.py:604
  344.5 31.5 %all-to-all-start.1 = ((bf16[4,512,384]{2,1,0:T(8,128)(2,1)}), bf16[4,512,384]{2,1,0:T(8,128)(2,1)}, u32[]{:S(2)}, u32[]{:S(2)}) async-start(bf16[4,512,384]{2,1,0:T(8,128)(2,1)} %bitcast.45), calls=%async_computation.1 | async-start | bytes 3145728 | tf_op jit(solution)/shard_map/all_to_all | solution.py:770
  348.9 97.3 %reduce-scatter.3.cloned.1.call-start = ((), (), s32[]{:S(2)}) async-start(), calls=%async_computation.6 | async-start | bytes 10616832 | tf_op jit(solution)/shard_map/reduce_scatter | solution.py:802
  368.8 142.6 %reduce-scatter.5.cloned.1.call-start = ((), (), s32[]{:S(2)}) async-start(), calls=%async_computation.7 | async-start | bytes 3981312 | tf_op jit(solution)/shard_map/reduce_scatter | solution.py:815
  370.2 4.7 copy-start.25
  370.2 4.7 copy-start.26
  371.4 15.4 %collective-permute-start.20 = (bf16[128,1536]{1,0:T(8,128)(2,1)}, bf16[128,1536]{1,0:T(8,128)(2,1)}, u32[]{:S(2)}, u32[]{:S(2)}) collective-permute-start(bf16[128,1536]{1,0:T(8,128)(2,1)} %get-tuple-element.161), channel_id=1, source_target_pairs={{0,1},{1,0},{2,3},{3,2},{4,5},{5,4},{6,7},{7,6},{8,9},{9,8},{10,11... | collective-permute-start | bytes 1179656 | tf_op jit(solution)/shard_map/ppermute | solution.py:604
  372.8 16.2 %collective-permute-start.21 = (bf16[128,1536]{1,0:T(8,128)(2,1)}, bf16[128,1536]{1,0:T(8,128)(2,1)}, u32[]{:S(2)}, u32[]{:S(2)}) collective-permute-start(bf16[128,1536]{1,0:T(8,128)(2,1)} %get-tuple-element.160), channel_id=1, source_target_pairs={{0,2},{1,3},{2,0},{3,1},{4,6},{5,7},{6,4},{7,5},{8,10},{9,11},{10,... | collective-permute-start | bytes 1179656 | tf_op jit(solution)/shard_map/ppermute | solution.py:604
  374.3 34.0 %collective-permute-start.22 = (bf16[128,1536]{1,0:T(8,128)(2,1)}, bf16[128,1536]{1,0:T(8,128)(2,1)}, u32[]{:S(2)}, u32[]{:S(2)}) collective-permute-start(bf16[128,1536]{1,0:T(8,128)(2,1)} %get-tuple-element.159), channel_id=1, source_target_pairs={{0,3},{1,2},{2,1},{3,0},{4,7},{5,6},{6,5},{7,4},{8,11},{9,10},{10,... | collective-permute-start | bytes 1179656 | tf_op jit(solution)/shard_map/ppermute | solution.py:604
  382.1 33.0 %copy-start.17 = (bf16[512,1536]{1,0:T(8,128)(2,1)S(1)}, bf16[512,1536]{1,0:T(8,128)(2,1)}, u32[]{:S(2)}) copy-start(bf16[512,1536]{1,0:T(8,128)(2,1)} %get-tuple-element.139) | copy-start | bytes 4718596
  411.6 11.8 %collective-permute-start.23 = (bf16[128,1536]{1,0:T(8,128)(2,1)}, bf16[128,1536]{1,0:T(8,128)(2,1)S(1)}, u32[]{:S(2)}, u32[]{:S(2)}) collective-permute-start(bf16[128,1536]{1,0:T(8,128)(2,1)} %get-tuple-element.134), channel_id=1, source_target_pairs={{0,1},{1,0},{2,3},{3,2},{4,5},{5,4},{6,7},{7,6},{8,9},{9,8},{10,11... | collective-permute-start | bytes 1179656 | tf_op jit(solution)/shard_map/ppermute | solution.py:604
  411.6 34.6 %collective-permute-start.24 = (bf16[128,1536]{1,0:T(8,128)(2,1)}, bf16[128,1536]{1,0:T(8,128)(2,1)}, u32[]{:S(2)}, u32[]{:S(2)}) collective-permute-start(bf16[128,1536]{1,0:T(8,128)(2,1)} %get-tuple-element.134), channel_id=1, source_target_pairs={{0,2},{1,3},{2,0},{3,1},{4,6},{5,7},{6,4},{7,5},{8,10},{9,11},{10,... | collective-permute-start | bytes 1179656 | tf_op jit(solution)/shard_map/ppermute | solution.py:604
  414.5 38.0 %collective-permute-start.25 = (bf16[128,1536]{1,0:T(8,128)(2,1)}, bf16[128,1536]{1,0:T(8,128)(2,1)}, u32[]{:S(2)}, u32[]{:S(2)}) collective-permute-start(bf16[128,1536]{1,0:T(8,128)(2,1)} %get-tuple-element.134), channel_id=1, source_target_pairs={{0,3},{1,2},{2,1},{3,0},{4,7},{5,6},{6,5},{7,4},{8,11},{9,10},{10,... | collective-permute-start | bytes 1179656 | tf_op jit(solution)/shard_map/ppermute | solution.py:604
  416.3 38.1 %collective-permute-start.26 = (bf16[128,1536]{1,0:T(8,128)(2,1)}, bf16[128,1536]{1,0:T(8,128)(2,1)}, u32[]{:S(2)}, u32[]{:S(2)}) collective-permute-start(bf16[128,1536]{1,0:T(8,128)(2,1)} %get-tuple-element.157), channel_id=1, source_target_pairs={{0,1},{1,0},{2,3},{3,2},{4,5},{5,4},{6,7},{7,6},{8,9},{9,8},{10,11... | collective-permute-start | bytes 1179656 | tf_op jit(solution)/shard_map/ppermute | solution.py:604
  423.4 34.9 %collective-permute-start.27 = (bf16[128,1536]{1,0:T(8,128)(2,1)}, bf16[128,1536]{1,0:T(8,128)(2,1)}, u32[]{:S(2)}, u32[]{:S(2)}) collective-permute-start(bf16[128,1536]{1,0:T(8,128)(2,1)} %get-tuple-element.156), channel_id=1, source_target_pairs={{0,2},{1,3},{2,0},{3,1},{4,6},{5,7},{6,4},{7,5},{8,10},{9,11},{10,... | collective-permute-start | bytes 1179656 | tf_op jit(solution)/shard_map/ppermute | solution.py:604
  426.7 37.8 %collective-permute-start.28 = (bf16[128,1536]{1,0:T(8,128)(2,1)}, bf16[128,1536]{1,0:T(8,128)(2,1)}, u32[]{:S(2)}, u32[]{:S(2)}) collective-permute-start(bf16[128,1536]{1,0:T(8,128)(2,1)} %get-tuple-element.155), channel_id=1, source_target_pairs={{0,3},{1,2},{2,1},{3,0},{4,7},{5,6},{6,5},{7,4},{8,11},{9,10},{10,... | collective-permute-start | bytes 1179656 | tf_op jit(solution)/shard_map/ppermute | solution.py:604
  446.2 24.9 %copy-start.6 = (f32[512,1536]{1,0:T(8,128)S(1)}, f32[512,1536]{1,0:T(8,128)}, u32[]{:S(2)}) copy-start(f32[512,1536]{1,0:T(8,128)} %get-tuple-element.116.middle_ref) | copy-start | bytes 9437188
  452.5 18.6 %copy-start.5 = (f32[512,1536]{1,0:T(8,128)S(1)}, f32[512,1536]{1,0:T(8,128)}, u32[]{:S(2)}) copy-start(f32[512,1536]{1,0:T(8,128)} %get-tuple-element.108.middle_ref) | copy-start | bytes 9437188
  467.6 13.3 %collective-permute-start.29 = (bf16[128,1536]{1,0:T(8,128)(2,1)}, bf16[128,1536]{1,0:T(8,128)(2,1)S(1)}, u32[]{:S(2)}, u32[]{:S(2)}) collective-permute-start(bf16[128,1536]{1,0:T(8,128)(2,1)} %get-tuple-element.140), channel_id=1, source_target_pairs={{0,1},{1,0},{2,3},{3,2},{4,5},{5,4},{6,7},{7,6},{8,9},{9,8},{10,11... | collective-permute-start | bytes 1179656 | tf_op jit(solution)/shard_map/ppermute | solution.py:604
  467.6 26.8 %collective-permute-start.30 = (bf16[128,1536]{1,0:T(8,128)(2,1)}, bf16[128,1536]{1,0:T(8,128)(2,1)S(1)}, u32[]{:S(2)}, u32[]{:S(2)}) collective-permute-start(bf16[128,1536]{1,0:T(8,128)(2,1)} %get-tuple-element.140), channel_id=1, source_target_pairs={{0,2},{1,3},{2,0},{3,1},{4,6},{5,7},{6,4},{7,5},{8,10},{9,11},{10,... | collective-permute-start | bytes 1179656 | tf_op jit(solution)/shard_map/ppermute | solution.py:604
  469.6 31.6 %collective-permute-start.31 = (bf16[128,1536]{1,0:T(8,128)(2,1)}, bf16[128,1536]{1,0:T(8,128)(2,1)S(1)}, u32[]{:S(2)}, u32[]{:S(2)}) collective-permute-start(bf16[128,1536]{1,0:T(8,128)(2,1)} %get-tuple-element.140), channel_id=1, source_target_pairs={{0,3},{1,2},{2,1},{3,0},{4,7},{5,6},{6,5},{7,4},{8,11},{9,10},{10,... | collective-permute-start | bytes 1179656 | tf_op jit(solution)/shard_map/ppermute | solution.py:604
  477.4 23.7 %copy-start.31 = (f32[1,1536]{1,0:T(1,128)S(1)}, f32[1,1536]{1,0:T(1,128)}, u32[]{:S(2)}) copy-start(f32[1,1536]{1,0:T(1,128)} %add.171) | copy-start | bytes 18436
  480.9 13.5 %collective-permute-start.32 = (f32[1,1536]{1,0:T(1,128)S(1)}, f32[1,1536]{1,0:T(1,128)S(1)}, u32[]{:S(2)}, u32[]{:S(2)}) collective-permute-start(f32[1,1536]{1,0:T(1,128)S(1)} %add.167), channel_id=1, source_target_pairs={{0,1},{1,0},{2,3},{3,2},{4,5},{5,4},{6,7},{7,6},{8,9},{9,8},{10,11... | collective-permute-start | bytes 18440 | tf_op jit(solution)/shard_map/ppermute | solution.py:604
  483.5 15.1 %collective-permute-start.33 = (f32[1,1536]{1,0:T(1,128)S(1)}, f32[1,1536]{1,0:T(1,128)S(1)}, u32[]{:S(2)}, u32[]{:S(2)}) collective-permute-start(f32[1,1536]{1,0:T(1,128)S(1)} %add.167), channel_id=1, source_target_pairs={{0,2},{1,3},{2,0},{3,1},{4,6},{5,7},{6,4},{7,5},{8,10},{9,11},{10,... | collective-permute-start | bytes 18440 | tf_op jit(solution)/shard_map/ppermute | solution.py:604
  483.5 17.6 %collective-permute-start.34 = (f32[1,1536]{1,0:T(1,128)S(1)}, f32[1,1536]{1,0:T(1,128)S(1)}, u32[]{:S(2)}, u32[]{:S(2)}) collective-permute-start(f32[1,1536]{1,0:T(1,128)S(1)} %add.167), channel_id=1, source_target_pairs={{0,3},{1,2},{2,1},{3,0},{4,7},{5,6},{6,5},{7,4},{8,11},{9,10},{10,... | collective-permute-start | bytes 18440 | tf_op jit(solution)/shard_map/ppermute | solution.py:604
  501.1 1.2 collective-permute-start.35
  502.4 7.6 %copy-start.18 = (bf16[192,3072]{1,0:T(8,128)(2,1)S(1)}, bf16[192,3072]{1,0:T(8,128)(2,1)}, u32[]{:S(2)}) copy-start(bf16[192,3072]{1,0:T(8,128)(2,1)} %reduce-scatter.3.cloned.1.call-done) | copy-start | bytes 3538948
  502.4 6.9 %collective-permute-start.36 = (f32[2,1536]{1,0:T(2,128)S(1)}, f32[2,1536]{1,0:T(2,128)S(1)}, u32[]{:S(2)}, u32[]{:S(2)}) collective-permute-start(f32[2,1536]{1,0:T(2,128)S(1)} %fusion.19), channel_id=1, source_target_pairs={{0,4},{4,0},{8,12},{12,8},{1,5},{5,1},{9,13},{13,9},{2,6},{6,2},{1... | collective-permute-start | bytes 36872 | tf_op jit(solution)/shard_map/ppermute | solution.py:604
  504.0 5.3 %collective-permute-start.37 = (f32[2,1536]{1,0:T(2,128)S(1)}, f32[2,1536]{1,0:T(2,128)S(1)}, u32[]{:S(2)}, u32[]{:S(2)}) collective-permute-start(f32[2,1536]{1,0:T(2,128)S(1)} %fusion.19), channel_id=1, source_target_pairs={{0,8},{4,12},{8,0},{12,4},{1,9},{5,13},{9,1},{13,5},{2,10},{6,14},... | collective-permute-start | bytes 36872 | tf_op jit(solution)/shard_map/ppermute | solution.py:604
  504.5 4.8 collective-permute-start.38
  (23 other events, 55.1 us)
Sparse Core Ops, SparseCore 0:
  36.3 103.3 all-gather.2
  141.6 59.0 all-gather.4
  368.9 77.1 reduce-scatter.2
  449.5 48.1 reduce-scatter.4

commit v4 on v3

--- a/solution.py
+++ b/solution.py
@@ -803,7 +803,7 @@
     held, pieces = pieces, to_owners(n_seqs - 1, terms)
     if n_seqs > 1:
         through_norm(n_seqs - 2, held)
-    grad_attn[0] = after(grad_attn[0], out_far, *last)
+    grad_attn[0] = after(grad_attn[0], *last)
     attn_grads = weight_grad(
         [normed_one[s * toks : (s + 1) * toks] for s in seqs],
         grad_attn,

time: 530 us -> 537 us (1.013)
  waiting for transfers between devices: 163 us -> 170 us
    ppermute x39, waiting for transfers between devices: 157 us -> 164 us  [swap(): return lax.ppermute(value, axis, [(i, i ^ step) for i in range(count)])]
    reduce_scatter x1, waiting for transfers between devices: 5.7 us -> 0.02 us  [local(): lax.psum_scatter(ffn_grads, both, scatter_dimension=0, tiled=True)]
    reduce_scatter x1, waiting for transfers between devices: 0.01 us -> 5.49 us  [local(): lax.psum_scatter(after(attn_grads, ffn_grads), both, scatter_dimension=0,...]
    unnamed x91 -> x95, local copies, waits for them, and re-layouts: 11.8 us -> 12.5 us
  transfers between devices with their start and end apart: 45 -> 45, of which waited for: 19 -> 15; matrix products, arithmetic and copies ran while one was open for 11% -> 10% of each run, Pallas kernels for 40% -> 39%
where the time goes in v4:
time: 537 us; the launch traced here: 530 us
  Pallas kernels  217 us (40%)
  waiting for transfers between devices  170 us (32%)
  starting transfers between devices  59.5 us (11%)
  local copies, waits for them, and re-layouts  45 us (8%)
  other arithmetic  24 us (4%)
  between operations  14.7 us (3%)
    ppermute x39, waiting for transfers between devices, swap(): return lax.ppermute(value, axis, [(i, i ^ step) for i in range(count)])  164 us
    pallas_call x3, Pallas kernels, ffn_groups(): pl.pallas_call(functools.partial(ffn_kernel, keep, bool(base), groups), g...  62.4 us
    ppermute x39, starting transfers between devices, swap(): return lax.ppermute(value, axis, [(i, i ^ step) for i in range(count)])  48.9 us
    pallas_call x2, Pallas kernels, attend_back(): pl.pallas_call(functools.partial(attend_back_kernel, n_groups, repeat, n_...  37.7 us
    pallas_call x2, Pallas kernels, weight_grad(): pl.pallas_call(functools.partial(weight_grad_kernel, n_seqs, tile, split)...  31.6 us
    pallas_call x2, Pallas kernels, attend(): pl.pallas_call(functools.partial(attend_kernel, n_groups, repeat, n_block...  27.9 us
    pallas_call x2, Pallas kernels, middle_of(): pl.pallas_call(functools.partial(middle_kernel, len(pieces)), grid=(steps...  15.1 us
    pallas_call x2, Pallas kernels, grad_middle_of(): pl.pallas_call(functools.partial(grad_middle_kernel, len(backs)), grid=(s...  14 us
  transfers between devices with their start and end apart: 45, of which 15 were waited for; matrix products, arithmetic and copies ran while one was open for 10% of the time, Pallas kernels for 39%

profile of v4, /device:TPU:12, one launch (start us, length us, event | category | flops | bytes accessed | tf_op | source)
XLA Modules:
  0.0 529.9 jit_solution(12572751237663403974)
XLA Ops:
  10.0 1.6 collective-permute-start
  12.0 1.5 collective-permute-start.2
  14.0 2.6 collective-permute-start.4
  17.7 7.1 %fusion.3 = (f32[512,768]{1,0:T(8,128)}, f32[512,768]{1,0:T(8,128)}) fusion(f32[768]{0:T(1024)S(1)} %get-tuple-element.179, f32[768]{0:T(1024)S(1)} %get-tuple-element.178, f32[512]{0:T(512)S(1)} %get-tuple-element.181, pred[768]{0:T(1024)(128)(4,1)S(1)} %iota_compare_fusion), kind=kLoop, calls=%fused_computation.7 | loop fusion | flops 1179648 | bytes 3154688 | tf_op jit(solution)/shard_map/mul | solution.py:592
  26.6 2.0 collective-permute-done.1
  30.6 2.4 collective-permute-done.5
  37.1 2.1 constant_dynamic-slice_fusion.15
  40.8 1.6 constant_dynamic-update-slice_fusion.9.weight_ref
  43.9 10.2 %project.1 = (bf16[1024,1536]{1,0:T(8,128)(2,1)}, bf16[1024,384]{1,0:T(8,128)(2,1)}, bf16[1024,384]{1,0:T(8,128)(2,1)}) custom-call(bf16[1024,1536]{1,0:T(8,128)(2,1)} %bitcast.49, f32[1,1536]{1,0:T(1,128)} %reshape.150.gain_ref, bf16[1536,896]{1,0:T(8,128)(2,1)} %copy-done.2, f32[512,768]{1,0:T(8,128)} %get-tuple-element.80.cos_ref, ...), custom_call_target="tpu_custom_call" | custom-call | flops 24159191040 | bytes 86507520 | tf_op jit(solution)/shard_map/project/pallas_call | solution.py:80
  54.1 1.5 collective-permute-start.7
  56.1 1.5 collective-permute-start.9
  58.2 1.9 slice_bitcast_fusion
  60.5 22.2 %collective-permute-done.7.refs_1_ = bf16[1024,384]{1,0:T(8,128)(2,1)S(1)} collective-permute-done((bf16[1024,384]{1,0:T(8,128)(2,1)}, bf16[1024,384]{1,0:T(8,128)(2,1)S(1)}, u32[]{:S(2)}, u32[]{:S(2)}) %collective-permute-start.7) | collective-permute-done | bytes 786464 | tf_op jit(solution)/shard_map/ppermute | solution.py:604
  82.7 31.7 %collective-permute-done.9.refs_3_ = bf16[1024,384]{1,0:T(8,128)(2,1)S(1)} collective-permute-done((bf16[1024,384]{1,0:T(8,128)(2,1)}, bf16[1024,384]{1,0:T(8,128)(2,1)S(1)}, u32[]{:S(2)}, u32[]{:S(2)}) %collective-permute-start.9) | collective-permute-done | bytes 786464 | tf_op jit(solution)/shard_map/ppermute | solution.py:604
  115.3 14.0 %attend.2 = (bf16[512,384]{1,0:T(8,128)(2,1)}, f32[4,2,256]{2,1,0:T(2,128)}) custom-call(s32[4]{0:T(128)} %pad_add_fusion.bases_ref, bf16[2,512,384]{2,1,0:T(8,128)(2,1)} %bitcast.58, s32[2,4,1,128]{3,2,1,0:T(1,128)} %broadcast_maximum_fusion.limit_ref, bf16[1024,384]{1,0:T(8,128)(2,1)} %get-tuple-element.85.refs_0_, bf16[1024,384]{1,0:T(8,128)(2,1)} %copy-done.38, ...), custom_call_target="tpu_custom_call" | custom-call | flops 42949672960 | bytes 23592960 | tf_op jit(solution)/shard_map/attend/pallas_call | solution.py:171
  134.8 1.8 fusion.20
  137.2 2.4 collective-permute-start.11
  140.2 13.9 %attend.3 = (bf16[512,384]{1,0:T(8,128)(2,1)}, f32[4,2,256]{2,1,0:T(2,128)}) custom-call(s32[4]{0:T(128)} %pad_add_fusion.bases_ref, bf16[2,512,384]{2,1,0:T(8,128)(2,1)} %bitcast.59, s32[2,4,1,128]{3,2,1,0:T(1,128)} %broadcast_maximum_fusion.limit_ref, bf16[1024,384]{1,0:T(8,128)(2,1)} %get-tuple-element.85.refs_0_, bf16[1024,384]{1,0:T(8,128)(2,1)} %copy-done.38, ...), custom_call_target="tpu_custom_call" | custom-call | flops 42949672960 | bytes 23592960 | tf_op jit(solution)/shard_map/attend/pallas_call | solution.py:171
  154.1 1.4 collective-permute-start.14
  155.5 2.0 collective-permute-start.15
  158.0 8.1 %collective-permute-done.11.refs_2_ = bf16[512,384]{1,0:T(8,128)(2,1)S(1)} collective-permute-done((bf16[512,384]{1,0:T(8,128)(2,1)S(1)}, bf16[512,384]{1,0:T(8,128)(2,1)S(1)}, u32[]{:S(2)}, u32[]{:S(2)}) %collective-permute-start.11) | collective-permute-done | bytes 393248 | tf_op jit(solution)/shard_map/ppermute | solution.py:604
  166.1 26.3 %collective-permute-done.12.refs_3_ = bf16[512,384]{1,0:T(8,128)(2,1)S(1)} collective-permute-done((bf16[512,384]{1,0:T(8,128)(2,1)S(1)}, bf16[512,384]{1,0:T(8,128)(2,1)S(1)}, u32[]{:S(2)}, u32[]{:S(2)}) %collective-permute-start.12) | collective-permute-done | bytes 393248 | tf_op jit(solution)/shard_map/ppermute | solution.py:604
  193.1 7.6 %middle_of.2 = (f32[512,1536]{1,0:T(8,128)}, bf16[512,1536]{1,0:T(8,128)(2,1)}) custom-call(bf16[1024,1536]{1,0:T(8,128)(2,1)} %bitcast.50, f32[1,1536]{1,0:T(1,128)} %reshape.151.gain_ref, bf16[1536,4608]{1,0:T(8,128)(2,1)} %all-gather.3.cloned.1.call-done.weight_ref.refs_0_.refs_1_.refs_2_, bf16[512,384]{1,0:T(8,128)(2,1)} %get-tuple-element.86.refs_0_.mixed_ref, ...), custom_call_target="tpu_custom_call" | custom-call | flops 24159191040 | bytes 125829120 | tf_op jit(solution)/shard_map/middle_of/pallas_call | solution.py:364
  200.7 16.5 %ffn_groups.3 = (bf16[512,1536]{1,0:T(8,128)(2,1)}, bf16[512,1536]{1,0:T(8,128)(2,1)}, bf16[512,3072]{1,0:T(8,128)(2,1)}) custom-call(bf16[512,1536]{1,0:T(8,128)(2,1)} %get-tuple-element.98.normed_ref.refs_0_, bf16[1024,1536]{1,0:T(8,128)(2,1)} %bitcast.39, bf16[1536,4608]{1,0:T(8,128)(2,1)} %all-gather.3.cloned.1.call-done.weight_ref.refs_0_.refs_1_.refs_2_, ...), custom_call_target="tpu_custom_call" | custom-call | flops 96636764160 | bytes 157286400 | tf_op jit(solution)/shard_map/ffn_groups/pallas_call | solution.py:420
  217.2 16.5 %ffn_groups.4 = (bf16[512,1536]{1,0:T(8,128)(2,1)}, bf16[512,1536]{1,0:T(8,128)(2,1)}) custom-call(bf16[512,1536]{1,0:T(8,128)(2,1)} %get-tuple-element.98.normed_ref.refs_0_, bf16[1024,1536]{1,0:T(8,128)(2,1)} %bitcast.40, bf16[1536,3072]{1,0:T(8,128)(2,1)} %all-gather.5.cloned.1.call-done.refs_0_.refs_1_.refs_2_.refs_3_.refs_4_.refs_5_, ...), custom_call_target="tpu_custom_call" | custom-call | flops 96636764160 | bytes 157286400 | tf_op jit(solution)/shard_map/ffn_groups/pallas_call | solution.py:420
  233.7 7.6 %middle_of.3 = (f32[512,1536]{1,0:T(8,128)}, bf16[512,1536]{1,0:T(8,128)(2,1)}) custom-call(bf16[1024,1536]{1,0:T(8,128)(2,1)} %bitcast.51, f32[1,1536]{1,0:T(1,128)} %reshape.151.gain_ref, bf16[1536,4608]{1,0:T(8,128)(2,1)} %all-gather.3.cloned.1.call-done.weight_ref.refs_0_.refs_1_.refs_2_, bf16[512,384]{1,0:T(8,128)(2,1)} %get-tuple-element.88.refs_0_.mixed_ref, ...), custom_call_target="tpu_custom_call" | custom-call | flops 24159191040 | bytes 125829120 | tf_op jit(solution)/shard_map/middle_of/pallas_call | solution.py:364
  241.3 29.3 %ffn_groups.5 = (bf16[512,1536]{1,0:T(8,128)(2,1)}, bf16[512,1536]{1,0:T(8,128)(2,1)}, bf16[512,3072]{1,0:T(8,128)(2,1)}) custom-call(bf16[512,1536]{1,0:T(8,128)(2,1)} %get-tuple-element.106.normed_ref.refs_1_, bf16[1024,1536]{1,0:T(8,128)(2,1)} %bitcast.41, bf16[1536,4608]{1,0:T(8,128)(2,1)} %all-gather.3.cloned.1.call-done.weight_ref.refs_0_.refs_1_.refs_2_, ...), custom_call_target="tpu_custom_call" | custom-call | flops 193273528320 | bytes 251658240 | tf_op jit(solution)/shard_map/ffn_groups/pallas_call | solution.py:420
  270.7 2.1 collective-permute-start.19
  275.3 7.0 %grad_middle_of.2 = (f32[512,1536]{1,0:T(8,128)}, bf16[512,1536]{1,0:T(8,128)(2,1)}, bf16[512,384]{1,0:T(8,128)(2,1)}, f32[1,1536]{1,0:T(1,128)}) custom-call(f32[512,1536]{1,0:T(8,128)} %get-tuple-element.108.middle_ref, bf16[1024,1536]{1,0:T(8,128)(2,1)} %bitcast.42, f32[1,1536]{1,0:T(1,128)} %reshape.151.gain_ref, ...), custom_call_target="tpu_custom_call" | custom-call | flops 181193932800 | bytes 3774873600 | tf_op jit(solution)/shard_map/grad_middle_of/pallas_call | solution.py:475
  282.2 18.9 %attend_back.2 = (bf16[512,384]{1,0:T(8,128)(2,1)}, bf16[2048,384]{1,0:T(8,128)(2,1)}) custom-call(s32[4]{0:T(128)} %pad_add_fusion.bases_ref, bf16[2,512,384]{2,1,0:T(8,128)(2,1)} %bitcast.60, s32[2,4,1,128]{3,2,1,0:T(1,128)} %broadcast_maximum_fusion.limit_ref, f32[4,2,256]{2,1,0:T(2,128)} %get-tuple-element.112.lse_ref, ...), custom_call_target="tpu_custom_call" | custom-call | flops 3221225472000 | bytes 1415577600 | tf_op jit(solution)/shard_map/attend_back/pallas_call | solution.py:272
  301.8 5.9 %all-to-all-start = ((bf16[4,512,384]{2,1,0:T(8,128)(2,1)}), bf16[4,512,384]{2,1,0:T(8,128)(2,1)}, u32[]{:S(2)}, u32[]{:S(2)}) async-start(bf16[4,512,384]{2,1,0:T(8,128)(2,1)} %bitcast.46), calls=%async_computation | async-start | bytes 3145728 | tf_op jit(solution)/shard_map/all_to_all | solution.py:770
  307.8 7.0 %grad_middle_of.3 = (f32[512,1536]{1,0:T(8,128)}, bf16[512,1536]{1,0:T(8,128)(2,1)}, bf16[512,384]{1,0:T(8,128)(2,1)}, f32[1,1536]{1,0:T(1,128)}) custom-call(f32[512,1536]{1,0:T(8,128)} %get-tuple-element.116.middle_ref, bf16[1024,1536]{1,0:T(8,128)(2,1)} %bitcast.43, f32[1,1536]{1,0:T(1,128)} %reshape.151.gain_ref, ...), custom_call_target="tpu_custom_call" | custom-call | flops 181193932800 | bytes 3774873600 | tf_op jit(solution)/shard_map/grad_middle_of/pallas_call | solution.py:475
  316.1 2.1 constant_dynamic-slice_fusion.14.wide_ref
  318.1 2.1 constant_dynamic-slice_fusion.8.wide_ref
  320.2 5.4 %project_back.2 = (bf16[512,384]{1,0:T(8,128)(2,1)}, bf16[512,1536]{1,0:T(8,128)(2,1)}) custom-call(bf16[512,384]{1,0:T(8,128)(2,1)} %get-tuple-element.119.query_ref, f32[512,384]{1,0:T(8,128)} %get-tuple-element.165.cos_ref, f32[512,384]{1,0:T(8,128)} %get-tuple-element.163.sin_ref, bf16[1536,896]{1,0:T(8,128)(2,1)} %copy-done.2, ...), custom_call_target="tpu_custom_call" | custom-call | flops 362387865600 | bytes 1179648000 | tf_op jit(solution)/shard_map/project_back/pallas_call | solution.py:326
  325.6 18.8 %attend_back.3 = (bf16[512,384]{1,0:T(8,128)(2,1)}, bf16[2048,384]{1,0:T(8,128)(2,1)}) custom-call(s32[4]{0:T(128)} %pad_add_fusion.bases_ref, bf16[2,512,384]{2,1,0:T(8,128)(2,1)} %bitcast.61, s32[2,4,1,128]{3,2,1,0:T(1,128)} %broadcast_maximum_fusion.limit_ref, f32[4,2,256]{2,1,0:T(2,128)} %get-tuple-element.123.lse_ref, ...), custom_call_target="tpu_custom_call" | custom-call | flops 3221225472000 | bytes 1415577600 | tf_op jit(solution)/shard_map/attend_back/pallas_call | solution.py:272
  344.5 4.4 all-to-all-start.1
  348.9 19.9 %weight_grad.2 = bf16[1536,3072]{1,0:T(8,128)(2,1)} custom-call(bf16[512,1536]{1,0:T(8,128)(2,1)} %get-tuple-element.98.normed_ref.refs_0_, bf16[512,1536]{1,0:T(8,128)(2,1)} %get-tuple-element.106.normed_ref.refs_1_, bf16[512,1536]{1,0:T(8,128)(2,1)} %get-tuple-element.150.refs_2_, bf16[512,1536]{1,0:T(8,128)(2,1)} %get-tuple-element.149.refs_3_, ...), custom_call_target="tpu_custom_call" | custom-call | flops 2899102924800 | bytes 6606028800 | tf_op jit(solution)/shard_map/weight_grad/pallas_call | solution.py:533
  372.7 1.6 collective-permute-start.21
  376.0 6.2 %project_back.3 = (bf16[512,384]{1,0:T(8,128)(2,1)}, bf16[512,1536]{1,0:T(8,128)(2,1)}) custom-call(bf16[512,384]{1,0:T(8,128)(2,1)} %get-tuple-element.129.query_ref, f32[512,384]{1,0:T(8,128)} %get-tuple-element.165.cos_ref, f32[512,384]{1,0:T(8,128)} %get-tuple-element.163.sin_ref, bf16[1536,896]{1,0:T(8,128)(2,1)} %copy-done.2, ...), custom_call_target="tpu_custom_call" | custom-call | flops 362387865600 | bytes 1179648000 | tf_op jit(solution)/shard_map/project_back/pallas_call | solution.py:326
  382.1 2.3 pad_maximum_fusion.3.refs_5_
  385.4 2.1 collective-permute-done.21.refs_2_
  387.5 6.3 %collective-permute-done.22.refs_3_ = bf16[128,1536]{1,0:T(8,128)(2,1)} collective-permute-done((bf16[128,1536]{1,0:T(8,128)(2,1)}, bf16[128,1536]{1,0:T(8,128)(2,1)}, u32[]{:S(2)}, u32[]{:S(2)}) %collective-permute-start.22) | collective-permute-done | bytes 393248 | tf_op jit(solution)/shard_map/ppermute | solution.py:604
  393.8 3.1 grad_inputs_of.2
  396.9 1.7 collective-permute-start.23
  398.6 11.8 %weight_grad.3 = bf16[1536,1152]{1,0:T(8,128)(2,1)} custom-call(bf16[512,1536]{1,0:T(8,128)(2,1)} %get-tuple-element.154.refs_0_, bf16[512,1536]{1,0:T(8,128)(2,1)} %get-tuple-element.153.refs_1_, bf16[512,1536]{1,0:T(8,128)(2,1)} %get-tuple-element.136.refs_2_, bf16[512,1536]{1,0:T(8,128)(2,1)} %get-tuple-element.137.refs_3_, ...), custom_call_target="tpu_custom_call" | custom-call | flops 1087163596800 | bytes 3656908800 | tf_op jit(solution)/shard_map/weight_grad/pallas_call | solution.py:533
  412.9 1.9 collective-permute-start.28
  414.9 8.4 %collective-permute-done.26.refs_1_ = bf16[128,1536]{1,0:T(8,128)(2,1)S(1)} collective-permute-done((bf16[128,1536]{1,0:T(8,128)(2,1)S(1)}, bf16[128,1536]{1,0:T(8,128)(2,1)S(1)}, u32[]{:S(2)}, u32[]{:S(2)}) %collective-permute-start.26) | collective-permute-done | bytes 393248 | tf_op jit(solution)/shard_map/ppermute | solution.py:604
  423.3 3.5 collective-permute-start.24
  426.8 13.7 %collective-permute-done.27.refs_2_ = bf16[128,1536]{1,0:T(8,128)(2,1)S(1)} collective-permute-done((bf16[128,1536]{1,0:T(8,128)(2,1)S(1)}, bf16[128,1536]{1,0:T(8,128)(2,1)S(1)}, u32[]{:S(2)}, u32[]{:S(2)}) %collective-permute-start.27) | collective-permute-done | bytes 393248 | tf_op jit(solution)/shard_map/ppermute | solution.py:604
  440.6 4.4 collective-permute-start.25
  445.0 21.6 %collective-permute-done.28.refs_3_ = bf16[128,1536]{1,0:T(8,128)(2,1)S(1)} collective-permute-done((bf16[128,1536]{1,0:T(8,128)(2,1)S(1)}, bf16[128,1536]{1,0:T(8,128)(2,1)S(1)}, u32[]{:S(2)}, u32[]{:S(2)}) %collective-permute-start.28) | collective-permute-done | bytes 393248 | tf_op jit(solution)/shard_map/ppermute | solution.py:604
  467.3 3.1 grad_inputs_of.3
  471.5 2.0 collective-permute-start.30
  476.3 15.7 %collective-permute-done.25 = bf16[128,1536]{1,0:T(8,128)(2,1)} collective-permute-done((bf16[128,1536]{1,0:T(8,128)(2,1)S(1)}, bf16[128,1536]{1,0:T(8,128)(2,1)}, u32[]{:S(2)}, u32[]{:S(2)}) %collective-permute-start.25) | collective-permute-done | bytes 393248 | tf_op jit(solution)/shard_map/ppermute | solution.py:604
  493.1 1.4 collective-permute-start.34
  495.6 3.2 collective-permute-start.32
  498.8 2.8 collective-permute-done.31
  501.8 1.9 pad_maximum_fusion
  503.8 1.9 collective-permute-start.38
  505.6 1.8 collective-permute-start.36
  507.4 4.7 fusion.1
  512.8 1.5 convert_bitcast_fusion
  514.3 5.5 %reduce-scatter.5.cloned.1.call-done = bf16[192,1152]{1,0:T(8,128)(2,1)} async-done(((bf16[1536,1152]{1,0:T(8,128)(2,1)}), bf16[192,1152]{1,0:T(8,128)(2,1)}) %reduce-scatter.5.cloned.1.call-update) | async-done | bytes 442384 | tf_op jit(solution)/shard_map/reduce_scatter | solution.py:815
  (206 shorter events, 50.8 us)
Async XLA Ops:
  7.2 10.5 %copy-start.12 = (bf16[192,1024]{1,0:T(8,128)(2,1)S(1)}, bf16[192,1024]{1,0:T(8,128)(2,1)}, u32[]{:S(2)}) copy-start(bf16[192,1024]{1,0:T(8,128)(2,1)} %param.21) | copy-start | bytes 1179652
  7.2 185.2 %all-gather.3.cloned.1.call-start = ((), (), s32[]{:S(2)}) async-start(), calls=%async_computation.4 | async-start | bytes 15925248 | tf_op jit(solution)/shard_map/all_gather | solution.py:669
  10.0 15.0 %collective-permute-start = (bf16[192,896]{1,0:T(8,128)(2,1)S(1)}, bf16[192,896]{1,0:T(8,128)(2,1)}, u32[]{:S(2)}, u32[]{:S(2)}) collective-permute-start(bf16[192,896]{1,0:T(8,128)(2,1)S(1)} %concatenate.25), channel_id=1, source_target_pairs={{0,4},{4,0},{8,12},{12,8},{1,5},{5,1},{9,13},{13,9},{2,6},{6,2},{1... | collective-permute-start | bytes 1032200 | tf_op jit(solution)/shard_map/ppermute | solution.py:604
  11.5 17.0 %collective-permute-start.1 = (bf16[192,896]{1,0:T(8,128)(2,1)S(1)}, bf16[192,896]{1,0:T(8,128)(2,1)}, u32[]{:S(2)}, u32[]{:S(2)}) collective-permute-start(bf16[192,896]{1,0:T(8,128)(2,1)S(1)} %concatenate.25), channel_id=1, source_target_pairs={{0,8},{4,12},{8,0},{12,4},{1,9},{5,13},{9,1},{13,5},{2,10},{6,14},... | collective-permute-start | bytes 1032200 | tf_op jit(solution)/shard_map/ppermute | solution.py:604
  12.0 17.5 %collective-permute-start.2 = (bf16[192,896]{1,0:T(8,128)(2,1)S(1)}, bf16[192,896]{1,0:T(8,128)(2,1)}, u32[]{:S(2)}, u32[]{:S(2)}) collective-permute-start(bf16[192,896]{1,0:T(8,128)(2,1)S(1)} %concatenate.25), channel_id=1, source_target_pairs={{0,12},{4,8},{8,4},{12,0},{1,13},{5,9},{9,5},{13,1},{2,14},{6,10},... | collective-permute-start | bytes 1032200 | tf_op jit(solution)/shard_map/ppermute | solution.py:604
  13.5 17.1 %collective-permute-start.3 = (bf16[192,384]{1,0:T(8,128)(2,1)}, bf16[192,384]{1,0:T(8,128)(2,1)}, u32[]{:S(2)}, u32[]{:S(2)}) collective-permute-start(bf16[192,384]{1,0:T(8,128)(2,1)} %bitcast.52), channel_id=1, source_target_pairs={{0,1},{1,0},{2,3},{3,2},{4,5},{5,4},{6,7},{7,6},{8,9},{9,8},{10,11... | collective-permute-start | bytes 442376 | tf_op jit(solution)/shard_map/ppermute | solution.py:604
  14.0 16.6 %collective-permute-start.4 = (bf16[192,384]{1,0:T(8,128)(2,1)}, bf16[192,384]{1,0:T(8,128)(2,1)}, u32[]{:S(2)}, u32[]{:S(2)}) collective-permute-start(bf16[192,384]{1,0:T(8,128)(2,1)} %bitcast.53), channel_id=1, source_target_pairs={{0,2},{1,3},{2,0},{3,1},{4,6},{5,7},{6,4},{7,5},{8,10},{9,11},{10,... | collective-permute-start | bytes 442376 | tf_op jit(solution)/shard_map/ppermute | solution.py:604
  17.7 7.1 %copy-start.14 = (bf16[1024,192]{0,1:T(8,128)(2,1)S(1)}, bf16[1024,192]{0,1:T(8,128)(2,1)}, u32[]{:S(2)}) copy-start(bf16[1024,192]{0,1:T(8,128)(2,1)} %param.22) | copy-start | bytes 1179652
  24.9 8.0 %copy-start.32 = (bf16[384,192]{0,1:T(8,128)(2,1)S(1)}, bf16[384,192]{0,1:T(8,128)(2,1)}, u32[]{:S(2)}) copy-start(bf16[384,192]{0,1:T(8,128)(2,1)} %param.18) | copy-start | bytes 442372
  25.0 8.0 %collective-permute-start.5 = (bf16[192,384]{1,0:T(8,128)(2,1)}, bf16[192,384]{1,0:T(8,128)(2,1)S(1)}, u32[]{:S(2)}, u32[]{:S(2)}) collective-permute-start(bf16[192,384]{1,0:T(8,128)(2,1)} %bitcast.54), channel_id=1, source_target_pairs={{0,3},{1,2},{2,1},{3,0},{4,7},{5,6},{6,5},{7,4},{8,11},{9,10},{10,... | collective-permute-start | bytes 442376 | tf_op jit(solution)/shard_map/ppermute | solution.py:604
  36.2 181.1 %all-gather.5.cloned.1.call-start = ((), (), s32[]{:S(2)}) async-start(), calls=%async_computation.5 | async-start | bytes 10616832 | tf_op jit(solution)/shard_map/all_gather | solution.py:669
  36.2 4.5 collective-permute-start.6
  43.9 14.3 %copy-start.3 = (bf16[2,512,1536]{2,1,0:T(8,128)(2,1)S(1)}, bf16[2,512,1536]{2,1,0:T(8,128)(2,1)}, u32[]{:S(2)}) copy-start(bf16[2,512,1536]{2,1,0:T(8,128)(2,1)} %param.23) | copy-start | bytes 9437188
  54.1 28.6 %collective-permute-start.7 = (bf16[1024,384]{1,0:T(8,128)(2,1)}, bf16[1024,384]{1,0:T(8,128)(2,1)S(1)}, u32[]{:S(2)}, u32[]{:S(2)}) collective-permute-start(bf16[1024,384]{1,0:T(8,128)(2,1)} %get-tuple-element.85.refs_0_), channel_id=1, source_target_pairs={{0,4},{4,0},{8,12},{12,8},{1,5},{5,1},{9,13},{13,9},{2,6},{6,2},{1... | collective-permute-start | bytes 2359304 | tf_op jit(solution)/shard_map/ppermute | solution.py:604
  55.6 27.1 %collective-permute-start.8 = (bf16[1024,384]{1,0:T(8,128)(2,1)}, bf16[1024,384]{1,0:T(8,128)(2,1)S(1)}, u32[]{:S(2)}, u32[]{:S(2)}) collective-permute-start(bf16[1024,384]{1,0:T(8,128)(2,1)} %get-tuple-element.85.refs_0_), channel_id=1, source_target_pairs={{0,8},{4,12},{8,0},{12,4},{1,9},{5,13},{9,1},{13,5},{2,10},{6,14},... | collective-permute-start | bytes 2359304 | tf_op jit(solution)/shard_map/ppermute | solution.py:604
  56.1 58.2 %collective-permute-start.9 = (bf16[1024,384]{1,0:T(8,128)(2,1)}, bf16[1024,384]{1,0:T(8,128)(2,1)S(1)}, u32[]{:S(2)}, u32[]{:S(2)}) collective-permute-start(bf16[1024,384]{1,0:T(8,128)(2,1)} %get-tuple-element.85.refs_0_), channel_id=1, source_target_pairs={{0,12},{4,8},{8,4},{12,0},{1,13},{5,9},{9,5},{13,1},{2,14},{6,10},... | collective-permute-start | bytes 2359304 | tf_op jit(solution)/shard_map/ppermute | solution.py:604
  60.1 69.2 %collective-permute-start.13 = (bf16[192,3072]{1,0:T(8,128)(2,1)S(1)}, bf16[192,3072]{1,0:T(8,128)(2,1)S(1)}, u32[]{:S(2)}, u32[]{:S(2)}) collective-permute-start(bf16[192,3072]{1,0:T(8,128)(2,1)S(1)} %copy-done.20), channel_id=1, source_target_pairs={{0,2},{1,3},{2,0},{3,1},{4,6},{5,7},{6,4},{7,5},{8,10},{9,11},{10,... | collective-permute-start | bytes 3538952 | tf_op jit(solution)/shard_map/ppermute | solution.py:604
  82.7 31.7 %copy-start.38 = (bf16[1024,384]{1,0:T(8,128)(2,1)}, bf16[1024,384]{1,0:T(8,128)(2,1)S(1)}, u32[]{:S(2)}) copy-start(bf16[1024,384]{1,0:T(8,128)(2,1)S(1)} %collective-permute-done.7.refs_1_) | copy-start | bytes 2359300
  82.7 31.7 %copy-start.39 = (bf16[1024,384]{1,0:T(8,128)(2,1)}, bf16[1024,384]{1,0:T(8,128)(2,1)S(1)}, u32[]{:S(2)}) copy-start(bf16[1024,384]{1,0:T(8,128)(2,1)S(1)} %collective-permute-done.8.refs_2_) | copy-start | bytes 2359300
  115.3 15.1 %copy-start.1 = (f32[512,768]{1,0:T(8,128)S(1)}, f32[512,768]{1,0:T(8,128)}, u32[]{:S(2)}) copy-start(f32[512,768]{1,0:T(8,128)} %get-tuple-element.80.cos_ref) | copy-start | bytes 4718596
  136.7 20.8 %collective-permute-start.10 = (bf16[512,384]{1,0:T(8,128)(2,1)S(1)}, bf16[512,384]{1,0:T(8,128)(2,1)S(1)}, u32[]{:S(2)}, u32[]{:S(2)}) collective-permute-start(bf16[512,384]{1,0:T(8,128)(2,1)S(1)} %copy-done.21), channel_id=1, source_target_pairs={{0,1},{1,0},{2,3},{3,2},{4,5},{5,4},{6,7},{7,6},{8,9},{9,8},{10,11... | collective-permute-start | bytes 1179656 | tf_op jit(solution)/shard_map/ppermute | solution.py:604
  137.2 28.9 %collective-permute-start.11 = (bf16[512,384]{1,0:T(8,128)(2,1)S(1)}, bf16[512,384]{1,0:T(8,128)(2,1)S(1)}, u32[]{:S(2)}, u32[]{:S(2)}) collective-permute-start(bf16[512,384]{1,0:T(8,128)(2,1)S(1)} %copy-done.21), channel_id=1, source_target_pairs={{0,2},{1,3},{2,0},{3,1},{4,6},{5,7},{6,4},{7,5},{8,10},{9,11},{10,... | collective-permute-start | bytes 1179656 | tf_op jit(solution)/shard_map/ppermute | solution.py:604
  139.6 52.7 %collective-permute-start.12 = (bf16[512,384]{1,0:T(8,128)(2,1)S(1)}, bf16[512,384]{1,0:T(8,128)(2,1)S(1)}, u32[]{:S(2)}, u32[]{:S(2)}) collective-permute-start(bf16[512,384]{1,0:T(8,128)(2,1)S(1)} %copy-done.21), channel_id=1, source_target_pairs={{0,3},{1,2},{2,1},{3,0},{4,7},{5,6},{6,5},{7,4},{8,11},{9,10},{10,... | collective-permute-start | bytes 1179656 | tf_op jit(solution)/shard_map/ppermute | solution.py:604
  154.1 79.7 %collective-permute-start.14 = (bf16[512,384]{1,0:T(8,128)(2,1)}, bf16[512,384]{1,0:T(8,128)(2,1)}, u32[]{:S(2)}, u32[]{:S(2)}) collective-permute-start(bf16[512,384]{1,0:T(8,128)(2,1)} %get-tuple-element.88.refs_0_.mixed_ref), channel_id=1, source_target_pairs={{0,1},{1,0},{2,3},{3,2},{4,5},{5,4},{6,7},{7,6},{8,9},{9,8},{10,11... | collective-permute-start | bytes 1179656 | tf_op jit(solution)/shard_map/ppermute | solution.py:604
  155.5 78.3 %collective-permute-start.15 = (bf16[512,384]{1,0:T(8,128)(2,1)}, bf16[512,384]{1,0:T(8,128)(2,1)}, u32[]{:S(2)}, u32[]{:S(2)}) collective-permute-start(bf16[512,384]{1,0:T(8,128)(2,1)} %get-tuple-element.88.refs_0_.mixed_ref), channel_id=1, source_target_pairs={{0,2},{1,3},{2,0},{3,1},{4,6},{5,7},{6,4},{7,5},{8,10},{9,11},{10,... | collective-permute-start | bytes 1179656 | tf_op jit(solution)/shard_map/ppermute | solution.py:604
  157.4 34.9 %copy-start.41 = (bf16[512,384]{1,0:T(8,128)(2,1)}, bf16[512,384]{1,0:T(8,128)(2,1)S(1)}, u32[]{:S(2)}) copy-start(bf16[512,384]{1,0:T(8,128)(2,1)S(1)} %collective-permute-done.10.refs_1_) | copy-start | bytes 1179652
  157.4 76.3 %collective-permute-start.16 = (bf16[512,384]{1,0:T(8,128)(2,1)}, bf16[512,384]{1,0:T(8,128)(2,1)}, u32[]{:S(2)}, u32[]{:S(2)}) collective-permute-start(bf16[512,384]{1,0:T(8,128)(2,1)} %get-tuple-element.88.refs_0_.mixed_ref), channel_id=1, source_target_pairs={{0,3},{1,2},{2,1},{3,0},{4,7},{5,6},{6,5},{7,4},{8,11},{9,10},{10,... | collective-permute-start | bytes 1179656 | tf_op jit(solution)/shard_map/ppermute | solution.py:604
  166.1 26.3 %copy-start.42 = (bf16[512,384]{1,0:T(8,128)(2,1)}, bf16[512,384]{1,0:T(8,128)(2,1)S(1)}, u32[]{:S(2)}) copy-start(bf16[512,384]{1,0:T(8,128)(2,1)S(1)} %collective-permute-done.11.refs_2_) | copy-start | bytes 1179652
  241.3 33.9 %collective-permute-start.17 = (bf16[512,1536]{1,0:T(8,128)(2,1)}, bf16[512,1536]{1,0:T(8,128)(2,1)}, u32[]{:S(2)}, u32[]{:S(2)}) collective-permute-start(bf16[512,1536]{1,0:T(8,128)(2,1)} %get-tuple-element.109.refs_0_), channel_id=1, source_target_pairs={{0,1},{1,0},{2,3},{3,2},{4,5},{5,4},{6,7},{7,6},{8,9},{9,8},{10,11... | collective-permute-start | bytes 4718600 | tf_op jit(solution)/shard_map/ppermute | solution.py:604
  241.3 31.4 %copy-start.9 = (bf16[512,1536]{1,0:T(8,128)(2,1)S(1)}, bf16[512,1536]{1,0:T(8,128)(2,1)}, u32[]{:S(2)}) copy-start(bf16[512,1536]{1,0:T(8,128)(2,1)} %get-tuple-element.102) | copy-start | bytes 4718596
  270.7 37.1 %collective-permute-start.19 = (bf16[512,1536]{1,0:T(8,128)(2,1)}, bf16[512,1536]{1,0:T(8,128)(2,1)}, u32[]{:S(2)}, u32[]{:S(2)}) collective-permute-start(bf16[512,1536]{1,0:T(8,128)(2,1)} %get-tuple-element.117.refs_0_), channel_id=1, source_target_pairs={{0,1},{1,0},{2,3},{3,2},{4,5},{5,4},{6,7},{7,6},{8,9},{9,8},{10,11... | collective-permute-start | bytes 4718600 | tf_op jit(solution)/shard_map/ppermute | solution.py:604
  301.1 206.3 %collective-permute-start.18 = (bf16[1024,1536]{1,0:T(8,128)(2,1)}, bf16[1024,1536]{1,0:T(8,128)(2,1)}, u32[]{:S(2)}, u32[]{:S(2)}) collective-permute-start(bf16[1024,1536]{1,0:T(8,128)(2,1)} %constant_dynamic-update-slice_fusion.7), channel_id=1, source_target_pairs={{0,1},{1,0},{2,3},{3,2},{4,5},{5,4},{6,7},{7,6},{8,9},{9,8},{10,11... | collective-permute-start | bytes 9437192 | tf_op jit(solution)/shard_map/ppermute | solution.py:604
  301.8 18.4 %all-to-all-start = ((bf16[4,512,384]{2,1,0:T(8,128)(2,1)}), bf16[4,512,384]{2,1,0:T(8,128)(2,1)}, u32[]{:S(2)}, u32[]{:S(2)}) async-start(bf16[4,512,384]{2,1,0:T(8,128)(2,1)} %bitcast.46), calls=%async_computation | async-start | bytes 3145728 | tf_op jit(solution)/shard_map/all_to_all | solution.py:770
  307.7 7.0 %copy-start.36 = (f32[1,1536]{1,0:T(1,128)S(1)}, f32[1,1536]{1,0:T(1,128)}, u32[]{:S(2)}) copy-start(f32[1,1536]{1,0:T(1,128)} %get-tuple-element.144) | copy-start | bytes 18436
  344.5 31.5 %all-to-all-start.1 = ((bf16[4,512,384]{2,1,0:T(8,128)(2,1)}), bf16[4,512,384]{2,1,0:T(8,128)(2,1)}, u32[]{:S(2)}, u32[]{:S(2)}) async-start(bf16[4,512,384]{2,1,0:T(8,128)(2,1)} %bitcast.45), calls=%async_computation.1 | async-start | bytes 3145728 | tf_op jit(solution)/shard_map/all_to_all | solution.py:770
  348.8 122.6 %reduce-scatter.3.cloned.1.call-start = ((), (), s32[]{:S(2)}) async-start(), calls=%async_computation.6 | async-start | bytes 10616832 | tf_op jit(solution)/shard_map/reduce_scatter | solution.py:802
  368.8 151.0 %reduce-scatter.5.cloned.1.call-start = ((), (), s32[]{:S(2)}) async-start(), calls=%async_computation.7 | async-start | bytes 3981312 | tf_op jit(solution)/shard_map/reduce_scatter | solution.py:815
  371.3 14.1 %collective-permute-start.20 = (bf16[128,1536]{1,0:T(8,128)(2,1)}, bf16[128,1536]{1,0:T(8,128)(2,1)}, u32[]{:S(2)}, u32[]{:S(2)}) collective-permute-start(bf16[128,1536]{1,0:T(8,128)(2,1)} %get-tuple-element.161), channel_id=1, source_target_pairs={{0,1},{1,0},{2,3},{3,2},{4,5},{5,4},{6,7},{7,6},{8,9},{9,8},{10,11... | collective-permute-start | bytes 1179656 | tf_op jit(solution)/shard_map/ppermute | solution.py:604
  372.7 14.8 %collective-permute-start.21 = (bf16[128,1536]{1,0:T(8,128)(2,1)}, bf16[128,1536]{1,0:T(8,128)(2,1)}, u32[]{:S(2)}, u32[]{:S(2)}) collective-permute-start(bf16[128,1536]{1,0:T(8,128)(2,1)} %get-tuple-element.160), channel_id=1, source_target_pairs={{0,2},{1,3},{2,0},{3,1},{4,6},{5,7},{6,4},{7,5},{8,10},{9,11},{10,... | collective-permute-start | bytes 1179656 | tf_op jit(solution)/shard_map/ppermute | solution.py:604
  374.3 19.5 %collective-permute-start.22 = (bf16[128,1536]{1,0:T(8,128)(2,1)}, bf16[128,1536]{1,0:T(8,128)(2,1)}, u32[]{:S(2)}, u32[]{:S(2)}) collective-permute-start(bf16[128,1536]{1,0:T(8,128)(2,1)} %get-tuple-element.159), channel_id=1, source_target_pairs={{0,3},{1,2},{2,1},{3,0},{4,7},{5,6},{6,5},{7,4},{8,11},{9,10},{10,... | collective-permute-start | bytes 1179656 | tf_op jit(solution)/shard_map/ppermute | solution.py:604
  376.0 6.2 %copy-start.25 = (bf16[512,384]{1,0:T(8,128)(2,1)S(1)}, bf16[512,384]{1,0:T(8,128)(2,1)}, u32[]{:S(2)}) copy-start(bf16[512,384]{1,0:T(8,128)(2,1)} %get-tuple-element.129.query_ref) | copy-start | bytes 1179652
  396.9 74.6 %collective-permute-start.23 = (bf16[128,1536]{1,0:T(8,128)(2,1)}, bf16[128,1536]{1,0:T(8,128)(2,1)}, u32[]{:S(2)}, u32[]{:S(2)}) collective-permute-start(bf16[128,1536]{1,0:T(8,128)(2,1)} %get-tuple-element.134), channel_id=1, source_target_pairs={{0,1},{1,0},{2,3},{3,2},{4,5},{5,4},{6,7},{7,6},{8,9},{9,8},{10,11... | collective-permute-start | bytes 1179656 | tf_op jit(solution)/shard_map/ppermute | solution.py:604
  398.6 11.8 %copy-start.16 = (bf16[512,1536]{1,0:T(8,128)(2,1)S(1)}, bf16[512,1536]{1,0:T(8,128)(2,1)}, u32[]{:S(2)}) copy-start(bf16[512,1536]{1,0:T(8,128)(2,1)} %get-tuple-element.139) | copy-start | bytes 4718596
  411.3 12.1 %collective-permute-start.26 = (bf16[128,1536]{1,0:T(8,128)(2,1)S(1)}, bf16[128,1536]{1,0:T(8,128)(2,1)S(1)}, u32[]{:S(2)}, u32[]{:S(2)}) collective-permute-start(bf16[128,1536]{1,0:T(8,128)(2,1)S(1)} %get-tuple-element.157), channel_id=1, source_target_pairs={{0,1},{1,0},{2,3},{3,2},{4,5},{5,4},{6,7},{7,6},{8,9},{9,8},{10,11... | collective-permute-start | bytes 1179656 | tf_op jit(solution)/shard_map/ppermute | solution.py:604
  411.6 29.0 %collective-permute-start.27 = (bf16[128,1536]{1,0:T(8,128)(2,1)S(1)}, bf16[128,1536]{1,0:T(8,128)(2,1)S(1)}, u32[]{:S(2)}, u32[]{:S(2)}) collective-permute-start(bf16[128,1536]{1,0:T(8,128)(2,1)S(1)} %get-tuple-element.156), channel_id=1, source_target_pairs={{0,2},{1,3},{2,0},{3,1},{4,6},{5,7},{6,4},{7,5},{8,10},{9,11},{10,... | collective-permute-start | bytes 1179656 | tf_op jit(solution)/shard_map/ppermute | solution.py:604
  412.9 53.7 %collective-permute-start.28 = (bf16[128,1536]{1,0:T(8,128)(2,1)S(1)}, bf16[128,1536]{1,0:T(8,128)(2,1)S(1)}, u32[]{:S(2)}, u32[]{:S(2)}) collective-permute-start(bf16[128,1536]{1,0:T(8,128)(2,1)S(1)} %get-tuple-element.155), channel_id=1, source_target_pairs={{0,3},{1,2},{2,1},{3,0},{4,7},{5,6},{6,5},{7,4},{8,11},{9,10},{10,... | collective-permute-start | bytes 1179656 | tf_op jit(solution)/shard_map/ppermute | solution.py:604
  423.3 43.2 %copy-start.27 = (bf16[128,1536]{1,0:T(8,128)(2,1)}, bf16[128,1536]{1,0:T(8,128)(2,1)S(1)}, u32[]{:S(2)}) copy-start(bf16[128,1536]{1,0:T(8,128)(2,1)S(1)} %collective-permute-done.26.refs_1_) | copy-start | bytes 1179652
  423.3 51.2 %collective-permute-start.24 = (bf16[128,1536]{1,0:T(8,128)(2,1)S(1)}, bf16[128,1536]{1,0:T(8,128)(2,1)}, u32[]{:S(2)}, u32[]{:S(2)}) collective-permute-start(bf16[128,1536]{1,0:T(8,128)(2,1)S(1)} %copy-done.30), channel_id=1, source_target_pairs={{0,2},{1,3},{2,0},{3,1},{4,6},{5,7},{6,4},{7,5},{8,10},{9,11},{10,... | collective-permute-start | bytes 1179656 | tf_op jit(solution)/shard_map/ppermute | solution.py:604
  440.6 26.0 %copy-start.28 = (bf16[128,1536]{1,0:T(8,128)(2,1)}, bf16[128,1536]{1,0:T(8,128)(2,1)S(1)}, u32[]{:S(2)}) copy-start(bf16[128,1536]{1,0:T(8,128)(2,1)S(1)} %collective-permute-done.27.refs_2_) | copy-start | bytes 1179652
  440.6 51.5 %collective-permute-start.25 = (bf16[128,1536]{1,0:T(8,128)(2,1)S(1)}, bf16[128,1536]{1,0:T(8,128)(2,1)}, u32[]{:S(2)}, u32[]{:S(2)}) collective-permute-start(bf16[128,1536]{1,0:T(8,128)(2,1)S(1)} %copy-done.30), channel_id=1, source_target_pairs={{0,3},{1,2},{2,1},{3,0},{4,7},{5,6},{6,5},{7,4},{8,11},{9,10},{10,... | collective-permute-start | bytes 1179656 | tf_op jit(solution)/shard_map/ppermute | solution.py:604
  470.4 22.7 %collective-permute-start.29 = (bf16[128,1536]{1,0:T(8,128)(2,1)}, bf16[128,1536]{1,0:T(8,128)(2,1)}, u32[]{:S(2)}, u32[]{:S(2)}) collective-permute-start(bf16[128,1536]{1,0:T(8,128)(2,1)} %get-tuple-element.140), channel_id=1, source_target_pairs={{0,1},{1,0},{2,3},{3,2},{4,5},{5,4},{6,7},{7,6},{8,9},{9,8},{10,11... | collective-permute-start | bytes 1179656 | tf_op jit(solution)/shard_map/ppermute | solution.py:604
  471.5 21.6 %copy-start.34 = (f32[1,1536]{1,0:T(1,128)S(1)}, f32[1,1536]{1,0:T(1,128)}, u32[]{:S(2)}) copy-start(f32[1,1536]{1,0:T(1,128)} %get-tuple-element.142) | copy-start | bytes 18436
  471.5 21.6 %copy-start.35 = (f32[1,1536]{1,0:T(1,128)S(1)}, f32[1,1536]{1,0:T(1,128)}, u32[]{:S(2)}) copy-start(f32[1,1536]{1,0:T(1,128)} %get-tuple-element.143) | copy-start | bytes 18436
  471.5 24.0 %collective-permute-start.30 = (bf16[128,1536]{1,0:T(8,128)(2,1)}, bf16[128,1536]{1,0:T(8,128)(2,1)S(1)}, u32[]{:S(2)}, u32[]{:S(2)}) collective-permute-start(bf16[128,1536]{1,0:T(8,128)(2,1)} %get-tuple-element.140), channel_id=1, source_target_pairs={{0,2},{1,3},{2,0},{3,1},{4,6},{5,7},{6,4},{7,5},{8,10},{9,11},{10,... | collective-permute-start | bytes 1179656 | tf_op jit(solution)/shard_map/ppermute | solution.py:604
  474.5 27.0 %collective-permute-start.31 = (bf16[128,1536]{1,0:T(8,128)(2,1)}, bf16[128,1536]{1,0:T(8,128)(2,1)S(1)}, u32[]{:S(2)}, u32[]{:S(2)}) collective-permute-start(bf16[128,1536]{1,0:T(8,128)(2,1)} %get-tuple-element.140), channel_id=1, source_target_pairs={{0,3},{1,2},{2,1},{3,0},{4,7},{5,6},{6,5},{7,4},{8,11},{9,10},{10,... | collective-permute-start | bytes 1179656 | tf_op jit(solution)/shard_map/ppermute | solution.py:604
  476.3 25.3 %copy-start.33 = (f32[1,1536]{1,0:T(1,128)S(1)}, f32[1,1536]{1,0:T(1,128)}, u32[]{:S(2)}) copy-start(f32[1,1536]{1,0:T(1,128)} %add.171) | copy-start | bytes 18436
  493.1 8.5 %collective-permute-start.34 = (f32[1,1536]{1,0:T(1,128)S(1)}, f32[1,1536]{1,0:T(1,128)S(1)}, u32[]{:S(2)}, u32[]{:S(2)}) collective-permute-start(f32[1,1536]{1,0:T(1,128)S(1)} %add.167), channel_id=1, source_target_pairs={{0,3},{1,2},{2,1},{3,0},{4,7},{5,6},{6,5},{7,4},{8,11},{9,10},{10,... | collective-permute-start | bytes 18440 | tf_op jit(solution)/shard_map/ppermute | solution.py:604
  494.5 7.1 %collective-permute-start.33 = (f32[1,1536]{1,0:T(1,128)S(1)}, f32[1,1536]{1,0:T(1,128)S(1)}, u32[]{:S(2)}, u32[]{:S(2)}) collective-permute-start(f32[1,1536]{1,0:T(1,128)S(1)} %add.167), channel_id=1, source_target_pairs={{0,2},{1,3},{2,0},{3,1},{4,6},{5,7},{6,4},{7,5},{8,10},{9,11},{10,... | collective-permute-start | bytes 18440 | tf_op jit(solution)/shard_map/ppermute | solution.py:604
  495.6 6.1 %collective-permute-start.32 = (f32[1,1536]{1,0:T(1,128)S(1)}, f32[1,1536]{1,0:T(1,128)S(1)}, u32[]{:S(2)}, u32[]{:S(2)}) collective-permute-start(f32[1,1536]{1,0:T(1,128)S(1)} %add.167), channel_id=1, source_target_pairs={{0,1},{1,0},{2,3},{3,2},{4,5},{5,4},{6,7},{7,6},{8,9},{9,8},{10,11... | collective-permute-start | bytes 18440 | tf_op jit(solution)/shard_map/ppermute | solution.py:604
  501.7 2.0 collective-permute-start.35
  503.8 9.0 %copy-start.18 = (bf16[192,3072]{1,0:T(8,128)(2,1)S(1)}, bf16[192,3072]{1,0:T(8,128)(2,1)}, u32[]{:S(2)}) copy-start(bf16[192,3072]{1,0:T(8,128)(2,1)} %reduce-scatter.3.cloned.1.call-done) | copy-start | bytes 3538948
  503.8 8.3 %collective-permute-start.38 = (f32[2,1536]{1,0:T(2,128)S(1)}, f32[2,1536]{1,0:T(2,128)S(1)}, u32[]{:S(2)}, u32[]{:S(2)}) collective-permute-start(f32[2,1536]{1,0:T(2,128)S(1)} %fusion.19), channel_id=1, source_target_pairs={{0,12},{4,8},{8,4},{12,0},{1,13},{5,9},{9,5},{13,1},{2,14},{6,10},... | collective-permute-start | bytes 36872 | tf_op jit(solution)/shard_map/ppermute | solution.py:604
  505.6 6.5 %collective-permute-start.36 = (f32[2,1536]{1,0:T(2,128)S(1)}, f32[2,1536]{1,0:T(2,128)S(1)}, u32[]{:S(2)}, u32[]{:S(2)}) collective-permute-start(f32[2,1536]{1,0:T(2,128)S(1)} %fusion.19), channel_id=1, source_target_pairs={{0,4},{4,0},{8,12},{12,8},{1,5},{5,1},{9,13},{13,9},{2,6},{6,2},{1... | collective-permute-start | bytes 36872 | tf_op jit(solution)/shard_map/ppermute | solution.py:604
  507.4 4.7 collective-permute-start.37
  (25 other events, 73.0 us)
Sparse Core Ops, SparseCore 0:
  36.3 103.3 all-gather.2
  141.6 59.0 all-gather.4
  368.9 77.1 reduce-scatter.2
  471.6 48.1 reduce-scatter.4
